TPU v7x, 512 devices: a whole 4x8x8 slice. The times are simulated.
512 devices in a mesh: sec: 2 (over y_lo), exp: 32 (over y_hi, x, core), hid: 8 (over z).
Axes of the slice: x: 4, y: 8 (y_hi: 4, y_lo: 2; y = y_hi * 2 + y_lo), z: 8, core: 2. Of those that a mesh axis runs over, the one named last changes fastest.
Arguments:
- tokens: bfloat16 [1024, 4096], P('exp', ('sec', 'hid')), may hold values from -1200 to 1200
- norm_gain: bfloat16 [4096], P(('sec', 'hid')), may hold values from 0.5 to 2
- route_weight: float32 [1024, 2], P('exp'), may hold values from 0.1 to 1
- block_experts: int32 [8, 2], replicated, may hold values from 0 to 7, all different within a row; in each aligned block of 8 rows (0 to 7, 8 to 15, ...) at most 4 rows name the same one
- w_gate: bfloat16 [2, 4096, 32768], P('sec', None, ('exp', 'hid')), may hold values from -0.09375 to 0.09375
- w_up: bfloat16 [2, 4096, 32768], P('sec', None, ('exp', 'hid')), may hold values from -0.09375 to 0.09375
- w_down: bfloat16 [2, 32768, 4096], P('sec', ('exp', 'hid')), may hold values from -0.0625 to 0.0625
Outputs:
- moe_out: bfloat16 [1024, 4096], P('exp', ('sec', 'hid'))
Inputs may be any that keep to these rules, and one draw needn't show every extreme that they name: `block_experts`: each row names 2 different experts; no expert is named by more than 4 rows, a bound that some block reaches; every expert is named by some row.
All inputs are finite; a program needn't handle non-finite values.
Results may differ from a plain program's by a relative error of at most 0.018.
Values may be sent and summed in bfloat16 or wider, within the bound.
No kernel may reach another device: no remote copies, remote signals or barrier semaphores. Data moves between devices by JAX's collectives and lax.ppermute only.
A program may use at most 64 MiB of HBM per device.

v0:
```python
import jax
import jax.numpy as jnp
from jax import lax
from jax.sharding import PartitionSpec as P

D = 4096
EXPERTS = 8
BLK = 128
MOST = 4


def per_device(tokens, norm_gain, route_weight, block_experts, w_gate, w_up, w_down):
    exp_devices = lax.axis_size("exp")
    group_size = exp_devices // EXPERTS
    my_expert = lax.axis_index("exp") // group_size
    tok_local = tokens.shape[0]
    total_rows = tok_local * exp_devices
    num_blocks = total_rows // BLK
    slot_count = MOST
    gate_local = w_gate[0]
    up_local = w_up[0]
    down_local = w_down[0]
    block_hit = jnp.any(block_experts == my_expert, axis=1)
    hit_flags = block_hit.astype(jnp.int32)
    slot_of_block = jnp.where(block_hit, jnp.cumsum(hit_flags) - 1, -1)
    slot_ids = jnp.arange(slot_count, dtype=jnp.int32)
    slot_match = slot_of_block[None, :] == slot_ids[:, None]
    block_ids = jnp.arange(num_blocks, dtype=jnp.int32)
    block_of_slot = jnp.sum(jnp.where(slot_match, block_ids[None, :], 0), axis=1)
    slot_valid = jnp.any(slot_match, axis=1)
    values = tokens.astype(jnp.float32)
    square_part = jnp.sum(values * values, axis=1)
    square_total = lax.psum(square_part, ("sec", "hid"))
    rms_value = jnp.sqrt(square_total / D + 1e-05)
    normed = (values * norm_gain.astype(jnp.float32) / rms_value[:, None]).astype(jnp.bfloat16)
    gathered = lax.all_gather(normed, "exp", axis=0, tiled=True)
    width = gathered.shape[1]
    picked = jnp.take(gathered.reshape(num_blocks, BLK, width), block_of_slot, axis=0)
    picked = jnp.where(slot_valid[:, None, None], picked, jnp.zeros_like(picked))
    picked_rows = picked.reshape(slot_count * BLK, width)
    feature_piece = lax.all_gather(picked_rows, ("sec", "hid"), axis=1, tiled=True)
    gate_acc = jnp.dot(feature_piece, gate_local, preferred_element_type=jnp.float32)
    up_acc = jnp.dot(feature_piece, up_local, preferred_element_type=jnp.float32)
    activated = (jax.nn.silu(gate_acc) * up_acc).astype(jnp.bfloat16)
    contribution = jnp.dot(activated, down_local, preferred_element_type=jnp.float32)
    term_vals = contribution.astype(jnp.bfloat16)
    own_rows = lax.axis_index("exp") * tok_local + jnp.arange(tok_local, dtype=jnp.int32)
    own_blocks = own_rows // BLK
    own_experts = jnp.take(block_experts, own_blocks, axis=0)
    source_expert = jnp.arange(exp_devices, dtype=jnp.int32) // group_size
    factor = jnp.sum(
        jnp.where(
            own_experts[None, :, :] == source_expert[:, None, None], route_weight[None, :, :], 0.0
        ),
        axis=2,
    )
    reduced = lax.psum_scatter(term_vals, ("sec", "hid"), scatter_dimension=1, tiled=True).astype(
        jnp.float32
    )
    width = reduced.shape[1]
    slot_grid = reduced.reshape(slot_count, BLK, width)
    safe_slot = jnp.maximum(slot_of_block, 0)
    expanded = jnp.take(slot_grid, safe_slot, axis=0)
    expanded = jnp.where(block_hit[:, None, None], expanded, jnp.zeros_like(expanded))
    outgoing = expanded.reshape(exp_devices, tok_local, width)
    received = lax.all_to_all(
        outgoing.astype(jnp.bfloat16), "exp", split_axis=0, concat_axis=0, tiled=True
    ).astype(outgoing.dtype)
    result = jnp.sum(received * factor[:, :, None], axis=0)
    return result.astype(jnp.bfloat16)


def solution(mesh):
    return jax.shard_map(
        per_device,
        mesh=mesh,
        in_specs=(
            P("exp", ("sec", "hid")),
            P(("sec", "hid")),
            P("exp", None),
            P(),
            P("sec", None, ("exp", "hid")),
            P("sec", None, ("exp", "hid")),
            P("sec", ("exp", "hid"), None),
        ),
        out_specs=P("exp", ("sec", "hid")),
        check_vma=False,
    )
```

profile of v0, /device:TPU:8, one launch (start us, length us, event | category | flops | bytes accessed | tf_op | source)
XLA Modules:
  0.0 313.2 jit_solution(5382523622550973638)
XLA Ops:
  6.5 0.8 compare_reduce_fusion
  7.4 0.2 reduce-window.4
  7.6 0.1 select_reduce_fusion.1
  7.7 0.1 fusion.16
  7.9 0.8 fusion.15
  8.7 39.5 %psum.7 = f32[32]{0:T(128)S(1)} all-reduce(f32[32]{0:T(128)S(1)} %fusion.15), channel_id=1, replica_groups=mesh['sec'=2,'exp'=32,'hid'=8] {'sec','hid'}, use_global_device_ids=true, to_apply=%region_5.6 | all-reduce | flops 32 | bytes 256 | tf_op jit(solution)/shard_map/psum | solution.py:33
  48.2 0.7 convert_element_type.37
  48.9 0.8 fusion.14
  49.7 47.2 %all_gather.6 = bf16[1024,256]{1,0:T(8,128)(2,1)S(1)} all-gather(bf16[32,256]{1,0:T(8,128)(2,1)S(1)} %fusion.14), channel_id=1, replica_groups=mesh['sec'=2,'exp'=32,'hid'=8] {'exp'}, dimensions={0}, use_global_device_ids=true | all-gather | bytes 540672 | tf_op jit(solution)/shard_map/all_gather | solution.py:36
  96.9 0.6 gather_fusion
  97.6 0.9 fusion.6
  98.5 81.6 %all-gather.2.cloned.1.call-done = bf16[512,4096]{1,0:T(8,128)(2,1)} async-done(((bf16[512,256]{1,0:T(8,128)(2,1)}), bf16[512,4096]{1,0:T(8,128)(2,1)}) %all-gather.2.cloned.1.call-update) | async-done | bytes 4194320 | tf_op jit(solution)/shard_map/all_gather | solution.py:41
  180.1 3.7 %fusion.4 = f32[512,128]{1,0:T(8,128)S(1)} fusion(bf16[512,4096]{1,0:T(8,128)(2,1)} %all-gather.2.cloned.1.call-done, bf16[1,4096,128]{2,1,0:T(8,128)(2,1)} %param.11), kind=kOutput, calls=%fused_computation.8 | convolution fusion | flops 536870912 | bytes 5505024 | tf_op jit(solution)/shard_map/dot_general | solution.py:42
  183.9 8.6 %convolution_convert_fusion = bf16[512,4096]{1,0:T(8,128)(2,1)} fusion(bf16[512,4096]{1,0:T(8,128)(2,1)} %all-gather.2.cloned.1.call-done, bf16[1,128,4096]{2,1,0:T(8,128)(2,1)S(1)} %copy-done, bf16[1,4096,128]{2,1,0:T(8,128)(2,1)S(1)} %copy-done.1, f32[512,128]{1,0:T(8,128)S(1)} %fusion.4), kind=kOutput, calls=%fused_computation.3 | convolution fusion | flops 1076232192 | bytes 10747904 | tf_op jit(solution)/shard_map/dot_general | solution.py:45
  192.6 0.1 broadcast_in_dim.109
  192.8 0.1 broadcast_in_dim.106
  192.9 82.3 %reduce-scatter.2.cloned.1.call-done = bf16[512,256]{1,0:T(8,128)(2,1)} async-done(((bf16[512,4096]{1,0:T(8,128)(2,1)}), bf16[512,256]{1,0:T(8,128)(2,1)}) %reduce-scatter.2.cloned.1.call-update) | async-done | bytes 262160 | tf_op jit(solution)/shard_map/reduce_scatter | solution.py:57
  275.2 1.5 gather_fusion.1
  276.7 1.0 select_convert_fusion
  277.7 9.2 %all-to-all-start = ((bf16[32,32,256]{2,1,0:T(8,128)(2,1)}), bf16[32,32,256]{2,1,0:T(8,128)(2,1)S(1)}, u32[]{:S(2)}, u32[]{:S(2)}) async-start(bf16[32,32,256]{2,1,0:T(8,128)(2,1)} %select_convert_fusion), calls=%async_computation.1 | async-start | bytes 1048576 | tf_op jit(solution)/shard_map/all_to_all | solution.py:66
  287.0 0.1 copy.12
  287.1 0.6 gather_fusion.2
  287.9 17.6 %all-to-all-done = bf16[32,32,256]{2,1,0:T(8,128)(2,1)S(1)} async-done(((bf16[32,32,256]{2,1,0:T(8,128)(2,1)}), bf16[32,32,256]{2,1,0:T(8,128)(2,1)S(1)}, u32[]{:S(2)}, u32[]{:S(2)}) %all-to-all-start) | async-done | bytes 524320 | tf_op jit(solution)/shard_map/all_to_all | solution.py:66
  305.5 0.8 multiply_reduce_fusion
  (30 shorter events, 0.6 us)
Async XLA Ops:
  6.5 177.3 %copy-start = (bf16[1,128,4096]{2,1,0:T(8,128)(2,1)S(1)}, bf16[1,128,4096]{2,1,0:T(8,128)(2,1)}, u32[]{:S(2)}) copy-start(bf16[1,128,4096]{2,1,0:T(8,128)(2,1)} %param.13) | copy-start | bytes 3145732
  6.5 177.3 %copy-start.1 = (bf16[1,4096,128]{2,1,0:T(8,128)(2,1)S(1)}, bf16[1,4096,128]{2,1,0:T(8,128)(2,1)}, u32[]{:S(2)}) copy-start(bf16[1,4096,128]{2,1,0:T(8,128)(2,1)} %param.12) | copy-start | bytes 3145732
  6.5 173.6 %all-gather.2.cloned.1.call-start = ((), (), s32[]{:S(2)}) async-start(), calls=%async_computation.2 | async-start | bytes 4456448 | tf_op jit(solution)/shard_map/all_gather | solution.py:41
  98.5 176.7 %reduce-scatter.2.cloned.1.call-start = ((), (), s32[]{:S(2)}) async-start(), calls=%async_computation.3 | async-start | bytes 4456448 | tf_op jit(solution)/shard_map/reduce_scatter | solution.py:57
  192.5 94.4 %copy-start.2 = (s32[8,2]{0,1:T(2,128)S(1)}, s32[8,2]{0,1:T(2,128)}, u32[]{:S(2)}) copy-start(s32[8,2]{0,1:T(2,128)} %param.10) | copy-start | bytes 196
  192.5 95.3 %copy-start.3 = (f32[32,2]{0,1:T(2,128)S(1)}, f32[32,2]{0,1:T(2,128)}, u32[]{:S(2)}) copy-start(f32[32,2]{0,1:T(2,128)} %param.9) | copy-start | bytes 772
  277.7 27.8 %all-to-all-start = ((bf16[32,32,256]{2,1,0:T(8,128)(2,1)}), bf16[32,32,256]{2,1,0:T(8,128)(2,1)S(1)}, u32[]{:S(2)}, u32[]{:S(2)}) async-start(bf16[32,32,256]{2,1,0:T(8,128)(2,1)} %select_convert_fusion), calls=%async_computation.1 | async-start | bytes 1048576 | tf_op jit(solution)/shard_map/all_to_all | solution.py:66
Sparse Core Ops, SparseCore 0:
  98.6 81.4 all-gather.1
  192.7 82.4 reduce-scatter.1
where the time goes:
time: 314 us; the launch traced here: 313 us
  waiting for transfers between devices  182 us (58%)
  blocking collectives  86.8 us (28%)
  between operations  13.5 us (4%)
  matrix products  12.4 us (4%)
  starting transfers between devices  9.24 us (3%)
  other arithmetic  6.52 us (2%)
  local copies, waits for them, and re-layouts  3.24 us (1%)
    reduce_scatter x1, waiting for transfers between devices, per_device(): lax.psum_scatter(term_vals, ('sec', 'hid'), scatter_dimension=1, tiled=True)  82.3 us
    all_gather x1, waiting for transfers between devices, per_device(): lax.all_gather(picked_rows, ('sec', 'hid'), axis=1, tiled=True)  81.6 us
    all_gather x1, blocking collectives, per_device(): gathered = lax.all_gather(normed, 'exp', axis=0, tiled=True)  47.2 us
    psum x1, blocking collectives, per_device(): square_total = lax.psum(square_part, ('sec', 'hid'))  39.5 us
    all_to_all x1, waiting for transfers between devices, per_device(): lax.all_to_all(outgoing.astype(jnp.bfloat16), 'exp', split_axis=0, concat...  17.6 us
    all_to_all x1, starting transfers between devices, per_device(): lax.all_to_all(outgoing.astype(jnp.bfloat16), 'exp', split_axis=0, concat...  9.2 us
    dot_general x1, matrix products, per_device(): jnp.dot(activated, down_local, preferred_element_type=jnp.float32)  8.64 us
  transfers between devices with their start and end apart: 3, of which 3 were waited for; matrix products, arithmetic and copies ran while one was open for 0% of the time, Pallas kernels for 0%

commit v1 on v0

v1 whole, which is shorter than its diff:
```python
import jax
import jax.numpy as jnp
from jax import lax
from jax.experimental import pallas as pl
from jax.experimental.pallas import tpu as pltpu
from jax.sharding import Mesh, PartitionSpec as P

EXPERTS = 8
BLK = 128
MOST = 4
F32 = jnp.float32
BF16 = jnp.bfloat16

GROUP = ("group",)
SQUARE = ("sec", "xlo")


def prep_kernel(x_ref, out_ref):
    n, rows, w = x_ref.shape
    rows -= 8
    copies = out_ref.shape[0]
    total = jnp.zeros((rows, w), F32)
    for z in range(n):
        x = x_ref[z, 0:rows, :].astype(F32)
        g = x_ref[z, rows : rows + 1, :].astype(F32)
        total = total + x * x
        y = (x * g).astype(BF16)
        for j in range(copies):
            out_ref[j, z * rows : (z + 1) * rows, :] = y
    col = jnp.sum(total, axis=1, keepdims=True)
    row = jnp.transpose(jnp.broadcast_to(col, (rows, rows)))[0:8, :]
    hi = row.astype(BF16).astype(F32)
    mid = (row - hi).astype(BF16).astype(F32)
    low = row - hi - mid
    which = lax.broadcasted_iota(jnp.int32, (8, rows), 0)
    parts = jnp.where(which == 0, hi, jnp.where(which == 1, mid, jnp.where(which == 2, low, 0.0)))
    parts = jnp.concatenate([parts, jnp.zeros((8, w - rows), F32)], axis=1).astype(BF16)
    for j in range(copies):
        out_ref[j, n * rows : n * rows + 8, :] = parts


def expert_kernel(x_ref, g0_ref, u0_ref, d0_ref, g1_ref, u1_ref, d1_ref, out_ref):
    _, tall, w = x_ref.shape
    rows = 128
    n = tall // rows
    features = 2 * n * w
    halves = []
    scales = []
    for x in range(2):
        pieces = [x_ref[2 * s + x, z * rows : (z + 1) * rows, :] for s in range(2) for z in range(n)]
        halves.append(jnp.concatenate(pieces, axis=1))
        parts = [x_ref[2 * s + x, n * rows : n * rows + 8, 0:rows].astype(F32) for s in range(2)]
        both = parts[0] + parts[1]
        total = both[0:1, :] + both[1:2, :] + both[2:3, :]
        inv = 1.0 / jnp.sqrt(total / features + 1e-05)
        scales.append(jnp.transpose(jnp.broadcast_to(inv, (rows, rows))))
    xs = jnp.concatenate(halves, axis=0)
    scale = jnp.concatenate(scales, axis=0)
    acts = []
    for g_ref, u_ref in ((g0_ref, u0_ref), (g1_ref, u1_ref)):
        acc = jnp.dot(xs, jnp.concatenate([g_ref[...], u_ref[...]], axis=1), preferred_element_type=F32)
        gate = acc[:, 0:rows] * scale
        up = acc[:, rows:] * scale
        acts.append((gate / (1.0 + jnp.exp(-gate)) * up).astype(BF16))
    act = jnp.concatenate(acts, axis=1)
    for s in range(2):
        for z in range(n):
            col = (s * n + z) * w
            down = jnp.concatenate([d0_ref[:, col : col + w], d1_ref[:, col : col + w]], axis=0)
            res = jnp.dot(act, down, preferred_element_type=F32).astype(BF16)
            for x in range(2):
                out_ref[2 * s + x, z * rows : (z + 1) * rows, :] = res[x * rows : (x + 1) * rows]


VM = pl.BlockSpec(memory_space=pltpu.VMEM)


def per_device(tokens, norm_gain, route_weight, block_experts, w_gate, w_up, w_down):
    rows, w = tokens.shape
    groups = lax.axis_size("group")
    n_hid = lax.axis_size("hid")
    me = lax.axis_index("group")
    gate0, up0, down0 = w_gate[0], w_up[0], w_down[0]
    swap = [(0, 1), (1, 0)]
    gate1 = lax.ppermute(gate0, "core", swap)
    up1 = lax.ppermute(up0, "core", swap)
    down1 = lax.ppermute(down0, "core", swap)

    hit = jnp.any(block_experts == me, axis=1)
    slot_of_block = jnp.maximum(jnp.cumsum(hit.astype(jnp.int32)) - 1, 0)
    slot_ids = jnp.arange(MOST, dtype=jnp.int32)
    match = (slot_of_block[None, :] == slot_ids[:, None]) & hit[None, :]
    block_of_slot = jnp.sum(jnp.where(match, jnp.arange(groups, dtype=jnp.int32)[None, :], 0), axis=1)

    blocks = lax.all_to_all(
        jnp.broadcast_to(tokens[None], (groups, rows, w)), GROUP, split_axis=0, concat_axis=0, tiled=True
    )
    picked = jnp.take(blocks, block_of_slot, axis=0, mode="clip").reshape(MOST * rows, w)
    picked = jnp.concatenate([picked, jnp.broadcast_to(norm_gain[None, :], (8, w))], axis=0)
    tall = MOST * rows
    wide = lax.all_to_all(
        jnp.broadcast_to(picked[None], (n_hid, tall + 8, w)), "hid", split_axis=0, concat_axis=0, tiled=True
    )
    ready = pl.pallas_call(
        prep_kernel,
        out_shape=jax.ShapeDtypeStruct((4, n_hid * tall + 8, w), BF16),
        in_specs=[VM],
        out_specs=VM,
        name="prep",
    )(wide)
    every = lax.all_to_all(ready, SQUARE, split_axis=0, concat_axis=0, tiled=True)
    partial = pl.pallas_call(
        expert_kernel,
        out_shape=jax.ShapeDtypeStruct((4, n_hid * tall, w), BF16),
        in_specs=[VM] * 7,
        out_specs=VM,
        name="expert",
    )(every, gate0, up0, down0, gate1, up1, down1)
    got = lax.all_to_all(partial, SQUARE, split_axis=0, concat_axis=0, tiled=True)
    summed = jnp.sum(got.astype(F32), axis=0).astype(BF16).reshape(n_hid, tall, w)
    got = lax.all_to_all(summed, "hid", split_axis=0, concat_axis=0, tiled=True)
    summed = jnp.sum(got.astype(F32), axis=0).astype(BF16).reshape(MOST, rows, w)
    outgoing = jnp.take(summed, slot_of_block, axis=0, mode="clip")
    back = lax.all_to_all(outgoing, GROUP, split_axis=0, concat_axis=0, tiled=True)
    mine = jnp.take(block_experts, me, axis=0, mode="clip")
    chosen = jnp.take(back, mine, axis=0, mode="clip").astype(F32)
    result = route_weight[:, 0:1] * chosen[0] + route_weight[:, 1:2] * chosen[1]
    return result.astype(BF16)


def solution(mesh):
    devices = mesh.devices.reshape(2, EXPERTS, 2, 2, 8)
    fine = Mesh(devices, ("sec", "group", "xlo", "core", "hid"))
    exp = ("group", "xlo", "core")
    return jax.shard_map(
        per_device,
        mesh=fine,
        in_specs=(
            P(exp, ("sec", "hid")),
            P(("sec", "hid")),
            P(exp, None),
            P(),
            P("sec", None, exp + ("hid",)),
            P("sec", None, exp + ("hid",)),
            P("sec", exp + ("hid",), None),
        ),
        out_specs=P(exp, ("sec", "hid")),
        check_vma=False,
    )
```

time: 314 us -> 152 us (0.48)
  waiting for transfers between devices: 182 us -> 49.5 us
  blocking collectives: 86.8 us -> 55 us
  starting transfers between devices: 9.24 us -> 27.2 us
  between operations: 13.5 us -> 0.12 us
  matrix products: 12.4 us -> 0 us
  Pallas kernels: 0 us -> 9.31 us
  local copies, waits for them, and re-layouts: 3.24 us -> 7.37 us
  other arithmetic: 6.52 us -> 3.03 us
    reduce_scatter x1 -> x0, waiting for transfers between devices: 82.3 us -> none  [per_device(): lax.psum_scatter(term_vals, ('sec', 'hid'), scatter_dimension=1, tiled=True)]
    all_gather x1 -> x0, waiting for transfers between devices: 81.6 us -> none  [per_device(): lax.all_gather(picked_rows, ('sec', 'hid'), axis=1, tiled=True)]
    all_to_all x0 -> x2, blocking collectives: none -> 55 us  [the longest x1 27.9 us: per_device(): lax.all_to_all(partial, SQUARE, split_axis=0, concat_axis=0, tiled=True)]
    all_gather x1 -> x0, blocking collectives: 47.2 us -> none  [per_device(): gathered = lax.all_gather(normed, 'exp', axis=0, tiled=True)]
    psum x1 -> x0, blocking collectives: 39.5 us -> none  [per_device(): square_total = lax.psum(square_part, ('sec', 'hid'))]
    all_to_all x1 -> x4, waiting for transfers between devices: 17.6 us -> 48 us  [the longest x1 16.2 us: per_device(): got = lax.all_to_all(summed, 'hid', split_axis=0, concat_axis=0, tiled=True)]
    dot_general x2 -> x0, matrix products: 12.4 us -> none  [the longest x1 8.64 us: per_device(): jnp.dot(activated, down_local, preferred_element_type=jnp.float32)]
    all_to_all x1 -> x4, starting transfers between devices: 9.2 us -> 20.9 us  [the longest x1 8.66 us: per_device(): lax.all_to_all(jnp.broadcast_to(tokens[None], (groups, rows, w)), GROUP,...]
  transfers between devices with their start and end apart: 3 -> 7, of which waited for: 3 -> 6; matrix products, arithmetic and copies ran while one was open for 0% -> 1% of each run, Pallas kernels for 0% -> 0%
where the time goes in v1:
time: 152 us
  blocking collectives  55 us (36%)
  waiting for transfers between devices  49.5 us (33%)
  starting transfers between devices  27.2 us (18%)
  Pallas kernels  9.31 us (6%)
  local copies, waits for them, and re-layouts  7.37 us (5%)
  other arithmetic  3.03 us (2%)
    all_to_all x1, blocking collectives, per_device(): lax.all_to_all(partial, SQUARE, split_axis=0, concat_axis=0, tiled=True)  27.9 us
    all_to_all x1, blocking collectives, per_device(): lax.all_to_all(jnp.broadcast_to(picked[None], (n_hid, tall + 8, w)), 'hid...  27.1 us
    all_to_all x1, waiting for transfers between devices, per_device(): got = lax.all_to_all(summed, 'hid', split_axis=0, concat_axis=0, tiled=True)  16.2 us
    all_to_all x1, waiting for transfers between devices, per_device(): lax.all_to_all(ready, SQUARE, split_axis=0, concat_axis=0, tiled=True)  12.2 us
    all_to_all x1, waiting for transfers between devices, per_device(): lax.all_to_all(outgoing, GROUP, split_axis=0, concat_axis=0, tiled=True)  10.3 us
    all_to_all x1, waiting for transfers between devices, per_device(): lax.all_to_all(jnp.broadcast_to(tokens[None], (groups, rows, w)), GROUP,...  9.23 us
    all_to_all x1, starting transfers between devices, per_device(): lax.all_to_all(jnp.broadcast_to(tokens[None], (groups, rows, w)), GROUP,...  8.66 us
    pallas_call x1, Pallas kernels, per_device(): pl.pallas_call(expert_kernel, out_shape=jax.ShapeDtypeStruct((4, n_hid *...  6.63 us
  transfers between devices with their start and end apart: 7, of which 6 were waited for; matrix products, arithmetic and copies ran while one was open for 1% of the time, Pallas kernels for 0%

profile of v1, /device:TPU:8, one launch (start us, length us, event | category | flops | bytes accessed | tf_op | source)
XLA Modules:
  0.0 151.6 jit_solution(11106091094477260646)
XLA Ops:
  0.0 1.4 broadcast_in_dim.48
  1.4 8.7 %all-to-all-start = ((bf16[8,32,256]{2,1,0:T(8,128)(2,1)}), bf16[8,32,256]{2,1,0:T(8,128)(2,1)S(1)}, u32[]{:S(2)}, u32[]{:S(2)}) async-start(bf16[8,32,256]{2,1,0:T(8,128)(2,1)} %broadcast_in_dim.48), calls=%async_computation | async-start | bytes 262144 | tf_op jit(solution)/shard_map/all_to_all | solution.py:95
  10.0 0.7 compare_reduce_fusion
  11.1 9.2 %all-to-all-done = bf16[8,32,256]{2,1,0:T(8,128)(2,1)S(1)} async-done(((bf16[8,32,256]{2,1,0:T(8,128)(2,1)}), bf16[8,32,256]{2,1,0:T(8,128)(2,1)S(1)}, u32[]{:S(2)}, u32[]{:S(2)}) %all-to-all-start) | async-done | bytes 131104 | tf_op jit(solution)/shard_map/all_to_all | solution.py:95
  20.9 0.7 broadcast_in_dim.52
  21.6 27.1 %all_to_all.30.x_ref = bf16[8,136,256]{2,1,0:T(8,128)(2,1)} all-to-all(bf16[8,136,256]{2,1,0:T(8,128)(2,1)S(1)} %broadcast_in_dim.53), channel_id=1, replica_groups=mesh['sec'=2,'group'=8,'xlo'=2,'core'=2,'hid'=8] {'hid'}, dimensions={0} | all-to-all | bytes 1114112 | tf_op jit(solution)/shard_map/all_to_all | solution.py:101
  48.7 2.7 %prep.1 = bf16[4,1032,256]{2,1,0:T(8,128)(2,1)} custom-call(bf16[8,136,256]{2,1,0:T(8,128)(2,1)} %all_to_all.30.x_ref), custom_call_target="tpu_custom_call" | custom-call | tf_op jit(solution)/shard_map/prep/pallas_call | solution.py:104
  51.4 5.0 %all-to-all-start.2 = ((bf16[4,1032,256]{2,1,0:T(8,128)(2,1)}), bf16[4,1032,256]{2,1,0:T(8,128)(2,1)S(1)}, u32[]{:S(2)}, u32[]{:S(2)}) async-start(bf16[4,1032,256]{2,1,0:T(8,128)(2,1)} %prep.1), calls=%async_computation.2 | async-start | bytes 4227072 | tf_op jit(solution)/shard_map/all_to_all | solution.py:111
  56.4 1.9 %collective-permute-start = (bf16[4096,128]{1,0:T(8,128)(2,1)S(1)}, bf16[4096,128]{1,0:T(8,128)(2,1)S(1)}, u32[]{:S(2)}, u32[]{:S(2)}) collective-permute-start(bf16[4096,128]{1,0:T(8,128)(2,1)S(1)} %bitcast.29), channel_id=1, source_target_pairs={{0,8},{8,0},{1,9},{9,1},{2,10},{10,2},{3,11},{11,3},{4,12},{12,4},... | collective-permute-start | bytes 3145736 | tf_op jit(solution)/shard_map/ppermute | solution.py:85
  58.3 2.4 %collective-permute-start.1 = (bf16[4096,128]{1,0:T(8,128)(2,1)}, bf16[4096,128]{1,0:T(8,128)(2,1)S(1)}, u32[]{:S(2)}, u32[]{:S(2)}) collective-permute-start(bf16[4096,128]{1,0:T(8,128)(2,1)} %bitcast.30), channel_id=1, source_target_pairs={{0,8},{8,0},{1,9},{9,1},{2,10},{10,2},{3,11},{11,3},{4,12},{12,4},... | collective-permute-start | bytes 3145736 | tf_op jit(solution)/shard_map/ppermute | solution.py:86
  60.7 1.9 %collective-permute-start.2 = (bf16[128,4096]{1,0:T(8,128)(2,1)}, bf16[128,4096]{1,0:T(8,128)(2,1)}, u32[]{:S(2)}, u32[]{:S(2)}) collective-permute-start(bf16[128,4096]{1,0:T(8,128)(2,1)} %bitcast.32), channel_id=1, source_target_pairs={{0,8},{8,0},{1,9},{9,1},{2,10},{10,2},{3,11},{11,3},{4,12},{12,4},... | collective-permute-start | bytes 3145736 | tf_op jit(solution)/shard_map/ppermute | solution.py:87
  63.6 1.0 copy-done.3
  64.6 1.0 collective-permute-done.2.d1_ref
  65.6 12.2 %all-to-all-done.2.x_ref = bf16[4,1032,256]{2,1,0:T(8,128)(2,1)S(1)} async-done(((bf16[4,1032,256]{2,1,0:T(8,128)(2,1)}), bf16[4,1032,256]{2,1,0:T(8,128)(2,1)S(1)}, u32[]{:S(2)}, u32[]{:S(2)}) %all-to-all-start.2) | async-done | bytes 2113568 | tf_op jit(solution)/shard_map/all_to_all | solution.py:111
  77.8 1.3 copy-done
  79.2 6.6 %expert.1 = bf16[4,1024,256]{2,1,0:T(8,128)(2,1)} custom-call(bf16[4,1032,256]{2,1,0:T(8,128)(2,1)} %copy-done, bf16[4096,128]{1,0:T(8,128)(2,1)} %bitcast.28, bf16[4096,128]{1,0:T(8,128)(2,1)} %bitcast.31, bf16[128,4096]{1,0:T(8,128)(2,1)} %bitcast.33, bf16[4096,128]{1,0:T(8,128)(2,1)} %copy-done.2, bf16[4096,128]{1,0:T(8,128)(2,1)} %copy-done.3, ...), custom_call_target="tpu_custom_call" | custom-call | tf_op jit(solution)/shard_map/expert/pallas_call | solution.py:112
  85.8 27.9 %all_to_all.31 = bf16[4,1024,256]{2,1,0:T(8,128)(2,1)S(1)} all-to-all(bf16[4,1024,256]{2,1,0:T(8,128)(2,1)} %expert.1), channel_id=1, replica_groups=mesh['sec'=2,'group'=8,'xlo'=2,'core'=2,'hid'=8] {'sec','xlo'}, dimensions={0} | all-to-all | bytes 4194304 | tf_op jit(solution)/shard_map/all_to_all | solution.py:119
  113.8 1.2 reduce_sum.34
  115.0 3.5 %all-to-all-start.4 = ((bf16[8,128,256]{2,1,0:T(8,128)(2,1)}), bf16[8,128,256]{2,1,0:T(8,128)(2,1)S(1)}, u32[]{:S(2)}, u32[]{:S(2)}) async-start(bf16[8,128,256]{2,1,0:T(8,128)(2,1)} %bitcast.7), calls=%async_computation.4 | async-start | bytes 1048576 | tf_op jit(solution)/shard_map/all_to_all | solution.py:121
  118.7 16.2 %all-to-all-done.4 = bf16[8,128,256]{2,1,0:T(8,128)(2,1)S(1)} async-done(((bf16[8,128,256]{2,1,0:T(8,128)(2,1)}), bf16[8,128,256]{2,1,0:T(8,128)(2,1)S(1)}, u32[]{:S(2)}, u32[]{:S(2)}) %all-to-all-start.4) | async-done | bytes 524320 | tf_op jit(solution)/shard_map/all_to_all | solution.py:121
  135.0 1.2 gather_fusion.1
  136.2 3.8 %all-to-all-start.5 = ((bf16[8,32,256]{2,1,0:T(8,128)(2,1)}), bf16[8,32,256]{2,1,0:T(8,128)(2,1)S(1)}, u32[]{:S(2)}, u32[]{:S(2)}) async-start(bf16[8,32,256]{2,1,0:T(8,128)(2,1)} %gather_fusion.1), calls=%async_computation.5 | async-start | bytes 262144 | tf_op jit(solution)/shard_map/all_to_all | solution.py:124
  139.9 10.3 %all-to-all-done.5 = bf16[8,32,256]{2,1,0:T(8,128)(2,1)S(1)} async-done(((bf16[8,32,256]{2,1,0:T(8,128)(2,1)}), bf16[8,32,256]{2,1,0:T(8,128)(2,1)S(1)}, u32[]{:S(2)}, u32[]{:S(2)}) %all-to-all-start.5) | async-done | bytes 131104 | tf_op jit(solution)/shard_map/all_to_all | solution.py:124
  150.9 0.7 fusion.2
  (27 shorter events, 2.7 us)
Async XLA Ops:
  1.4 18.9 %all-to-all-start = ((bf16[8,32,256]{2,1,0:T(8,128)(2,1)}), bf16[8,32,256]{2,1,0:T(8,128)(2,1)S(1)}, u32[]{:S(2)}, u32[]{:S(2)}) async-start(bf16[8,32,256]{2,1,0:T(8,128)(2,1)} %broadcast_in_dim.48), calls=%async_computation | async-start | bytes 262144 | tf_op jit(solution)/shard_map/all_to_all | solution.py:95
  51.4 5.0 %copy-start.1 = (bf16[1,4096,128]{2,1,0:T(8,128)(2,1)S(1)}, bf16[1,4096,128]{2,1,0:T(8,128)(2,1)}, u32[]{:S(2)}) copy-start(bf16[1,4096,128]{2,1,0:T(8,128)(2,1)} %param.11) | copy-start | bytes 3145732
  51.4 26.5 %all-to-all-start.2 = ((bf16[4,1032,256]{2,1,0:T(8,128)(2,1)}), bf16[4,1032,256]{2,1,0:T(8,128)(2,1)S(1)}, u32[]{:S(2)}, u32[]{:S(2)}) async-start(bf16[4,1032,256]{2,1,0:T(8,128)(2,1)} %prep.1), calls=%async_computation.2 | async-start | bytes 4227072 | tf_op jit(solution)/shard_map/all_to_all | solution.py:111
  56.4 6.3 %collective-permute-start = (bf16[4096,128]{1,0:T(8,128)(2,1)S(1)}, bf16[4096,128]{1,0:T(8,128)(2,1)S(1)}, u32[]{:S(2)}, u32[]{:S(2)}) collective-permute-start(bf16[4096,128]{1,0:T(8,128)(2,1)S(1)} %bitcast.29), channel_id=1, source_target_pairs={{0,8},{8,0},{1,9},{9,1},{2,10},{10,2},{3,11},{11,3},{4,12},{12,4},... | collective-permute-start | bytes 3145736 | tf_op jit(solution)/shard_map/ppermute | solution.py:85
  58.3 4.9 %collective-permute-start.1 = (bf16[4096,128]{1,0:T(8,128)(2,1)}, bf16[4096,128]{1,0:T(8,128)(2,1)S(1)}, u32[]{:S(2)}, u32[]{:S(2)}) collective-permute-start(bf16[4096,128]{1,0:T(8,128)(2,1)} %bitcast.30), channel_id=1, source_target_pairs={{0,8},{8,0},{1,9},{9,1},{2,10},{10,2},{3,11},{11,3},{4,12},{12,4},... | collective-permute-start | bytes 3145736 | tf_op jit(solution)/shard_map/ppermute | solution.py:86
  60.7 4.9 %collective-permute-start.2 = (bf16[128,4096]{1,0:T(8,128)(2,1)}, bf16[128,4096]{1,0:T(8,128)(2,1)}, u32[]{:S(2)}, u32[]{:S(2)}) collective-permute-start(bf16[128,4096]{1,0:T(8,128)(2,1)} %bitcast.32), channel_id=1, source_target_pairs={{0,8},{8,0},{1,9},{9,1},{2,10},{10,2},{3,11},{11,3},{4,12},{12,4},... | collective-permute-start | bytes 3145736 | tf_op jit(solution)/shard_map/ppermute | solution.py:87
  62.7 1.0 copy-start.2
  63.6 1.0 copy-start.3
  77.8 1.3 copy-start
  113.7 4.7 %copy-start.4 = (s32[8,2]{0,1:T(2,128)S(1)}, s32[8,2]{0,1:T(2,128)}, u32[]{:S(2)}) copy-start(s32[8,2]{0,1:T(2,128)} %param.10) | copy-start | bytes 196
  113.7 26.2 %copy-start.5 = (f32[32,2]{0,1:T(2,128)S(1)}, f32[32,2]{0,1:T(2,128)}, u32[]{:S(2)}) copy-start(f32[32,2]{0,1:T(2,128)} %param.9) | copy-start | bytes 772
  115.0 19.9 %all-to-all-start.4 = ((bf16[8,128,256]{2,1,0:T(8,128)(2,1)}), bf16[8,128,256]{2,1,0:T(8,128)(2,1)S(1)}, u32[]{:S(2)}, u32[]{:S(2)}) async-start(bf16[8,128,256]{2,1,0:T(8,128)(2,1)} %bitcast.7), calls=%async_computation.4 | async-start | bytes 1048576 | tf_op jit(solution)/shard_map/all_to_all | solution.py:121
  136.2 14.1 %all-to-all-start.5 = ((bf16[8,32,256]{2,1,0:T(8,128)(2,1)}), bf16[8,32,256]{2,1,0:T(8,128)(2,1)S(1)}, u32[]{:S(2)}, u32[]{:S(2)}) async-start(bf16[8,32,256]{2,1,0:T(8,128)(2,1)} %gather_fusion.1), calls=%async_computation.5 | async-start | bytes 262144 | tf_op jit(solution)/shard_map/all_to_all | solution.py:124

commit v2 on v1

v2 whole, which is shorter than its diff:
```python
import jax
import jax.numpy as jnp
from jax import lax
from jax.experimental import pallas as pl
from jax.experimental.pallas import tpu as pltpu
from jax.sharding import Mesh, PartitionSpec as P


EXPERTS = 8
MOST = 4
HID = 8
F32 = jnp.float32
BF16 = jnp.bfloat16

GROUP = ("group",)
SQUARE = ("sec", "xlo")


def prep_kernel(x_ref, out_ref, y_ref, sems):
    n, rows, w = x_ref.shape
    rows -= 8
    copies = out_ref.shape[0]
    total = jnp.zeros((rows, w), F32)
    for z in range(n):
        x = x_ref[z, 0:rows, :].astype(F32)
        g = x_ref[z, rows : rows + 1, :].astype(F32)
        total = total + x * x
        y_ref[z * rows : (z + 1) * rows, :] = (x * g).astype(BF16)
    col = jnp.sum(total, axis=1, keepdims=True)
    row = jnp.transpose(jnp.broadcast_to(col, (rows, rows)))[0:8, :]
    hi = row.astype(BF16).astype(F32)
    mid = (row - hi).astype(BF16).astype(F32)
    low = row - hi - mid
    which = lax.broadcasted_iota(jnp.int32, (8, rows), 0)
    parts = jnp.where(which == 0, hi, jnp.where(which == 1, mid, jnp.where(which == 2, low, 0.0)))
    y_ref[n * rows : n * rows + 8, :] = jnp.concatenate([parts, jnp.zeros((8, w - rows), F32)], axis=1).astype(BF16)
    sends = [pltpu.make_async_copy(y_ref, out_ref.at[j], sems.at[j]) for j in range(copies)]
    for send in sends:
        send.start()
    for send in sends:
        send.wait()


def gate_up_kernel(x_ref, g0, u0, g1, u1, act_ref, w_ref, sems):
    _, tall, w = x_ref.shape
    n = HID
    rows = (tall - 8) // n
    depth = n * w
    ff = g0.shape[1]
    loads = []
    for s in range(2):
        for c, pair in enumerate(((g0, u0), (g1, u1))):
            for k, ref in enumerate(pair):
                loads.append(
                    pltpu.make_async_copy(
                        ref.at[s * depth : (s + 1) * depth, :],
                        w_ref.at[c, s * depth : (s + 1) * depth, k * ff : (k + 1) * ff],
                        sems.at[len(loads)],
                    )
                )
    for load in loads:
        load.start()
    scales = []
    for x in range(2):
        parts = [x_ref[2 * s + x, n * rows : n * rows + 8, 0:rows].astype(F32) for s in range(2)]
        both = parts[0] + parts[1]
        total = both[0:1, :] + both[1:2, :] + both[2:3, :]
        inv = 1.0 / jnp.sqrt(total / (2 * depth) + 1e-05)
        scales.append(jnp.transpose(jnp.broadcast_to(inv, (rows, rows))))
    scale = jnp.concatenate(scales, axis=0)
    accs = [None, None]
    for s in range(2):
        xs = jnp.concatenate(
            [
                jnp.concatenate([x_ref[2 * s + x, z * rows : (z + 1) * rows, :] for z in range(n)], axis=1)
                for x in range(2)
            ],
            axis=0,
        )
        for c in range(2):
            loads[4 * s + 2 * c].wait()
            loads[4 * s + 2 * c + 1].wait()
            part = jnp.dot(xs, w_ref[c, s * depth : (s + 1) * depth, :], preferred_element_type=F32)
            accs[c] = part if accs[c] is None else accs[c] + part
    for c, acc in enumerate(accs):
        gate = acc[:, 0:ff] * scale
        up = acc[:, ff:] * scale
        act = (gate / (1.0 + jnp.exp(-gate)) * up).astype(BF16)
        for s in range(2):
            for x in range(2):
                act_ref[2 * s + x, :, c * ff : (c + 1) * ff] = act[x * rows : (x + 1) * rows]


def down_kernel(where_ref, act_ref, *refs):
    *downs, out_ref, w_ref, sems = refs
    n, _, w = out_ref.shape
    ff = downs[0].shape[0]
    half = n * w // 2
    loads = []
    for h in range(2):
        for i, ref in enumerate(downs):
            loads.append(
                pltpu.make_async_copy(
                    ref.at[:, h * half : (h + 1) * half],
                    w_ref.at[i * ff : (i + 1) * ff, h * half : (h + 1) * half],
                    sems.at[len(loads)],
                )
            )
    for load in loads:
        load.start()
    act = jnp.concatenate([act_ref[where_ref[k]] for k in range(4)], axis=1)
    for h in range(2):
        for load in loads[8 * h : 8 * h + 8]:
            load.wait()
        for z in range(h * n // 2, (h + 1) * n // 2):
            out_ref[z] = jnp.dot(act, w_ref[:, z * w : (z + 1) * w], preferred_element_type=F32).astype(BF16)


VM = pl.BlockSpec(memory_space=pltpu.VMEM)
SM = pl.BlockSpec(memory_space=pltpu.SMEM)
ANY = pl.BlockSpec(memory_space=pl.ANY)


def vm(x):
    return pltpu.with_memory_space_constraint(x, pltpu.VMEM)


def prepared(x):
    n, rows, w = x.shape
    tall = n * (rows - 8) + 8
    return pl.pallas_call(
        prep_kernel,
        out_shape=pltpu.HBM((4, tall, w), BF16),
        in_specs=[VM],
        out_specs=ANY,
        scratch_shapes=[pltpu.VMEM((tall, w), BF16), pltpu.SemaphoreType.DMA((4,))],
        compiler_params=pltpu.CompilerParams(vmem_limit_bytes=4 << 20),
        name="prep",
    )(vm(x))


def gated(x, weights):
    _, tall, _ = x.shape
    deep, ff = weights[0].shape
    return pl.pallas_call(
        gate_up_kernel,
        out_shape=jax.ShapeDtypeStruct((4, (tall - 8) // HID, 2 * ff), BF16),
        in_specs=[VM] + [ANY] * 4,
        out_specs=VM,
        scratch_shapes=[pltpu.VMEM((2, deep, 2 * ff), BF16), pltpu.SemaphoreType.DMA((8,))],
        compiler_params=pltpu.CompilerParams(vmem_limit_bytes=16 << 20),
        name="gate_up",
    )(vm(x), *weights)


def lowered(where, act, downs):
    _, rows, _ = act.shape
    ff, wide = downs[0].shape
    return pl.pallas_call(
        down_kernel,
        out_shape=jax.ShapeDtypeStruct((HID, rows, wide // HID), BF16),
        in_specs=[SM, VM] + [ANY] * 8,
        out_specs=VM,
        scratch_shapes=[pltpu.VMEM((8 * ff, wide), BF16), pltpu.SemaphoreType.DMA((16,))],
        compiler_params=pltpu.CompilerParams(vmem_limit_bytes=16 << 20),
        name="down",
    )(where, vm(act), *downs)


def exchange(x, axes):
    return lax.all_to_all(x, axes, split_axis=0, concat_axis=0, tiled=True)


def added(x):
    return jnp.sum(x.astype(F32), axis=0).astype(BF16)


def shifted(x, flip):
    return lax.ppermute(x, SQUARE, [(i, i ^ flip) for i in range(4)])


def layer(tokens, norm_gain, route_weight, block_experts, w_gate, w_up, w_down):
    rows, w = tokens.shape
    groups = lax.axis_size("group")
    n_hid = lax.axis_size("hid")
    me = lax.axis_index("group")
    gate0, up0, down0 = w_gate[0], w_up[0], w_down[0]
    sec = lax.axis_index("sec")
    place = sec * 2 + lax.axis_index("xlo")
    part = down0.shape[1] // 2
    down_here = lax.dynamic_slice_in_dim(down0, sec * part, part, 1)
    down_away = lax.dynamic_slice_in_dim(down0, (1 - sec) * part, part, 1)
    direct = [down_here]
    for flip, source in ((1, down_here), (2, down_away), (3, down_away)):
        direct.append(shifted(source, flip))

    def swapped(x):
        return lax.ppermute(x, "core", [(0, 1), (1, 0)])

    gate1, up1 = swapped(gate0), swapped(up0)
    downs = [d for piece in direct for d in (piece, swapped(piece))]
    where = place ^ jnp.arange(4, dtype=jnp.int32)

    hit = jnp.any(block_experts == me, axis=1)
    slot_of_block = jnp.maximum(jnp.cumsum(hit.astype(jnp.int32)) - 1, 0)
    slot_ids = jnp.arange(MOST, dtype=jnp.int32)
    match = (slot_of_block[None, :] == slot_ids[:, None]) & hit[None, :]
    block_of_slot = jnp.sum(jnp.where(match, jnp.arange(groups, dtype=jnp.int32)[None, :], 0), axis=1)

    mine = jnp.take(block_experts, me, axis=0, mode="clip")
    named = mine[None, :] == jnp.arange(EXPERTS, dtype=jnp.int32)[:, None]
    factor = jnp.sum(jnp.where(named[:, None, :], route_weight[None], 0.0), axis=2)

    blocks = exchange(jnp.broadcast_to(tokens[None], (groups, rows, w)), GROUP)
    tall = MOST * rows
    picked = jnp.take(blocks, block_of_slot, axis=0, mode="clip").reshape(tall, w)
    picked = jnp.concatenate([picked, jnp.broadcast_to(norm_gain[None, :], (8, w))], axis=0)
    wide = exchange(jnp.broadcast_to(picked[None], (n_hid, tall + 8, w)), "hid")
    every = exchange(prepared(wide), SQUARE)
    act = exchange(gated(every, (gate0, up0, gate1, up1)), SQUARE)
    summed = added(exchange(lowered(where, act, downs), "hid")).reshape(MOST, rows, w)
    outgoing = jnp.take(summed, slot_of_block, axis=0, mode="clip")
    back = exchange(outgoing, GROUP)
    return jnp.sum(back.astype(F32) * factor[:, :, None], axis=0).astype(BF16)


def solution(mesh):
    devices = mesh.devices.reshape(2, EXPERTS, 2, 2, 8)
    fine = Mesh(devices, ("sec", "group", "xlo", "core", "hid"))
    exp = ("group", "xlo", "core")
    return jax.shard_map(
        layer,
        mesh=fine,
        in_specs=(
            P(exp, ("sec", "hid")),
            P(("sec", "hid")),
            P(exp, None),
            P(),
            P("sec", None, exp + ("hid",)),
            P("sec", None, exp + ("hid",)),
            P("sec", exp + ("hid",), None),
        ),
        out_specs=P(exp, ("sec", "hid")),
        check_vma=False,
    )
```

time: 152 us -> 161 us (1.059)
  blocking collectives: 55 us -> 27 us
  starting transfers between devices: 27.2 us -> 47.9 us
  waiting for transfers between devices: 49.5 us -> 66.7 us
  local copies, waits for them, and re-layouts: 7.37 us -> 5.28 us
    all_to_all x2 -> x1, blocking collectives: 55 us -> 27 us  [exchange(): return lax.all_to_all(x, axes, split_axis=0, concat_axis=0, tiled=True)]
    ppermute x3 -> x9, waiting for transfers between devices: 1.51 us -> 24.9 us  [the longest x3 24.8 us: shifted(): return lax.ppermute(x, SQUARE, [(i, i ^ flip) for i in range(4)])]
    ppermute x3 -> x9, starting transfers between devices: 6.24 us -> 22.2 us  [the longest x6 13 us: swapped(): return lax.ppermute(x, 'core', [(0, 1), (1, 0)])]
    all_to_all x4 -> x5, waiting for transfers between devices: 48 us -> 41.9 us  [exchange(): return lax.all_to_all(x, axes, split_axis=0, concat_axis=0, tiled=True)]
    all_to_all x4 -> x5, starting transfers between devices: 20.9 us -> 25.7 us  [exchange(): return lax.all_to_all(x, axes, split_axis=0, concat_axis=0, tiled=True)]
    unnamed x12 -> x4, local copies, waits for them, and re-layouts: 2.8 us -> 0.01 us
    pallas_call x2 -> x3, Pallas kernels: 9.31 us -> 10.5 us  [the longest x1 5.08 us: gated(): pl.pallas_call(gate_up_kernel, out_shape=jax.ShapeDtypeStruct((4, (tall -...]
  transfers between devices with their start and end apart: 7 -> 14, of which waited for: 6 -> 6; matrix products, arithmetic and copies ran while one was open for 1% -> 2% of each run, Pallas kernels for 0% -> 3%
where the time goes in v2:
time: 161 us; the launch traced here: 160 us
  waiting for transfers between devices  66.7 us (41%)
  starting transfers between devices  47.9 us (30%)
  blocking collectives  27 us (17%)
  Pallas kernels  10.5 us (7%)
  local copies, waits for them, and re-layouts  5.28 us (3%)
  other arithmetic  1.97 us (1%)
    all_to_all x5, waiting for transfers between devices, exchange(): return lax.all_to_all(x, axes, split_axis=0, concat_axis=0, tiled=True)  41.9 us
    all_to_all x1, blocking collectives, exchange(): return lax.all_to_all(x, axes, split_axis=0, concat_axis=0, tiled=True)  27 us
    all_to_all x5, starting transfers between devices, exchange(): return lax.all_to_all(x, axes, split_axis=0, concat_axis=0, tiled=True)  25.7 us
    ppermute x3, waiting for transfers between devices, shifted(): return lax.ppermute(x, SQUARE, [(i, i ^ flip) for i in range(4)])  24.8 us
    ppermute x6, starting transfers between devices, swapped(): return lax.ppermute(x, 'core', [(0, 1), (1, 0)])  13 us
    ppermute x3, starting transfers between devices, shifted(): return lax.ppermute(x, SQUARE, [(i, i ^ flip) for i in range(4)])  9.22 us
    pallas_call x1, Pallas kernels, gated(): pl.pallas_call(gate_up_kernel, out_shape=jax.ShapeDtypeStruct((4, (tall -...  5.08 us
    pallas_call x1, Pallas kernels, lowered(): pl.pallas_call(down_kernel, out_shape=jax.ShapeDtypeStruct((HID, rows, wi...  3.76 us
  transfers between devices with their start and end apart: 14, of which 6 were waited for; matrix products, arithmetic and copies ran while one was open for 2% of the time, Pallas kernels for 3%

profile of v2, /device:TPU:8, one launch (start us, length us, event | category | flops | bytes accessed | tf_op | source)
XLA Modules:
  0.0 159.6 jit_solution(13045284688362483453)
XLA Ops:
  1.4 8.7 %all-to-all-start = ((bf16[8,32,256]{2,1,0:T(8,128)(2,1)}), bf16[8,32,256]{2,1,0:T(8,128)(2,1)S(1)}, u32[]{:S(2)}, u32[]{:S(2)}) async-start(bf16[8,32,256]{2,1,0:T(8,128)(2,1)} %broadcast_in_dim.48), calls=%async_computation | async-start | bytes 262144 | tf_op jit(solution)/shard_map/all_to_all | solution.py:171
  11.1 9.2 %all-to-all-done = bf16[8,32,256]{2,1,0:T(8,128)(2,1)S(1)} async-done(((bf16[8,32,256]{2,1,0:T(8,128)(2,1)}), bf16[8,32,256]{2,1,0:T(8,128)(2,1)S(1)}, u32[]{:S(2)}, u32[]{:S(2)}) %all-to-all-start) | async-done | bytes 131104 | tf_op jit(solution)/shard_map/all_to_all | solution.py:171
  21.6 27.0 %all_to_all.30.x_ref = bf16[8,136,256]{2,1,0:T(8,128)(2,1)S(1)} all-to-all(bf16[8,136,256]{2,1,0:T(8,128)(2,1)S(1)} %broadcast_in_dim.74), channel_id=1, replica_groups=mesh['sec'=2,'group'=8,'xlo'=2,'core'=2,'hid'=8] {'hid'}, dimensions={0} | all-to-all | bytes 1114112 | tf_op jit(solution)/shard_map/all_to_all | solution.py:171
  48.6 1.7 %prep.1 = bf16[4,1032,256]{2,1,0:T(8,128)(2,1)} custom-call(bf16[8,136,256]{2,1,0:T(8,128)(2,1)S(1)} %all_to_all.30.x_ref), custom_call_target="tpu_custom_call" | custom-call | tf_op jit(solution)/shard_map/prep/pallas_call | solution.py:131
  50.2 4.9 %all-to-all-start.2 = ((bf16[4,1032,256]{2,1,0:T(8,128)(2,1)}), bf16[4,1032,256]{2,1,0:T(8,128)(2,1)S(1)}, u32[]{:S(2)}, u32[]{:S(2)}) async-start(bf16[4,1032,256]{2,1,0:T(8,128)(2,1)} %prep.1), calls=%async_computation.2 | async-start | bytes 4227072 | tf_op jit(solution)/shard_map/all_to_all | solution.py:171
  55.1 1.9 %collective-permute-start = (bf16[4096,128]{1,0:T(8,128)(2,1)}, bf16[4096,128]{1,0:T(8,128)(2,1)}, u32[]{:S(2)}, u32[]{:S(2)}) collective-permute-start(bf16[4096,128]{1,0:T(8,128)(2,1)} %bitcast.3.g0), channel_id=1, source_target_pairs={{0,8},{8,0},{1,9},{9,1},{2,10},{10,2},{3,11},{11,3},{4,12},{12,4},... | collective-permute-start | bytes 3145736 | tf_op jit(solution)/shard_map/ppermute | solution.py:198
  57.0 2.4 %collective-permute-start.1 = (bf16[4096,128]{1,0:T(8,128)(2,1)}, bf16[4096,128]{1,0:T(8,128)(2,1)}, u32[]{:S(2)}, u32[]{:S(2)}) collective-permute-start(bf16[4096,128]{1,0:T(8,128)(2,1)} %bitcast.4.u0), channel_id=1, source_target_pairs={{0,8},{8,0},{1,9},{9,1},{2,10},{10,2},{3,11},{11,3},{4,12},{12,4},... | collective-permute-start | bytes 3145736 | tf_op jit(solution)/shard_map/ppermute | solution.py:198
  60.8 3.4 %collective-permute-start.3 = (bf16[128,2048]{1,0:T(8,128)(2,1)S(1)}, bf16[128,2048]{1,0:T(8,128)(2,1)S(1)}, u32[]{:S(2)}, u32[]{:S(2)}) collective-permute-start(bf16[128,2048]{1,0:T(8,128)(2,1)S(1)} %get-tuple-element.17.refs_0_), channel_id=1, source_target_pairs={{0,16},{16,0},{256,272},{272,256},{1,17},{17,1},{257,273},{273,257... | collective-permute-start | bytes 1572872 | tf_op jit(solution)/shard_map/ppermute | solution.py:179
  64.1 2.5 %collective-permute-start.5 = (bf16[128,2048]{1,0:T(8,128)(2,1)S(1)}, bf16[128,2048]{1,0:T(8,128)(2,1)}, u32[]{:S(2)}, u32[]{:S(2)}) collective-permute-start(bf16[128,2048]{1,0:T(8,128)(2,1)S(1)} %get-tuple-element.16), channel_id=1, source_target_pairs={{0,256},{16,272},{256,0},{272,16},{1,257},{17,273},{257,1},{273,17... | collective-permute-start | bytes 1572872 | tf_op jit(solution)/shard_map/ppermute | solution.py:179
  66.6 3.4 %collective-permute-start.7 = (bf16[128,2048]{1,0:T(8,128)(2,1)S(1)}, bf16[128,2048]{1,0:T(8,128)(2,1)}, u32[]{:S(2)}, u32[]{:S(2)}) collective-permute-start(bf16[128,2048]{1,0:T(8,128)(2,1)S(1)} %get-tuple-element.16), channel_id=1, source_target_pairs={{0,272},{16,256},{256,16},{272,0},{1,273},{17,257},{257,17},{273,1... | collective-permute-start | bytes 1572872 | tf_op jit(solution)/shard_map/ppermute | solution.py:179
  70.0 22.1 %collective-permute-done.3.refs_2_ = bf16[128,2048]{1,0:T(8,128)(2,1)S(1)} collective-permute-done((bf16[128,2048]{1,0:T(8,128)(2,1)S(1)}, bf16[128,2048]{1,0:T(8,128)(2,1)S(1)}, u32[]{:S(2)}, u32[]{:S(2)}) %collective-permute-start.3) | collective-permute-done | bytes 524320 | tf_op jit(solution)/shard_map/ppermute | solution.py:179
  92.1 1.9 %collective-permute-start.2 = (bf16[128,2048]{1,0:T(8,128)(2,1)S(1)}, bf16[128,2048]{1,0:T(8,128)(2,1)}, u32[]{:S(2)}, u32[]{:S(2)}) collective-permute-start(bf16[128,2048]{1,0:T(8,128)(2,1)S(1)} %get-tuple-element.17.refs_0_), channel_id=1, source_target_pairs={{0,8},{8,0},{1,9},{9,1},{2,10},{10,2},{3,11},{11,3},{4,12},{12,4},... | collective-permute-start | bytes 1572872 | tf_op jit(solution)/shard_map/ppermute | solution.py:198
  94.1 2.4 %collective-permute-start.4 = (bf16[128,2048]{1,0:T(8,128)(2,1)S(1)}, bf16[128,2048]{1,0:T(8,128)(2,1)}, u32[]{:S(2)}, u32[]{:S(2)}) collective-permute-start(bf16[128,2048]{1,0:T(8,128)(2,1)S(1)} %collective-permute-done.3.refs_2_), channel_id=1, source_target_pairs={{0,8},{8,0},{1,9},{9,1},{2,10},{10,2},{3,11},{11,3},{4,12},{12,4},... | collective-permute-start | bytes 1572872 | tf_op jit(solution)/shard_map/ppermute | solution.py:198
  96.5 2.7 %collective-permute-done.7.refs_6_ = bf16[128,2048]{1,0:T(8,128)(2,1)} collective-permute-done((bf16[128,2048]{1,0:T(8,128)(2,1)S(1)}, bf16[128,2048]{1,0:T(8,128)(2,1)}, u32[]{:S(2)}, u32[]{:S(2)}) %collective-permute-start.7) | collective-permute-done | bytes 524320 | tf_op jit(solution)/shard_map/ppermute | solution.py:179
  99.2 1.9 %collective-permute-start.6 = (bf16[128,2048]{1,0:T(8,128)(2,1)}, bf16[128,2048]{1,0:T(8,128)(2,1)}, u32[]{:S(2)}, u32[]{:S(2)}) collective-permute-start(bf16[128,2048]{1,0:T(8,128)(2,1)} %collective-permute-done.5.refs_4_), channel_id=1, source_target_pairs={{0,8},{8,0},{1,9},{9,1},{2,10},{10,2},{3,11},{11,3},{4,12},{12,4},... | collective-permute-start | bytes 1572872 | tf_op jit(solution)/shard_map/ppermute | solution.py:198
  101.1 2.4 %collective-permute-start.8 = (bf16[128,2048]{1,0:T(8,128)(2,1)}, bf16[128,2048]{1,0:T(8,128)(2,1)}, u32[]{:S(2)}, u32[]{:S(2)}) collective-permute-start(bf16[128,2048]{1,0:T(8,128)(2,1)} %collective-permute-done.7.refs_6_), channel_id=1, source_target_pairs={{0,8},{8,0},{1,9},{9,1},{2,10},{10,2},{3,11},{11,3},{4,12},{12,4},... | collective-permute-start | bytes 1572872 | tf_op jit(solution)/shard_map/ppermute | solution.py:198
  103.6 5.1 %gate_up.1 = bf16[4,128,256]{2,1,0:T(8,128)(2,1)} custom-call(bf16[4,1032,256]{2,1,0:T(8,128)(2,1)S(1)} %all-to-all-done.2.x_ref, bf16[4096,128]{1,0:T(8,128)(2,1)} %bitcast.3.g0, bf16[4096,128]{1,0:T(8,128)(2,1)} %bitcast.4.u0, bf16[4096,128]{1,0:T(8,128)(2,1)} %collective-permute-done.g1, bf16[4096,128]{1,0:T(8,128)(2,1)} %collective-permute-done.1.u1), custom_call_target="tpu_custom_call" | custom-call | tf_op jit(solution)/shard_map/gate_up/pallas_call | solution.py:145
  108.6 4.9 %all-to-all-start.3 = ((bf16[4,128,256]{2,1,0:T(8,128)(2,1)}), bf16[4,128,256]{2,1,0:T(8,128)(2,1)S(1)}, u32[]{:S(2)}, u32[]{:S(2)}) async-start(bf16[4,128,256]{2,1,0:T(8,128)(2,1)} %gate_up.1), calls=%async_computation.3 | async-start | bytes 524288 | tf_op jit(solution)/shard_map/all_to_all | solution.py:171
  113.5 5.0 %all-to-all-done.3.act_ref = bf16[4,128,256]{2,1,0:T(8,128)(2,1)S(1)} async-done(((bf16[4,128,256]{2,1,0:T(8,128)(2,1)}), bf16[4,128,256]{2,1,0:T(8,128)(2,1)S(1)}, u32[]{:S(2)}, u32[]{:S(2)}) %all-to-all-start.3) | async-done | bytes 262176 | tf_op jit(solution)/shard_map/all_to_all | solution.py:171
  118.6 3.8 %down.1 = bf16[8,128,256]{2,1,0:T(8,128)(2,1)} custom-call(s32[4]{0:T(128)S(1)} %iota_xor_fusion.where_ref, bf16[4,128,256]{2,1,0:T(8,128)(2,1)S(1)} %all-to-all-done.3.act_ref, bf16[128,2048]{1,0:T(8,128)(2,1)S(1)} %get-tuple-element.17.refs_0_, bf16[128,2048]{1,0:T(8,128)(2,1)} %collective-permute-done.2.refs_1_, ...), custom_call_target="tpu_custom_call" | custom-call | tf_op jit(solution)/shard_map/down/pallas_call | solution.py:159
  122.3 3.5 %all-to-all-start.4 = ((bf16[8,128,256]{2,1,0:T(8,128)(2,1)}), bf16[8,128,256]{2,1,0:T(8,128)(2,1)S(1)}, u32[]{:S(2)}, u32[]{:S(2)}) async-start(bf16[8,128,256]{2,1,0:T(8,128)(2,1)} %down.1), calls=%async_computation.4 | async-start | bytes 1048576 | tf_op jit(solution)/shard_map/all_to_all | solution.py:171
  126.0 17.5 %all-to-all-done.4 = bf16[8,128,256]{2,1,0:T(8,128)(2,1)S(1)} async-done(((bf16[8,128,256]{2,1,0:T(8,128)(2,1)}), bf16[8,128,256]{2,1,0:T(8,128)(2,1)S(1)}, u32[]{:S(2)}, u32[]{:S(2)}) %all-to-all-start.4) | async-done | bytes 524320 | tf_op jit(solution)/shard_map/all_to_all | solution.py:171
  144.8 3.8 %all-to-all-start.5 = ((bf16[8,32,256]{2,1,0:T(8,128)(2,1)}), bf16[8,32,256]{2,1,0:T(8,128)(2,1)S(1)}, u32[]{:S(2)}, u32[]{:S(2)}) async-start(bf16[8,32,256]{2,1,0:T(8,128)(2,1)} %gather_fusion.1), calls=%async_computation.5 | async-start | bytes 262144 | tf_op jit(solution)/shard_map/all_to_all | solution.py:171
  148.7 10.1 %all-to-all-done.5 = bf16[8,32,256]{2,1,0:T(8,128)(2,1)S(1)} async-done(((bf16[8,32,256]{2,1,0:T(8,128)(2,1)}), bf16[8,32,256]{2,1,0:T(8,128)(2,1)S(1)}, u32[]{:S(2)}, u32[]{:S(2)}) %all-to-all-start.5) | async-done | bytes 131104 | tf_op jit(solution)/shard_map/all_to_all | solution.py:171
  (32 shorter events, 7.3 us)
Async XLA Ops:
  1.4 18.9 %all-to-all-start = ((bf16[8,32,256]{2,1,0:T(8,128)(2,1)}), bf16[8,32,256]{2,1,0:T(8,128)(2,1)S(1)}, u32[]{:S(2)}, u32[]{:S(2)}) async-start(bf16[8,32,256]{2,1,0:T(8,128)(2,1)} %broadcast_in_dim.48), calls=%async_computation | async-start | bytes 262144 | tf_op jit(solution)/shard_map/all_to_all | solution.py:171
  50.2 53.3 %all-to-all-start.2 = ((bf16[4,1032,256]{2,1,0:T(8,128)(2,1)}), bf16[4,1032,256]{2,1,0:T(8,128)(2,1)S(1)}, u32[]{:S(2)}, u32[]{:S(2)}) async-start(bf16[4,1032,256]{2,1,0:T(8,128)(2,1)} %prep.1), calls=%async_computation.2 | async-start | bytes 4227072 | tf_op jit(solution)/shard_map/all_to_all | solution.py:171
  55.1 46.0 %collective-permute-start = (bf16[4096,128]{1,0:T(8,128)(2,1)}, bf16[4096,128]{1,0:T(8,128)(2,1)}, u32[]{:S(2)}, u32[]{:S(2)}) collective-permute-start(bf16[4096,128]{1,0:T(8,128)(2,1)} %bitcast.3.g0), channel_id=1, source_target_pairs={{0,8},{8,0},{1,9},{9,1},{2,10},{10,2},{3,11},{11,3},{4,12},{12,4},... | collective-permute-start | bytes 3145736 | tf_op jit(solution)/shard_map/ppermute | solution.py:198
  57.0 46.5 %collective-permute-start.1 = (bf16[4096,128]{1,0:T(8,128)(2,1)}, bf16[4096,128]{1,0:T(8,128)(2,1)}, u32[]{:S(2)}, u32[]{:S(2)}) collective-permute-start(bf16[4096,128]{1,0:T(8,128)(2,1)} %bitcast.4.u0), channel_id=1, source_target_pairs={{0,8},{8,0},{1,9},{9,1},{2,10},{10,2},{3,11},{11,3},{4,12},{12,4},... | collective-permute-start | bytes 3145736 | tf_op jit(solution)/shard_map/ppermute | solution.py:198
  60.8 31.4 %collective-permute-start.3 = (bf16[128,2048]{1,0:T(8,128)(2,1)S(1)}, bf16[128,2048]{1,0:T(8,128)(2,1)S(1)}, u32[]{:S(2)}, u32[]{:S(2)}) collective-permute-start(bf16[128,2048]{1,0:T(8,128)(2,1)S(1)} %get-tuple-element.17.refs_0_), channel_id=1, source_target_pairs={{0,16},{16,0},{256,272},{272,256},{1,17},{17,1},{257,273},{273,257... | collective-permute-start | bytes 1572872 | tf_op jit(solution)/shard_map/ppermute | solution.py:179
  64.1 29.9 %collective-permute-start.5 = (bf16[128,2048]{1,0:T(8,128)(2,1)S(1)}, bf16[128,2048]{1,0:T(8,128)(2,1)}, u32[]{:S(2)}, u32[]{:S(2)}) collective-permute-start(bf16[128,2048]{1,0:T(8,128)(2,1)S(1)} %get-tuple-element.16), channel_id=1, source_target_pairs={{0,256},{16,272},{256,0},{272,16},{1,257},{17,273},{257,1},{273,17... | collective-permute-start | bytes 1572872 | tf_op jit(solution)/shard_map/ppermute | solution.py:179
  66.6 32.6 %collective-permute-start.7 = (bf16[128,2048]{1,0:T(8,128)(2,1)S(1)}, bf16[128,2048]{1,0:T(8,128)(2,1)}, u32[]{:S(2)}, u32[]{:S(2)}) collective-permute-start(bf16[128,2048]{1,0:T(8,128)(2,1)S(1)} %get-tuple-element.16), channel_id=1, source_target_pairs={{0,272},{16,256},{256,16},{272,0},{1,273},{17,257},{257,17},{273,1... | collective-permute-start | bytes 1572872 | tf_op jit(solution)/shard_map/ppermute | solution.py:179
  92.1 21.4 %collective-permute-start.2 = (bf16[128,2048]{1,0:T(8,128)(2,1)S(1)}, bf16[128,2048]{1,0:T(8,128)(2,1)}, u32[]{:S(2)}, u32[]{:S(2)}) collective-permute-start(bf16[128,2048]{1,0:T(8,128)(2,1)S(1)} %get-tuple-element.17.refs_0_), channel_id=1, source_target_pairs={{0,8},{8,0},{1,9},{9,1},{2,10},{10,2},{3,11},{11,3},{4,12},{12,4},... | collective-permute-start | bytes 1572872 | tf_op jit(solution)/shard_map/ppermute | solution.py:198
  94.1 19.5 %collective-permute-start.4 = (bf16[128,2048]{1,0:T(8,128)(2,1)S(1)}, bf16[128,2048]{1,0:T(8,128)(2,1)}, u32[]{:S(2)}, u32[]{:S(2)}) collective-permute-start(bf16[128,2048]{1,0:T(8,128)(2,1)S(1)} %collective-permute-done.3.refs_2_), channel_id=1, source_target_pairs={{0,8},{8,0},{1,9},{9,1},{2,10},{10,2},{3,11},{11,3},{4,12},{12,4},... | collective-permute-start | bytes 1572872 | tf_op jit(solution)/shard_map/ppermute | solution.py:198
  99.2 14.3 %collective-permute-start.6 = (bf16[128,2048]{1,0:T(8,128)(2,1)}, bf16[128,2048]{1,0:T(8,128)(2,1)}, u32[]{:S(2)}, u32[]{:S(2)}) collective-permute-start(bf16[128,2048]{1,0:T(8,128)(2,1)} %collective-permute-done.5.refs_4_), channel_id=1, source_target_pairs={{0,8},{8,0},{1,9},{9,1},{2,10},{10,2},{3,11},{11,3},{4,12},{12,4},... | collective-permute-start | bytes 1572872 | tf_op jit(solution)/shard_map/ppermute | solution.py:198
  101.1 12.4 %collective-permute-start.8 = (bf16[128,2048]{1,0:T(8,128)(2,1)}, bf16[128,2048]{1,0:T(8,128)(2,1)}, u32[]{:S(2)}, u32[]{:S(2)}) collective-permute-start(bf16[128,2048]{1,0:T(8,128)(2,1)} %collective-permute-done.7.refs_6_), channel_id=1, source_target_pairs={{0,8},{8,0},{1,9},{9,1},{2,10},{10,2},{3,11},{11,3},{4,12},{12,4},... | collective-permute-start | bytes 1572872 | tf_op jit(solution)/shard_map/ppermute | solution.py:198
  108.6 9.9 %all-to-all-start.3 = ((bf16[4,128,256]{2,1,0:T(8,128)(2,1)}), bf16[4,128,256]{2,1,0:T(8,128)(2,1)S(1)}, u32[]{:S(2)}, u32[]{:S(2)}) async-start(bf16[4,128,256]{2,1,0:T(8,128)(2,1)} %gate_up.1), calls=%async_computation.3 | async-start | bytes 524288 | tf_op jit(solution)/shard_map/all_to_all | solution.py:171
  113.5 12.3 %copy-start = (s32[8,2]{0,1:T(2,128)S(1)}, s32[8,2]{0,1:T(2,128)}, u32[]{:S(2)}) copy-start(s32[8,2]{0,1:T(2,128)} %param.10) | copy-start | bytes 196
  122.3 26.3 %copy-start.1 = (f32[32,2]{0,1:T(2,128)S(1)}, f32[32,2]{0,1:T(2,128)}, u32[]{:S(2)}) copy-start(f32[32,2]{0,1:T(2,128)} %param.9) | copy-start | bytes 772
  122.3 21.2 %all-to-all-start.4 = ((bf16[8,128,256]{2,1,0:T(8,128)(2,1)}), bf16[8,128,256]{2,1,0:T(8,128)(2,1)S(1)}, u32[]{:S(2)}, u32[]{:S(2)}) async-start(bf16[8,128,256]{2,1,0:T(8,128)(2,1)} %down.1), calls=%async_computation.4 | async-start | bytes 1048576 | tf_op jit(solution)/shard_map/all_to_all | solution.py:171
  144.8 14.0 %all-to-all-start.5 = ((bf16[8,32,256]{2,1,0:T(8,128)(2,1)}), bf16[8,32,256]{2,1,0:T(8,128)(2,1)S(1)}, u32[]{:S(2)}, u32[]{:S(2)}) async-start(bf16[8,32,256]{2,1,0:T(8,128)(2,1)} %gather_fusion.1), calls=%async_computation.5 | async-start | bytes 262144 | tf_op jit(solution)/shard_map/all_to_all | solution.py:171

commit v3 on v2

--- a/solution.py
+++ b/solution.py
@@ -118,11 +118,15 @@
 
 VM = pl.BlockSpec(memory_space=pltpu.VMEM)
 SM = pl.BlockSpec(memory_space=pltpu.SMEM)
-ANY = pl.BlockSpec(memory_space=pl.ANY)
+HBM = pl.BlockSpec(memory_space=pltpu.HBM)
 
 
 def vm(x):
     return pltpu.with_memory_space_constraint(x, pltpu.VMEM)
+
+
+def hbm(x):
+    return pltpu.with_memory_space_constraint(x, pltpu.HBM)
 
 
 def prepared(x):
@@ -132,7 +136,7 @@
         prep_kernel,
         out_shape=pltpu.HBM((4, tall, w), BF16),
         in_specs=[VM],
-        out_specs=ANY,
+        out_specs=HBM,
         scratch_shapes=[pltpu.VMEM((tall, w), BF16), pltpu.SemaphoreType.DMA((4,))],
         compiler_params=pltpu.CompilerParams(vmem_limit_bytes=4 << 20),
         name="prep",
@@ -145,12 +149,12 @@
     return pl.pallas_call(
         gate_up_kernel,
         out_shape=jax.ShapeDtypeStruct((4, (tall - 8) // HID, 2 * ff), BF16),
-        in_specs=[VM] + [ANY] * 4,
+        in_specs=[VM] + [HBM] * 4,
         out_specs=VM,
         scratch_shapes=[pltpu.VMEM((2, deep, 2 * ff), BF16), pltpu.SemaphoreType.DMA((8,))],
         compiler_params=pltpu.CompilerParams(vmem_limit_bytes=16 << 20),
         name="gate_up",
-    )(vm(x), *weights)
+    )(vm(x), *[hbm(v) for v in weights])
 
 
 def lowered(where, act, downs):
@@ -159,12 +163,12 @@
     return pl.pallas_call(
         down_kernel,
         out_shape=jax.ShapeDtypeStruct((HID, rows, wide // HID), BF16),
-        in_specs=[SM, VM] + [ANY] * 8,
+        in_specs=[SM, VM] + [HBM] * 8,
         out_specs=VM,
         scratch_shapes=[pltpu.VMEM((8 * ff, wide), BF16), pltpu.SemaphoreType.DMA((16,))],
         compiler_params=pltpu.CompilerParams(vmem_limit_bytes=16 << 20),
         name="down",
-    )(where, vm(act), *downs)
+    )(where, vm(act), *[hbm(v) for v in downs])
 
 
 def exchange(x, axes):
@@ -216,7 +220,8 @@
     picked = jnp.take(blocks, block_of_slot, axis=0, mode="clip").reshape(tall, w)
     picked = jnp.concatenate([picked, jnp.broadcast_to(norm_gain[None, :], (8, w))], axis=0)
     wide = exchange(jnp.broadcast_to(picked[None], (n_hid, tall + 8, w)), "hid")
-    every = exchange(prepared(wide), SQUARE)
+    ready = prepared(wide)
+    every = exchange(ready, SQUARE)
     act = exchange(gated(every, (gate0, up0, gate1, up1)), SQUARE)
     summed = added(exchange(lowered(where, act, downs), "hid")).reshape(MOST, rows, w)
     outgoing = jnp.take(summed, slot_of_block, axis=0, mode="clip")

time: 161 us -> 161 us (level)
  no operation moved by 1% of the time
where the time goes in v3:
time: 161 us; the launch traced here: 160 us
  waiting for transfers between devices  66.7 us (41%)
  starting transfers between devices  47.9 us (30%)
  blocking collectives  27 us (17%)
  Pallas kernels  10.8 us (7%)
  local copies, waits for them, and re-layouts  5.31 us (3%)
  other arithmetic  1.97 us (1%)
    all_to_all x5, waiting for transfers between devices, exchange(): return lax.all_to_all(x, axes, split_axis=0, concat_axis=0, tiled=True)  41.9 us
    all_to_all x1, blocking collectives, exchange(): return lax.all_to_all(x, axes, split_axis=0, concat_axis=0, tiled=True)  27 us
    all_to_all x5, starting transfers between devices, exchange(): return lax.all_to_all(x, axes, split_axis=0, concat_axis=0, tiled=True)  25.7 us
    ppermute x3, waiting for transfers between devices, shifted(): return lax.ppermute(x, SQUARE, [(i, i ^ flip) for i in range(4)])  24.8 us
    ppermute x6, starting transfers between devices, swapped(): return lax.ppermute(x, 'core', [(0, 1), (1, 0)])  13 us
    ppermute x3, starting transfers between devices, shifted(): return lax.ppermute(x, SQUARE, [(i, i ^ flip) for i in range(4)])  9.22 us
    pallas_call x1, Pallas kernels, gated(): pl.pallas_call(gate_up_kernel, out_shape=jax.ShapeDtypeStruct((4, (tall -...  5.08 us
    pallas_call x1, Pallas kernels, lowered(): pl.pallas_call(down_kernel, out_shape=jax.ShapeDtypeStruct((HID, rows, wi...  4.05 us
  transfers between devices with their start and end apart: 14, of which 6 were waited for; matrix products, arithmetic and copies ran while one was open for 2% of the time, Pallas kernels for 3%

profile of v3, /device:TPU:8, one launch (start us, length us, event | category | flops | bytes accessed | tf_op | source)
XLA Modules:
  0.0 159.9 jit_solution(3541544164730072134)
XLA Ops:
  1.4 8.7 %all-to-all-start = ((bf16[8,32,256]{2,1,0:T(8,128)(2,1)}), bf16[8,32,256]{2,1,0:T(8,128)(2,1)S(1)}, u32[]{:S(2)}, u32[]{:S(2)}) async-start(bf16[8,32,256]{2,1,0:T(8,128)(2,1)} %broadcast_in_dim.48), calls=%async_computation | async-start | bytes 262144 | tf_op jit(solution)/shard_map/all_to_all | solution.py:175
  11.1 9.2 %all-to-all-done = bf16[8,32,256]{2,1,0:T(8,128)(2,1)S(1)} async-done(((bf16[8,32,256]{2,1,0:T(8,128)(2,1)}), bf16[8,32,256]{2,1,0:T(8,128)(2,1)S(1)}, u32[]{:S(2)}, u32[]{:S(2)}) %all-to-all-start) | async-done | bytes 131104 | tf_op jit(solution)/shard_map/all_to_all | solution.py:175
  21.6 27.0 %all_to_all.30.x_ref = bf16[8,136,256]{2,1,0:T(8,128)(2,1)S(1)} all-to-all(bf16[8,136,256]{2,1,0:T(8,128)(2,1)S(1)} %broadcast_in_dim.74), channel_id=1, replica_groups=mesh['sec'=2,'group'=8,'xlo'=2,'core'=2,'hid'=8] {'hid'}, dimensions={0} | all-to-all | bytes 1114112 | tf_op jit(solution)/shard_map/all_to_all | solution.py:175
  48.6 1.6 %prep.1 = bf16[4,1032,256]{2,1,0:T(8,128)(2,1)} custom-call(bf16[8,136,256]{2,1,0:T(8,128)(2,1)S(1)} %all_to_all.30.x_ref), custom_call_target="tpu_custom_call" | custom-call | tf_op jit(solution)/shard_map/prep/pallas_call | solution.py:135
  50.2 4.9 %all-to-all-start.2 = ((bf16[4,1032,256]{2,1,0:T(8,128)(2,1)}), bf16[4,1032,256]{2,1,0:T(8,128)(2,1)S(1)}, u32[]{:S(2)}, u32[]{:S(2)}) async-start(bf16[4,1032,256]{2,1,0:T(8,128)(2,1)} %prep.1), calls=%async_computation.2 | async-start | bytes 4227072 | tf_op jit(solution)/shard_map/all_to_all | solution.py:175
  55.1 1.9 %collective-permute-start = (bf16[4096,128]{1,0:T(8,128)(2,1)}, bf16[4096,128]{1,0:T(8,128)(2,1)}, u32[]{:S(2)}, u32[]{:S(2)}) collective-permute-start(bf16[4096,128]{1,0:T(8,128)(2,1)} %bitcast.3.g0), channel_id=1, source_target_pairs={{0,8},{8,0},{1,9},{9,1},{2,10},{10,2},{3,11},{11,3},{4,12},{12,4},... | collective-permute-start | bytes 3145736 | tf_op jit(solution)/shard_map/ppermute | solution.py:202
  57.0 2.4 %collective-permute-start.1 = (bf16[4096,128]{1,0:T(8,128)(2,1)}, bf16[4096,128]{1,0:T(8,128)(2,1)}, u32[]{:S(2)}, u32[]{:S(2)}) collective-permute-start(bf16[4096,128]{1,0:T(8,128)(2,1)} %bitcast.4.u0), channel_id=1, source_target_pairs={{0,8},{8,0},{1,9},{9,1},{2,10},{10,2},{3,11},{11,3},{4,12},{12,4},... | collective-permute-start | bytes 3145736 | tf_op jit(solution)/shard_map/ppermute | solution.py:202
  60.8 3.4 %collective-permute-start.3 = (bf16[128,2048]{1,0:T(8,128)(2,1)S(1)}, bf16[128,2048]{1,0:T(8,128)(2,1)S(1)}, u32[]{:S(2)}, u32[]{:S(2)}) collective-permute-start(bf16[128,2048]{1,0:T(8,128)(2,1)S(1)} %get-tuple-element.17.refs_0_), channel_id=1, source_target_pairs={{0,16},{16,0},{256,272},{272,256},{1,17},{17,1},{257,273},{273,257... | collective-permute-start | bytes 1572872 | tf_op jit(solution)/shard_map/ppermute | solution.py:183
  64.2 2.5 %collective-permute-start.5 = (bf16[128,2048]{1,0:T(8,128)(2,1)S(1)}, bf16[128,2048]{1,0:T(8,128)(2,1)}, u32[]{:S(2)}, u32[]{:S(2)}) collective-permute-start(bf16[128,2048]{1,0:T(8,128)(2,1)S(1)} %get-tuple-element.16), channel_id=1, source_target_pairs={{0,256},{16,272},{256,0},{272,16},{1,257},{17,273},{257,1},{273,17... | collective-permute-start | bytes 1572872 | tf_op jit(solution)/shard_map/ppermute | solution.py:183
  66.6 3.4 %collective-permute-start.7 = (bf16[128,2048]{1,0:T(8,128)(2,1)S(1)}, bf16[128,2048]{1,0:T(8,128)(2,1)}, u32[]{:S(2)}, u32[]{:S(2)}) collective-permute-start(bf16[128,2048]{1,0:T(8,128)(2,1)S(1)} %get-tuple-element.16), channel_id=1, source_target_pairs={{0,272},{16,256},{256,16},{272,0},{1,273},{17,257},{257,17},{273,1... | collective-permute-start | bytes 1572872 | tf_op jit(solution)/shard_map/ppermute | solution.py:183
  70.0 22.1 %collective-permute-done.3.refs_2_ = bf16[128,2048]{1,0:T(8,128)(2,1)S(1)} collective-permute-done((bf16[128,2048]{1,0:T(8,128)(2,1)S(1)}, bf16[128,2048]{1,0:T(8,128)(2,1)S(1)}, u32[]{:S(2)}, u32[]{:S(2)}) %collective-permute-start.3) | collective-permute-done | bytes 524320 | tf_op jit(solution)/shard_map/ppermute | solution.py:183
  92.1 1.9 %collective-permute-start.2 = (bf16[128,2048]{1,0:T(8,128)(2,1)S(1)}, bf16[128,2048]{1,0:T(8,128)(2,1)}, u32[]{:S(2)}, u32[]{:S(2)}) collective-permute-start(bf16[128,2048]{1,0:T(8,128)(2,1)S(1)} %get-tuple-element.17.refs_0_), channel_id=1, source_target_pairs={{0,8},{8,0},{1,9},{9,1},{2,10},{10,2},{3,11},{11,3},{4,12},{12,4},... | collective-permute-start | bytes 1572872 | tf_op jit(solution)/shard_map/ppermute | solution.py:202
  94.1 2.4 %collective-permute-start.4 = (bf16[128,2048]{1,0:T(8,128)(2,1)S(1)}, bf16[128,2048]{1,0:T(8,128)(2,1)}, u32[]{:S(2)}, u32[]{:S(2)}) collective-permute-start(bf16[128,2048]{1,0:T(8,128)(2,1)S(1)} %collective-permute-done.3.refs_2_), channel_id=1, source_target_pairs={{0,8},{8,0},{1,9},{9,1},{2,10},{10,2},{3,11},{11,3},{4,12},{12,4},... | collective-permute-start | bytes 1572872 | tf_op jit(solution)/shard_map/ppermute | solution.py:202
  96.5 2.7 %collective-permute-done.7.refs_6_ = bf16[128,2048]{1,0:T(8,128)(2,1)} collective-permute-done((bf16[128,2048]{1,0:T(8,128)(2,1)S(1)}, bf16[128,2048]{1,0:T(8,128)(2,1)}, u32[]{:S(2)}, u32[]{:S(2)}) %collective-permute-start.7) | collective-permute-done | bytes 524320 | tf_op jit(solution)/shard_map/ppermute | solution.py:183
  99.2 1.9 %collective-permute-start.6 = (bf16[128,2048]{1,0:T(8,128)(2,1)}, bf16[128,2048]{1,0:T(8,128)(2,1)}, u32[]{:S(2)}, u32[]{:S(2)}) collective-permute-start(bf16[128,2048]{1,0:T(8,128)(2,1)} %collective-permute-done.5.refs_4_), channel_id=1, source_target_pairs={{0,8},{8,0},{1,9},{9,1},{2,10},{10,2},{3,11},{11,3},{4,12},{12,4},... | collective-permute-start | bytes 1572872 | tf_op jit(solution)/shard_map/ppermute | solution.py:202
  101.1 2.4 %collective-permute-start.8 = (bf16[128,2048]{1,0:T(8,128)(2,1)}, bf16[128,2048]{1,0:T(8,128)(2,1)}, u32[]{:S(2)}, u32[]{:S(2)}) collective-permute-start(bf16[128,2048]{1,0:T(8,128)(2,1)} %collective-permute-done.7.refs_6_), channel_id=1, source_target_pairs={{0,8},{8,0},{1,9},{9,1},{2,10},{10,2},{3,11},{11,3},{4,12},{12,4},... | collective-permute-start | bytes 1572872 | tf_op jit(solution)/shard_map/ppermute | solution.py:202
  103.6 5.1 %gate_up.1 = bf16[4,128,256]{2,1,0:T(8,128)(2,1)} custom-call(bf16[4,1032,256]{2,1,0:T(8,128)(2,1)S(1)} %all-to-all-done.2.x_ref, bf16[4096,128]{1,0:T(8,128)(2,1)} %bitcast.3.g0, bf16[4096,128]{1,0:T(8,128)(2,1)} %bitcast.4.u0, bf16[4096,128]{1,0:T(8,128)(2,1)} %collective-permute-done.g1, bf16[4096,128]{1,0:T(8,128)(2,1)} %collective-permute-done.1.u1), custom_call_target="tpu_custom_call" | custom-call | tf_op jit(solution)/shard_map/gate_up/pallas_call | solution.py:149
  108.7 4.9 %all-to-all-start.3 = ((bf16[4,128,256]{2,1,0:T(8,128)(2,1)}), bf16[4,128,256]{2,1,0:T(8,128)(2,1)S(1)}, u32[]{:S(2)}, u32[]{:S(2)}) async-start(bf16[4,128,256]{2,1,0:T(8,128)(2,1)} %gate_up.1), calls=%async_computation.3 | async-start | bytes 524288 | tf_op jit(solution)/shard_map/all_to_all | solution.py:175
  113.6 5.0 %all-to-all-done.3.act_ref = bf16[4,128,256]{2,1,0:T(8,128)(2,1)S(1)} async-done(((bf16[4,128,256]{2,1,0:T(8,128)(2,1)}), bf16[4,128,256]{2,1,0:T(8,128)(2,1)S(1)}, u32[]{:S(2)}, u32[]{:S(2)}) %all-to-all-start.3) | async-done | bytes 262176 | tf_op jit(solution)/shard_map/all_to_all | solution.py:175
  118.6 4.1 %down.1 = bf16[8,128,256]{2,1,0:T(8,128)(2,1)} custom-call(s32[4]{0:T(128)S(1)} %iota_xor_fusion.where_ref, bf16[4,128,256]{2,1,0:T(8,128)(2,1)S(1)} %all-to-all-done.3.act_ref, bf16[128,2048]{1,0:T(8,128)(2,1)} %copy-done, bf16[128,2048]{1,0:T(8,128)(2,1)} %collective-permute-done.2.refs_1_, bf16[128,2048]{1,0:T(8,128)(2,1)} %copy-done.1, ...), custom_call_target="tpu_custom_call" | custom-call | tf_op jit(solution)/shard_map/down/pallas_call | solution.py:163
  122.7 3.5 %all-to-all-start.4 = ((bf16[8,128,256]{2,1,0:T(8,128)(2,1)}), bf16[8,128,256]{2,1,0:T(8,128)(2,1)S(1)}, u32[]{:S(2)}, u32[]{:S(2)}) async-start(bf16[8,128,256]{2,1,0:T(8,128)(2,1)} %down.1), calls=%async_computation.4 | async-start | bytes 1048576 | tf_op jit(solution)/shard_map/all_to_all | solution.py:175
  126.4 17.5 %all-to-all-done.4 = bf16[8,128,256]{2,1,0:T(8,128)(2,1)S(1)} async-done(((bf16[8,128,256]{2,1,0:T(8,128)(2,1)}), bf16[8,128,256]{2,1,0:T(8,128)(2,1)S(1)}, u32[]{:S(2)}, u32[]{:S(2)}) %all-to-all-start.4) | async-done | bytes 524320 | tf_op jit(solution)/shard_map/all_to_all | solution.py:175
  145.1 3.8 %all-to-all-start.5 = ((bf16[8,32,256]{2,1,0:T(8,128)(2,1)}), bf16[8,32,256]{2,1,0:T(8,128)(2,1)S(1)}, u32[]{:S(2)}, u32[]{:S(2)}) async-start(bf16[8,32,256]{2,1,0:T(8,128)(2,1)} %gather_fusion.1), calls=%async_computation.5 | async-start | bytes 262144 | tf_op jit(solution)/shard_map/all_to_all | solution.py:175
  149.1 10.1 %all-to-all-done.5 = bf16[8,32,256]{2,1,0:T(8,128)(2,1)S(1)} async-done(((bf16[8,32,256]{2,1,0:T(8,128)(2,1)}), bf16[8,32,256]{2,1,0:T(8,128)(2,1)S(1)}, u32[]{:S(2)}, u32[]{:S(2)}) %all-to-all-start.5) | async-done | bytes 131104 | tf_op jit(solution)/shard_map/all_to_all | solution.py:175
  (36 shorter events, 7.3 us)
Async XLA Ops:
  1.4 18.9 %all-to-all-start = ((bf16[8,32,256]{2,1,0:T(8,128)(2,1)}), bf16[8,32,256]{2,1,0:T(8,128)(2,1)S(1)}, u32[]{:S(2)}, u32[]{:S(2)}) async-start(bf16[8,32,256]{2,1,0:T(8,128)(2,1)} %broadcast_in_dim.48), calls=%async_computation | async-start | bytes 262144 | tf_op jit(solution)/shard_map/all_to_all | solution.py:175
  50.2 53.3 %all-to-all-start.2 = ((bf16[4,1032,256]{2,1,0:T(8,128)(2,1)}), bf16[4,1032,256]{2,1,0:T(8,128)(2,1)S(1)}, u32[]{:S(2)}, u32[]{:S(2)}) async-start(bf16[4,1032,256]{2,1,0:T(8,128)(2,1)} %prep.1), calls=%async_computation.2 | async-start | bytes 4227072 | tf_op jit(solution)/shard_map/all_to_all | solution.py:175
  55.1 46.0 %collective-permute-start = (bf16[4096,128]{1,0:T(8,128)(2,1)}, bf16[4096,128]{1,0:T(8,128)(2,1)}, u32[]{:S(2)}, u32[]{:S(2)}) collective-permute-start(bf16[4096,128]{1,0:T(8,128)(2,1)} %bitcast.3.g0), channel_id=1, source_target_pairs={{0,8},{8,0},{1,9},{9,1},{2,10},{10,2},{3,11},{11,3},{4,12},{12,4},... | collective-permute-start | bytes 3145736 | tf_op jit(solution)/shard_map/ppermute | solution.py:202
  57.0 46.5 %collective-permute-start.1 = (bf16[4096,128]{1,0:T(8,128)(2,1)}, bf16[4096,128]{1,0:T(8,128)(2,1)}, u32[]{:S(2)}, u32[]{:S(2)}) collective-permute-start(bf16[4096,128]{1,0:T(8,128)(2,1)} %bitcast.4.u0), channel_id=1, source_target_pairs={{0,8},{8,0},{1,9},{9,1},{2,10},{10,2},{3,11},{11,3},{4,12},{12,4},... | collective-permute-start | bytes 3145736 | tf_op jit(solution)/shard_map/ppermute | solution.py:202
  60.8 47.9 %copy-start = (bf16[128,2048]{1,0:T(8,128)(2,1)}, bf16[128,2048]{1,0:T(8,128)(2,1)S(1)}, u32[]{:S(2)}) copy-start(bf16[128,2048]{1,0:T(8,128)(2,1)S(1)} %get-tuple-element.17.refs_0_) | copy-start | bytes 1572868
  60.8 31.4 %collective-permute-start.3 = (bf16[128,2048]{1,0:T(8,128)(2,1)S(1)}, bf16[128,2048]{1,0:T(8,128)(2,1)S(1)}, u32[]{:S(2)}, u32[]{:S(2)}) collective-permute-start(bf16[128,2048]{1,0:T(8,128)(2,1)S(1)} %get-tuple-element.17.refs_0_), channel_id=1, source_target_pairs={{0,16},{16,0},{256,272},{272,256},{1,17},{17,1},{257,273},{273,257... | collective-permute-start | bytes 1572872 | tf_op jit(solution)/shard_map/ppermute | solution.py:183
  64.2 29.9 %collective-permute-start.5 = (bf16[128,2048]{1,0:T(8,128)(2,1)S(1)}, bf16[128,2048]{1,0:T(8,128)(2,1)}, u32[]{:S(2)}, u32[]{:S(2)}) collective-permute-start(bf16[128,2048]{1,0:T(8,128)(2,1)S(1)} %get-tuple-element.16), channel_id=1, source_target_pairs={{0,256},{16,272},{256,0},{272,16},{1,257},{17,273},{257,1},{273,17... | collective-permute-start | bytes 1572872 | tf_op jit(solution)/shard_map/ppermute | solution.py:183
  66.6 32.6 %collective-permute-start.7 = (bf16[128,2048]{1,0:T(8,128)(2,1)S(1)}, bf16[128,2048]{1,0:T(8,128)(2,1)}, u32[]{:S(2)}, u32[]{:S(2)}) collective-permute-start(bf16[128,2048]{1,0:T(8,128)(2,1)S(1)} %get-tuple-element.16), channel_id=1, source_target_pairs={{0,272},{16,256},{256,16},{272,0},{1,273},{17,257},{257,17},{273,1... | collective-permute-start | bytes 1572872 | tf_op jit(solution)/shard_map/ppermute | solution.py:183
  92.1 16.5 %copy-start.1 = (bf16[128,2048]{1,0:T(8,128)(2,1)}, bf16[128,2048]{1,0:T(8,128)(2,1)S(1)}, u32[]{:S(2)}) copy-start(bf16[128,2048]{1,0:T(8,128)(2,1)S(1)} %collective-permute-done.3.refs_2_) | copy-start | bytes 1572868
  92.1 21.4 %collective-permute-start.2 = (bf16[128,2048]{1,0:T(8,128)(2,1)S(1)}, bf16[128,2048]{1,0:T(8,128)(2,1)}, u32[]{:S(2)}, u32[]{:S(2)}) collective-permute-start(bf16[128,2048]{1,0:T(8,128)(2,1)S(1)} %get-tuple-element.17.refs_0_), channel_id=1, source_target_pairs={{0,8},{8,0},{1,9},{9,1},{2,10},{10,2},{3,11},{11,3},{4,12},{12,4},... | collective-permute-start | bytes 1572872 | tf_op jit(solution)/shard_map/ppermute | solution.py:202
  94.1 19.5 %collective-permute-start.4 = (bf16[128,2048]{1,0:T(8,128)(2,1)S(1)}, bf16[128,2048]{1,0:T(8,128)(2,1)}, u32[]{:S(2)}, u32[]{:S(2)}) collective-permute-start(bf16[128,2048]{1,0:T(8,128)(2,1)S(1)} %collective-permute-done.3.refs_2_), channel_id=1, source_target_pairs={{0,8},{8,0},{1,9},{9,1},{2,10},{10,2},{3,11},{11,3},{4,12},{12,4},... | collective-permute-start | bytes 1572872 | tf_op jit(solution)/shard_map/ppermute | solution.py:202
  99.2 14.4 %collective-permute-start.6 = (bf16[128,2048]{1,0:T(8,128)(2,1)}, bf16[128,2048]{1,0:T(8,128)(2,1)}, u32[]{:S(2)}, u32[]{:S(2)}) collective-permute-start(bf16[128,2048]{1,0:T(8,128)(2,1)} %collective-permute-done.5.refs_4_), channel_id=1, source_target_pairs={{0,8},{8,0},{1,9},{9,1},{2,10},{10,2},{3,11},{11,3},{4,12},{12,4},... | collective-permute-start | bytes 1572872 | tf_op jit(solution)/shard_map/ppermute | solution.py:202
  101.1 12.4 %collective-permute-start.8 = (bf16[128,2048]{1,0:T(8,128)(2,1)}, bf16[128,2048]{1,0:T(8,128)(2,1)}, u32[]{:S(2)}, u32[]{:S(2)}) collective-permute-start(bf16[128,2048]{1,0:T(8,128)(2,1)} %collective-permute-done.7.refs_6_), channel_id=1, source_target_pairs={{0,8},{8,0},{1,9},{9,1},{2,10},{10,2},{3,11},{11,3},{4,12},{12,4},... | collective-permute-start | bytes 1572872 | tf_op jit(solution)/shard_map/ppermute | solution.py:202
  108.7 9.9 %all-to-all-start.3 = ((bf16[4,128,256]{2,1,0:T(8,128)(2,1)}), bf16[4,128,256]{2,1,0:T(8,128)(2,1)S(1)}, u32[]{:S(2)}, u32[]{:S(2)}) async-start(bf16[4,128,256]{2,1,0:T(8,128)(2,1)} %gate_up.1), calls=%async_computation.3 | async-start | bytes 524288 | tf_op jit(solution)/shard_map/all_to_all | solution.py:175
  113.5 12.6 %copy-start.2 = (s32[8,2]{0,1:T(2,128)S(1)}, s32[8,2]{0,1:T(2,128)}, u32[]{:S(2)}) copy-start(s32[8,2]{0,1:T(2,128)} %param.10) | copy-start | bytes 196
  122.6 26.3 %copy-start.3 = (f32[32,2]{0,1:T(2,128)S(1)}, f32[32,2]{0,1:T(2,128)}, u32[]{:S(2)}) copy-start(f32[32,2]{0,1:T(2,128)} %param.9) | copy-start | bytes 772
  122.7 21.2 %all-to-all-start.4 = ((bf16[8,128,256]{2,1,0:T(8,128)(2,1)}), bf16[8,128,256]{2,1,0:T(8,128)(2,1)S(1)}, u32[]{:S(2)}, u32[]{:S(2)}) async-start(bf16[8,128,256]{2,1,0:T(8,128)(2,1)} %down.1), calls=%async_computation.4 | async-start | bytes 1048576 | tf_op jit(solution)/shard_map/all_to_all | solution.py:175
  145.1 14.0 %all-to-all-start.5 = ((bf16[8,32,256]{2,1,0:T(8,128)(2,1)}), bf16[8,32,256]{2,1,0:T(8,128)(2,1)S(1)}, u32[]{:S(2)}, u32[]{:S(2)}) async-start(bf16[8,32,256]{2,1,0:T(8,128)(2,1)} %gather_fusion.1), calls=%async_computation.5 | async-start | bytes 262144 | tf_op jit(solution)/shard_map/all_to_all | solution.py:175

commit v4 on v3

--- a/solution.py
+++ b/solution.py
@@ -41,79 +41,126 @@
         send.wait()
 
 
-def gate_up_kernel(x_ref, g0, u0, g1, u1, act_ref, w_ref, sems):
+def gate_up_kernel(x_ref, g0, u0, g1, u1, act_ref, w_ref, acc_ref, sems):
     _, tall, w = x_ref.shape
     n = HID
     rows = (tall - 8) // n
-    depth = n * w
-    ff = g0.shape[1]
-    loads = []
-    for s in range(2):
-        for c, pair in enumerate(((g0, u0), (g1, u1))):
-            for k, ref in enumerate(pair):
-                loads.append(
-                    pltpu.make_async_copy(
-                        ref.at[s * depth : (s + 1) * depth, :],
-                        w_ref.at[c, s * depth : (s + 1) * depth, k * ff : (k + 1) * ff],
-                        sems.at[len(loads)],
-                    )
-                )
-    for load in loads:
-        load.start()
+    deep, ff = g0.shape
+    chunks = 4
+    per = deep // chunks
+    loads = [
+        [
+            pltpu.make_async_copy(
+                ref.at[c * per : (c + 1) * per, :], w_ref.at[i, c * per : (c + 1) * per, :], sems.at[c, i]
+            )
+            for i, ref in enumerate((g0, u0, g1, u1))
+        ]
+        for c in range(chunks)
+    ]
+    for c in range(2):
+        for load in loads[c]:
+            load.start()
     scales = []
     for x in range(2):
         parts = [x_ref[2 * s + x, n * rows : n * rows + 8, 0:rows].astype(F32) for s in range(2)]
         both = parts[0] + parts[1]
         total = both[0:1, :] + both[1:2, :] + both[2:3, :]
-        inv = 1.0 / jnp.sqrt(total / (2 * depth) + 1e-05)
+        inv = 1.0 / jnp.sqrt(total / deep + 1e-05)
         scales.append(jnp.transpose(jnp.broadcast_to(inv, (rows, rows))))
-    scale = jnp.concatenate(scales, axis=0)
-    accs = [None, None]
-    for s in range(2):
+    for c in range(chunks):
+        pieces = range(c * per // w, (c + 1) * per // w)
         xs = jnp.concatenate(
             [
-                jnp.concatenate([x_ref[2 * s + x, z * rows : (z + 1) * rows, :] for z in range(n)], axis=1)
+                jnp.concatenate(
+                    [x_ref[2 * (p // n) + x, (p % n) * rows : (p % n + 1) * rows, :] for p in pieces], axis=1
+                )
                 for x in range(2)
             ],
             axis=0,
         )
-        for c in range(2):
-            loads[4 * s + 2 * c].wait()
-            loads[4 * s + 2 * c + 1].wait()
-            part = jnp.dot(xs, w_ref[c, s * depth : (s + 1) * depth, :], preferred_element_type=F32)
-            accs[c] = part if accs[c] is None else accs[c] + part
-    for c, acc in enumerate(accs):
-        gate = acc[:, 0:ff] * scale
-        up = acc[:, ff:] * scale
-        act = (gate / (1.0 + jnp.exp(-gate)) * up).astype(BF16)
-        for s in range(2):
-            for x in range(2):
-                act_ref[2 * s + x, :, c * ff : (c + 1) * ff] = act[x * rows : (x + 1) * rows]
+        for load in loads[c]:
+            load.wait()
+        if c + 2 < chunks:
+            for load in loads[c + 2]:
+                load.start()
+        ws = jnp.concatenate([w_ref[i, c * per : (c + 1) * per, :] for i in range(4)], axis=1)
+        part = jnp.dot(xs, ws, preferred_element_type=F32)
+        if c == 0:
+            acc_ref[...] = part
+        elif c + 1 < chunks:
+            acc_ref[...] += part
+        else:
+            acc = acc_ref[...] + part
+    for k in range(2):
+        for x in range(2):
+            block = acc[x * rows : (x + 1) * rows, 2 * k * ff : 2 * (k + 1) * ff]
+            gate = block[:, 0:ff] * scales[x]
+            up = block[:, ff:] * scales[x]
+            act = (gate / (1.0 + jnp.exp(-gate)) * up).astype(BF16)
+            for s in range(2):
+                act_ref[2 * s + x, :, k * ff : (k + 1) * ff] = act
 
 
 def down_kernel(where_ref, act_ref, *refs):
     *downs, out_ref, w_ref, sems = refs
     n, _, w = out_ref.shape
     ff = downs[0].shape[0]
-    half = n * w // 2
-    loads = []
+    chunks = 4
+    per = n * w // chunks
+    loads = [
+        [
+            pltpu.make_async_copy(
+                ref.at[:, h * per : (h + 1) * per],
+                w_ref.at[i * ff : (i + 1) * ff, h * per : (h + 1) * per],
+                sems.at[h, i],
+            )
+            for i, ref in enumerate(downs)
+        ]
+        for h in range(chunks)
+    ]
     for h in range(2):
-        for i, ref in enumerate(downs):
-            loads.append(
-                pltpu.make_async_copy(
-                    ref.at[:, h * half : (h + 1) * half],
-                    w_ref.at[i * ff : (i + 1) * ff, h * half : (h + 1) * half],
-                    sems.at[len(loads)],
-                )
-            )
-    for load in loads:
-        load.start()
+        for load in loads[h]:
+            load.start()
     act = jnp.concatenate([act_ref[where_ref[k]] for k in range(4)], axis=1)
-    for h in range(2):
-        for load in loads[8 * h : 8 * h + 8]:
+    for h in range(chunks):
+        for load in loads[h]:
             load.wait()
-        for z in range(h * n // 2, (h + 1) * n // 2):
+        if h + 2 < chunks:
+            for load in loads[h + 2]:
+                load.start()
+        for z in range(h * n // chunks, (h + 1) * n // chunks):
             out_ref[z] = jnp.dot(act, w_ref[:, z * w : (z + 1) * w], preferred_element_type=F32).astype(BF16)
+
+
+def spread_kernel(x_ref, out_ref, sems):
+    sends = [pltpu.make_async_copy(x_ref, out_ref.at[j], sems.at[j]) for j in range(out_ref.shape[0])]
+    for send in sends:
+        send.start()
+    for send in sends:
+        send.wait()
+
+
+def pick_kernel(block_ref, x_ref, gain_ref, out_ref, y_ref, sems):
+    _, rows, w = x_ref.shape
+    for k in range(MOST):
+        y_ref[k * rows : (k + 1) * rows, :] = x_ref[block_ref[k]]
+    y_ref[MOST * rows : MOST * rows + 8, :] = jnp.broadcast_to(gain_ref[...].astype(F32), (8, w)).astype(BF16)
+    spread_kernel(y_ref, out_ref, sems)
+
+
+def home_kernel(slot_ref, x_ref, out_ref, y_ref, sems):
+    _, rows, _ = out_ref.shape
+    total = x_ref[0].astype(F32)
+    for z in range(1, x_ref.shape[0]):
+        total = total + x_ref[z].astype(F32)
+    total = total.astype(BF16)
+    for k in range(MOST):
+        y_ref[k] = total[k * rows : (k + 1) * rows]
+    sends = [pltpu.make_async_copy(y_ref.at[slot_ref[b]], out_ref.at[b], sems.at[b]) for b in range(out_ref.shape[0])]
+    for send in sends:
+        send.start()
+    for send in sends:
+        send.wait()
 
 
 VM = pl.BlockSpec(memory_space=pltpu.VMEM)
@@ -145,13 +192,18 @@
 
 def gated(x, weights):
     _, tall, _ = x.shape
+    rows = (tall - 8) // HID
     deep, ff = weights[0].shape
     return pl.pallas_call(
         gate_up_kernel,
-        out_shape=jax.ShapeDtypeStruct((4, (tall - 8) // HID, 2 * ff), BF16),
+        out_shape=pltpu.HBM((4, rows, 2 * ff), BF16),
         in_specs=[VM] + [HBM] * 4,
         out_specs=VM,
-        scratch_shapes=[pltpu.VMEM((2, deep, 2 * ff), BF16), pltpu.SemaphoreType.DMA((8,))],
+        scratch_shapes=[
+            pltpu.VMEM((4, deep, ff), BF16),
+            pltpu.VMEM((2 * rows, 4 * ff), F32),
+            pltpu.SemaphoreType.DMA((4, 4)),
+        ],
         compiler_params=pltpu.CompilerParams(vmem_limit_bytes=16 << 20),
         name="gate_up",
     )(vm(x), *[hbm(v) for v in weights])
@@ -165,26 +217,59 @@
         out_shape=jax.ShapeDtypeStruct((HID, rows, wide // HID), BF16),
         in_specs=[SM, VM] + [HBM] * 8,
         out_specs=VM,
-        scratch_shapes=[pltpu.VMEM((8 * ff, wide), BF16), pltpu.SemaphoreType.DMA((16,))],
+        scratch_shapes=[pltpu.VMEM((8 * ff, wide), BF16), pltpu.SemaphoreType.DMA((4, 8))],
         compiler_params=pltpu.CompilerParams(vmem_limit_bytes=16 << 20),
         name="down",
     )(where, vm(act), *[hbm(v) for v in downs])
 
 
+def repeated(x, copies):
+    return pl.pallas_call(
+        spread_kernel,
+        out_shape=pltpu.HBM((copies, *x.shape), x.dtype),
+        in_specs=[HBM],
+        out_specs=HBM,
+        scratch_shapes=[pltpu.SemaphoreType.DMA((copies,))],
+        compiler_params=pltpu.CompilerParams(vmem_limit_bytes=1 << 20),
+    )(hbm(x))
+
+
+def picked_rows(block_of_slot, blocks, norm_gain, copies):
+    _, rows, w = blocks.shape
+    tall = MOST * rows + 8
+    return pl.pallas_call(
+        pick_kernel,
+        out_shape=pltpu.HBM((copies, tall, w), BF16),
+        in_specs=[SM, VM, VM],
+        out_specs=HBM,
+        scratch_shapes=[pltpu.VMEM((tall, w), BF16), pltpu.SemaphoreType.DMA((copies,))],
+        compiler_params=pltpu.CompilerParams(vmem_limit_bytes=1 << 20),
+    )(block_of_slot, vm(blocks), norm_gain[None, :])
+
+
+def homed(slot_of_block, parts):
+    _, tall, w = parts.shape
+    rows = tall // MOST
+    return pl.pallas_call(
+        home_kernel,
+        out_shape=pltpu.HBM((slot_of_block.shape[0], rows, w), BF16),
+        in_specs=[SM, VM],
+        out_specs=HBM,
+        scratch_shapes=[pltpu.VMEM((MOST, rows, w), BF16), pltpu.SemaphoreType.DMA((slot_of_block.shape[0],))],
+        compiler_params=pltpu.CompilerParams(vmem_limit_bytes=2 << 20),
+        name="home",
+    )(slot_of_block, vm(parts))
+
+
 def exchange(x, axes):
     return lax.all_to_all(x, axes, split_axis=0, concat_axis=0, tiled=True)
 
 
-def added(x):
-    return jnp.sum(x.astype(F32), axis=0).astype(BF16)
-
-
 def shifted(x, flip):
     return lax.ppermute(x, SQUARE, [(i, i ^ flip) for i in range(4)])
 
 
 def layer(tokens, norm_gain, route_weight, block_experts, w_gate, w_up, w_down):
-    rows, w = tokens.shape
     groups = lax.axis_size("group")
     n_hid = lax.axis_size("hid")
     me = lax.axis_index("group")
@@ -215,17 +300,14 @@
     named = mine[None, :] == jnp.arange(EXPERTS, dtype=jnp.int32)[:, None]
     factor = jnp.sum(jnp.where(named[:, None, :], route_weight[None], 0.0), axis=2)
 
-    blocks = exchange(jnp.broadcast_to(tokens[None], (groups, rows, w)), GROUP)
-    tall = MOST * rows
-    picked = jnp.take(blocks, block_of_slot, axis=0, mode="clip").reshape(tall, w)
-    picked = jnp.concatenate([picked, jnp.broadcast_to(norm_gain[None, :], (8, w))], axis=0)
-    wide = exchange(jnp.broadcast_to(picked[None], (n_hid, tall + 8, w)), "hid")
+    blocks = exchange(repeated(tokens, groups), GROUP)
+    wide = picked_rows(block_of_slot, blocks, norm_gain, n_hid)
+    wide = exchange(wide, "hid")
     ready = prepared(wide)
     every = exchange(ready, SQUARE)
     act = exchange(gated(every, (gate0, up0, gate1, up1)), SQUARE)
-    summed = added(exchange(lowered(where, act, downs), "hid")).reshape(MOST, rows, w)
-    outgoing = jnp.take(summed, slot_of_block, axis=0, mode="clip")
-    back = exchange(outgoing, GROUP)
+    parts = exchange(lowered(where, act, downs), "hid")
+    back = exchange(homed(slot_of_block, parts), GROUP)
     return jnp.sum(back.astype(F32) * factor[:, :, None], axis=0).astype(BF16)
 
 

time: 161 us -> 165 us (1.025)
  Pallas kernels: 10.8 us -> 18.5 us
  local copies, waits for them, and re-layouts: 5.31 us -> 2.15 us
    pallas_call x1 -> x4, Pallas kernels: 5.08 us -> 12 us  [the longest x1 5.14 us: repeated(): pl.pallas_call(spread_kernel, out_shape=pltpu.HBM((copies, *x.shape), x.d...]
    gather x2 -> x0, local copies, waits for them, and re-layouts: 1.75 us -> none  [the longest x1 1.2 us: layer(): outgoing = jnp.take(summed, slot_of_block, axis=0, mode='clip')]
where the time goes in v4:
time: 165 us; the launch traced here: 164 us
  waiting for transfers between devices  66.1 us (40%)
  starting transfers between devices  47.9 us (29%)
  blocking collectives  27.2 us (16%)
  Pallas kernels  18.5 us (11%)
  local copies, waits for them, and re-layouts  2.15 us (1%)
  other arithmetic  1.87 us (1%)
    all_to_all x5, waiting for transfers between devices, exchange(): return lax.all_to_all(x, axes, split_axis=0, concat_axis=0, tiled=True)  41.2 us
    all_to_all x1, blocking collectives, exchange(): return lax.all_to_all(x, axes, split_axis=0, concat_axis=0, tiled=True)  27.2 us
    all_to_all x5, starting transfers between devices, exchange(): return lax.all_to_all(x, axes, split_axis=0, concat_axis=0, tiled=True)  25.7 us
    ppermute x3, waiting for transfers between devices, shifted(): return lax.ppermute(x, SQUARE, [(i, i ^ flip) for i in range(4)])  24.8 us
    ppermute x6, starting transfers between devices, swapped(): return lax.ppermute(x, 'core', [(0, 1), (1, 0)])  13 us
    ppermute x3, starting transfers between devices, shifted(): return lax.ppermute(x, SQUARE, [(i, i ^ flip) for i in range(4)])  9.22 us
    pallas_call x1, Pallas kernels, repeated(): pl.pallas_call(spread_kernel, out_shape=pltpu.HBM((copies, *x.shape), x.d...  5.14 us
    pallas_call x1, Pallas kernels, lowered(): pl.pallas_call(down_kernel, out_shape=jax.ShapeDtypeStruct((HID, rows, wi...  4.8 us
  transfers between devices with their start and end apart: 14, of which 6 were waited for; matrix products, arithmetic and copies ran while one was open for 2% of the time, Pallas kernels for 3%

profile of v4, /device:TPU:8, one launch (start us, length us, event | category | flops | bytes accessed | tf_op | source)
XLA Modules:
  0.0 164.0 jit_solution(15432884757330590945)
XLA Ops:
  0.0 5.1 %shard_map.73 = bf16[8,32,256]{2,1,0:T(8,128)(2,1)} custom-call(bf16[32,256]{1,0:T(8,128)(2,1)} %x_ref.1), custom_call_target="tpu_custom_call" | custom-call | tf_op jit(solution)/shard_map/pallas_call | solution.py:227
  5.1 8.7 %all-to-all-start = ((bf16[8,32,256]{2,1,0:T(8,128)(2,1)}), bf16[8,32,256]{2,1,0:T(8,128)(2,1)S(1)}, u32[]{:S(2)}, u32[]{:S(2)}) async-start(bf16[8,32,256]{2,1,0:T(8,128)(2,1)} %shard_map.73), calls=%async_computation | async-start | bytes 262144 | tf_op jit(solution)/shard_map/all_to_all | solution.py:265
  15.5 8.6 %all-to-all-done.x_ref = bf16[8,32,256]{2,1,0:T(8,128)(2,1)S(1)} async-done(((bf16[8,32,256]{2,1,0:T(8,128)(2,1)}), bf16[8,32,256]{2,1,0:T(8,128)(2,1)S(1)}, u32[]{:S(2)}, u32[]{:S(2)}) %all-to-all-start) | async-done | bytes 131104 | tf_op jit(solution)/shard_map/all_to_all | solution.py:265
  25.5 27.2 %all_to_all.30.x_ref = bf16[8,136,256]{2,1,0:T(8,128)(2,1)S(1)} all-to-all(bf16[8,136,256]{2,1,0:T(8,128)(2,1)} %shard_map.74), channel_id=1, replica_groups=mesh['sec'=2,'group'=8,'xlo'=2,'core'=2,'hid'=8] {'hid'}, dimensions={0} | all-to-all | bytes 1114112 | tf_op jit(solution)/shard_map/all_to_all | solution.py:265
  54.4 4.9 %all-to-all-start.2 = ((bf16[4,1032,256]{2,1,0:T(8,128)(2,1)}), bf16[4,1032,256]{2,1,0:T(8,128)(2,1)S(1)}, u32[]{:S(2)}, u32[]{:S(2)}) async-start(bf16[4,1032,256]{2,1,0:T(8,128)(2,1)} %prep.1), calls=%async_computation.2 | async-start | bytes 4227072 | tf_op jit(solution)/shard_map/all_to_all | solution.py:265
  59.3 1.9 %collective-permute-start = (bf16[4096,128]{1,0:T(8,128)(2,1)}, bf16[4096,128]{1,0:T(8,128)(2,1)}, u32[]{:S(2)}, u32[]{:S(2)}) collective-permute-start(bf16[4096,128]{1,0:T(8,128)(2,1)} %bitcast.2.g0), channel_id=1, source_target_pairs={{0,8},{8,0},{1,9},{9,1},{2,10},{10,2},{3,11},{11,3},{4,12},{12,4},... | collective-permute-start | bytes 3145736 | tf_op jit(solution)/shard_map/ppermute | solution.py:287
  61.2 2.4 %collective-permute-start.1 = (bf16[4096,128]{1,0:T(8,128)(2,1)}, bf16[4096,128]{1,0:T(8,128)(2,1)}, u32[]{:S(2)}, u32[]{:S(2)}) collective-permute-start(bf16[4096,128]{1,0:T(8,128)(2,1)} %bitcast.3.u0), channel_id=1, source_target_pairs={{0,8},{8,0},{1,9},{9,1},{2,10},{10,2},{3,11},{11,3},{4,12},{12,4},... | collective-permute-start | bytes 3145736 | tf_op jit(solution)/shard_map/ppermute | solution.py:287
  65.0 3.4 %collective-permute-start.3 = (bf16[128,2048]{1,0:T(8,128)(2,1)S(1)}, bf16[128,2048]{1,0:T(8,128)(2,1)S(1)}, u32[]{:S(2)}, u32[]{:S(2)}) collective-permute-start(bf16[128,2048]{1,0:T(8,128)(2,1)S(1)} %get-tuple-element.17.refs_0_), channel_id=1, source_target_pairs={{0,16},{16,0},{256,272},{272,256},{1,17},{17,1},{257,273},{273,257... | collective-permute-start | bytes 1572872 | tf_op jit(solution)/shard_map/ppermute | solution.py:269
  68.4 2.5 %collective-permute-start.5 = (bf16[128,2048]{1,0:T(8,128)(2,1)S(1)}, bf16[128,2048]{1,0:T(8,128)(2,1)}, u32[]{:S(2)}, u32[]{:S(2)}) collective-permute-start(bf16[128,2048]{1,0:T(8,128)(2,1)S(1)} %get-tuple-element.16), channel_id=1, source_target_pairs={{0,256},{16,272},{256,0},{272,16},{1,257},{17,273},{257,1},{273,17... | collective-permute-start | bytes 1572872 | tf_op jit(solution)/shard_map/ppermute | solution.py:269
  70.8 3.4 %collective-permute-start.7 = (bf16[128,2048]{1,0:T(8,128)(2,1)S(1)}, bf16[128,2048]{1,0:T(8,128)(2,1)}, u32[]{:S(2)}, u32[]{:S(2)}) collective-permute-start(bf16[128,2048]{1,0:T(8,128)(2,1)S(1)} %get-tuple-element.16), channel_id=1, source_target_pairs={{0,272},{16,256},{256,16},{272,0},{1,273},{17,257},{257,17},{273,1... | collective-permute-start | bytes 1572872 | tf_op jit(solution)/shard_map/ppermute | solution.py:269
  74.2 22.1 %collective-permute-done.3.refs_2_ = bf16[128,2048]{1,0:T(8,128)(2,1)S(1)} collective-permute-done((bf16[128,2048]{1,0:T(8,128)(2,1)S(1)}, bf16[128,2048]{1,0:T(8,128)(2,1)S(1)}, u32[]{:S(2)}, u32[]{:S(2)}) %collective-permute-start.3) | collective-permute-done | bytes 524320 | tf_op jit(solution)/shard_map/ppermute | solution.py:269
  96.3 1.9 %collective-permute-start.2 = (bf16[128,2048]{1,0:T(8,128)(2,1)S(1)}, bf16[128,2048]{1,0:T(8,128)(2,1)}, u32[]{:S(2)}, u32[]{:S(2)}) collective-permute-start(bf16[128,2048]{1,0:T(8,128)(2,1)S(1)} %get-tuple-element.17.refs_0_), channel_id=1, source_target_pairs={{0,8},{8,0},{1,9},{9,1},{2,10},{10,2},{3,11},{11,3},{4,12},{12,4},... | collective-permute-start | bytes 1572872 | tf_op jit(solution)/shard_map/ppermute | solution.py:287
  98.3 2.4 %collective-permute-start.4 = (bf16[128,2048]{1,0:T(8,128)(2,1)S(1)}, bf16[128,2048]{1,0:T(8,128)(2,1)}, u32[]{:S(2)}, u32[]{:S(2)}) collective-permute-start(bf16[128,2048]{1,0:T(8,128)(2,1)S(1)} %collective-permute-done.3.refs_2_), channel_id=1, source_target_pairs={{0,8},{8,0},{1,9},{9,1},{2,10},{10,2},{3,11},{11,3},{4,12},{12,4},... | collective-permute-start | bytes 1572872 | tf_op jit(solution)/shard_map/ppermute | solution.py:287
  100.7 2.7 %collective-permute-done.7.refs_6_ = bf16[128,2048]{1,0:T(8,128)(2,1)} collective-permute-done((bf16[128,2048]{1,0:T(8,128)(2,1)S(1)}, bf16[128,2048]{1,0:T(8,128)(2,1)}, u32[]{:S(2)}, u32[]{:S(2)}) %collective-permute-start.7) | collective-permute-done | bytes 524320 | tf_op jit(solution)/shard_map/ppermute | solution.py:269
  103.4 1.9 %collective-permute-start.6 = (bf16[128,2048]{1,0:T(8,128)(2,1)}, bf16[128,2048]{1,0:T(8,128)(2,1)}, u32[]{:S(2)}, u32[]{:S(2)}) collective-permute-start(bf16[128,2048]{1,0:T(8,128)(2,1)} %collective-permute-done.5.refs_4_), channel_id=1, source_target_pairs={{0,8},{8,0},{1,9},{9,1},{2,10},{10,2},{3,11},{11,3},{4,12},{12,4},... | collective-permute-start | bytes 1572872 | tf_op jit(solution)/shard_map/ppermute | solution.py:287
  105.3 2.4 %collective-permute-start.8 = (bf16[128,2048]{1,0:T(8,128)(2,1)}, bf16[128,2048]{1,0:T(8,128)(2,1)}, u32[]{:S(2)}, u32[]{:S(2)}) collective-permute-start(bf16[128,2048]{1,0:T(8,128)(2,1)} %collective-permute-done.7.refs_6_), channel_id=1, source_target_pairs={{0,8},{8,0},{1,9},{9,1},{2,10},{10,2},{3,11},{11,3},{4,12},{12,4},... | collective-permute-start | bytes 1572872 | tf_op jit(solution)/shard_map/ppermute | solution.py:287
  107.8 4.1 %gate_up.1 = bf16[4,128,256]{2,1,0:T(8,128)(2,1)} custom-call(bf16[4,1032,256]{2,1,0:T(8,128)(2,1)S(1)} %all-to-all-done.2.x_ref, bf16[4096,128]{1,0:T(8,128)(2,1)} %bitcast.2.g0, bf16[4096,128]{1,0:T(8,128)(2,1)} %bitcast.3.u0, bf16[4096,128]{1,0:T(8,128)(2,1)} %collective-permute-done.g1, bf16[4096,128]{1,0:T(8,128)(2,1)} %collective-permute-done.1.u1), custom_call_target="tpu_custom_call" | custom-call | tf_op jit(solution)/shard_map/gate_up/pallas_call | solution.py:197
  111.9 4.9 %all-to-all-start.3 = ((bf16[4,128,256]{2,1,0:T(8,128)(2,1)}), bf16[4,128,256]{2,1,0:T(8,128)(2,1)S(1)}, u32[]{:S(2)}, u32[]{:S(2)}) async-start(bf16[4,128,256]{2,1,0:T(8,128)(2,1)} %gate_up.1), calls=%async_computation.3 | async-start | bytes 524288 | tf_op jit(solution)/shard_map/all_to_all | solution.py:265
  116.8 5.0 %all-to-all-done.3.act_ref = bf16[4,128,256]{2,1,0:T(8,128)(2,1)S(1)} async-done(((bf16[4,128,256]{2,1,0:T(8,128)(2,1)}), bf16[4,128,256]{2,1,0:T(8,128)(2,1)S(1)}, u32[]{:S(2)}, u32[]{:S(2)}) %all-to-all-start.3) | async-done | bytes 262176 | tf_op jit(solution)/shard_map/all_to_all | solution.py:265
  121.8 4.8 %down.1 = bf16[8,128,256]{2,1,0:T(8,128)(2,1)} custom-call(s32[4]{0:T(128)S(1)} %iota_xor_fusion.where_ref, bf16[4,128,256]{2,1,0:T(8,128)(2,1)S(1)} %all-to-all-done.3.act_ref, bf16[128,2048]{1,0:T(8,128)(2,1)} %copy-done, bf16[128,2048]{1,0:T(8,128)(2,1)} %collective-permute-done.2.refs_1_, bf16[128,2048]{1,0:T(8,128)(2,1)} %copy-done.1, ...), custom_call_target="tpu_custom_call" | custom-call | tf_op jit(solution)/shard_map/down/pallas_call | solution.py:215
  126.6 3.5 %all-to-all-start.4 = ((bf16[8,128,256]{2,1,0:T(8,128)(2,1)}), bf16[8,128,256]{2,1,0:T(8,128)(2,1)S(1)}, u32[]{:S(2)}, u32[]{:S(2)}) async-start(bf16[8,128,256]{2,1,0:T(8,128)(2,1)} %down.1), calls=%async_computation.4 | async-start | bytes 1048576 | tf_op jit(solution)/shard_map/all_to_all | solution.py:265
  130.3 17.5 %all-to-all-done.4.x_ref = bf16[8,128,256]{2,1,0:T(8,128)(2,1)S(1)} async-done(((bf16[8,128,256]{2,1,0:T(8,128)(2,1)}), bf16[8,128,256]{2,1,0:T(8,128)(2,1)S(1)}, u32[]{:S(2)}, u32[]{:S(2)}) %all-to-all-start.4) | async-done | bytes 524320 | tf_op jit(solution)/shard_map/all_to_all | solution.py:265
  149.2 3.8 %all-to-all-start.5 = ((bf16[8,32,256]{2,1,0:T(8,128)(2,1)}), bf16[8,32,256]{2,1,0:T(8,128)(2,1)S(1)}, u32[]{:S(2)}, u32[]{:S(2)}) async-start(bf16[8,32,256]{2,1,0:T(8,128)(2,1)} %home.1), calls=%async_computation.5 | async-start | bytes 262144 | tf_op jit(solution)/shard_map/all_to_all | solution.py:265
  153.1 10.1 %all-to-all-done.5 = bf16[8,32,256]{2,1,0:T(8,128)(2,1)S(1)} async-done(((bf16[8,32,256]{2,1,0:T(8,128)(2,1)}), bf16[8,32,256]{2,1,0:T(8,128)(2,1)S(1)}, u32[]{:S(2)}, u32[]{:S(2)}) %all-to-all-start.5) | async-done | bytes 131104 | tf_op jit(solution)/shard_map/all_to_all | solution.py:265
  (31 shorter events, 8.5 us)
Async XLA Ops:
  5.1 18.9 %all-to-all-start = ((bf16[8,32,256]{2,1,0:T(8,128)(2,1)}), bf16[8,32,256]{2,1,0:T(8,128)(2,1)S(1)}, u32[]{:S(2)}, u32[]{:S(2)}) async-start(bf16[8,32,256]{2,1,0:T(8,128)(2,1)} %shard_map.73), calls=%async_computation | async-start | bytes 262144 | tf_op jit(solution)/shard_map/all_to_all | solution.py:265
  54.4 53.3 %all-to-all-start.2 = ((bf16[4,1032,256]{2,1,0:T(8,128)(2,1)}), bf16[4,1032,256]{2,1,0:T(8,128)(2,1)S(1)}, u32[]{:S(2)}, u32[]{:S(2)}) async-start(bf16[4,1032,256]{2,1,0:T(8,128)(2,1)} %prep.1), calls=%async_computation.2 | async-start | bytes 4227072 | tf_op jit(solution)/shard_map/all_to_all | solution.py:265
  59.3 46.0 %collective-permute-start = (bf16[4096,128]{1,0:T(8,128)(2,1)}, bf16[4096,128]{1,0:T(8,128)(2,1)}, u32[]{:S(2)}, u32[]{:S(2)}) collective-permute-start(bf16[4096,128]{1,0:T(8,128)(2,1)} %bitcast.2.g0), channel_id=1, source_target_pairs={{0,8},{8,0},{1,9},{9,1},{2,10},{10,2},{3,11},{11,3},{4,12},{12,4},... | collective-permute-start | bytes 3145736 | tf_op jit(solution)/shard_map/ppermute | solution.py:287
  61.2 46.5 %collective-permute-start.1 = (bf16[4096,128]{1,0:T(8,128)(2,1)}, bf16[4096,128]{1,0:T(8,128)(2,1)}, u32[]{:S(2)}, u32[]{:S(2)}) collective-permute-start(bf16[4096,128]{1,0:T(8,128)(2,1)} %bitcast.3.u0), channel_id=1, source_target_pairs={{0,8},{8,0},{1,9},{9,1},{2,10},{10,2},{3,11},{11,3},{4,12},{12,4},... | collective-permute-start | bytes 3145736 | tf_op jit(solution)/shard_map/ppermute | solution.py:287
  65.0 46.9 %copy-start = (bf16[128,2048]{1,0:T(8,128)(2,1)}, bf16[128,2048]{1,0:T(8,128)(2,1)S(1)}, u32[]{:S(2)}) copy-start(bf16[128,2048]{1,0:T(8,128)(2,1)S(1)} %get-tuple-element.17.refs_0_) | copy-start | bytes 1572868
  65.0 31.4 %collective-permute-start.3 = (bf16[128,2048]{1,0:T(8,128)(2,1)S(1)}, bf16[128,2048]{1,0:T(8,128)(2,1)S(1)}, u32[]{:S(2)}, u32[]{:S(2)}) collective-permute-start(bf16[128,2048]{1,0:T(8,128)(2,1)S(1)} %get-tuple-element.17.refs_0_), channel_id=1, source_target_pairs={{0,16},{16,0},{256,272},{272,256},{1,17},{17,1},{257,273},{273,257... | collective-permute-start | bytes 1572872 | tf_op jit(solution)/shard_map/ppermute | solution.py:269
  68.4 29.9 %collective-permute-start.5 = (bf16[128,2048]{1,0:T(8,128)(2,1)S(1)}, bf16[128,2048]{1,0:T(8,128)(2,1)}, u32[]{:S(2)}, u32[]{:S(2)}) collective-permute-start(bf16[128,2048]{1,0:T(8,128)(2,1)S(1)} %get-tuple-element.16), channel_id=1, source_target_pairs={{0,256},{16,272},{256,0},{272,16},{1,257},{17,273},{257,1},{273,17... | collective-permute-start | bytes 1572872 | tf_op jit(solution)/shard_map/ppermute | solution.py:269
  70.8 32.6 %collective-permute-start.7 = (bf16[128,2048]{1,0:T(8,128)(2,1)S(1)}, bf16[128,2048]{1,0:T(8,128)(2,1)}, u32[]{:S(2)}, u32[]{:S(2)}) collective-permute-start(bf16[128,2048]{1,0:T(8,128)(2,1)S(1)} %get-tuple-element.16), channel_id=1, source_target_pairs={{0,272},{16,256},{256,16},{272,0},{1,273},{17,257},{257,17},{273,1... | collective-permute-start | bytes 1572872 | tf_op jit(solution)/shard_map/ppermute | solution.py:269
  96.3 15.6 %copy-start.1 = (bf16[128,2048]{1,0:T(8,128)(2,1)}, bf16[128,2048]{1,0:T(8,128)(2,1)S(1)}, u32[]{:S(2)}) copy-start(bf16[128,2048]{1,0:T(8,128)(2,1)S(1)} %collective-permute-done.3.refs_2_) | copy-start | bytes 1572868
  96.3 20.5 %collective-permute-start.2 = (bf16[128,2048]{1,0:T(8,128)(2,1)S(1)}, bf16[128,2048]{1,0:T(8,128)(2,1)}, u32[]{:S(2)}, u32[]{:S(2)}) collective-permute-start(bf16[128,2048]{1,0:T(8,128)(2,1)S(1)} %get-tuple-element.17.refs_0_), channel_id=1, source_target_pairs={{0,8},{8,0},{1,9},{9,1},{2,10},{10,2},{3,11},{11,3},{4,12},{12,4},... | collective-permute-start | bytes 1572872 | tf_op jit(solution)/shard_map/ppermute | solution.py:287
  98.3 18.5 %collective-permute-start.4 = (bf16[128,2048]{1,0:T(8,128)(2,1)S(1)}, bf16[128,2048]{1,0:T(8,128)(2,1)}, u32[]{:S(2)}, u32[]{:S(2)}) collective-permute-start(bf16[128,2048]{1,0:T(8,128)(2,1)S(1)} %collective-permute-done.3.refs_2_), channel_id=1, source_target_pairs={{0,8},{8,0},{1,9},{9,1},{2,10},{10,2},{3,11},{11,3},{4,12},{12,4},... | collective-permute-start | bytes 1572872 | tf_op jit(solution)/shard_map/ppermute | solution.py:287
  103.4 13.4 %collective-permute-start.6 = (bf16[128,2048]{1,0:T(8,128)(2,1)}, bf16[128,2048]{1,0:T(8,128)(2,1)}, u32[]{:S(2)}, u32[]{:S(2)}) collective-permute-start(bf16[128,2048]{1,0:T(8,128)(2,1)} %collective-permute-done.5.refs_4_), channel_id=1, source_target_pairs={{0,8},{8,0},{1,9},{9,1},{2,10},{10,2},{3,11},{11,3},{4,12},{12,4},... | collective-permute-start | bytes 1572872 | tf_op jit(solution)/shard_map/ppermute | solution.py:287
  105.3 11.5 %collective-permute-start.8 = (bf16[128,2048]{1,0:T(8,128)(2,1)}, bf16[128,2048]{1,0:T(8,128)(2,1)}, u32[]{:S(2)}, u32[]{:S(2)}) collective-permute-start(bf16[128,2048]{1,0:T(8,128)(2,1)} %collective-permute-done.7.refs_6_), channel_id=1, source_target_pairs={{0,8},{8,0},{1,9},{9,1},{2,10},{10,2},{3,11},{11,3},{4,12},{12,4},... | collective-permute-start | bytes 1572872 | tf_op jit(solution)/shard_map/ppermute | solution.py:287
  111.9 9.9 %all-to-all-start.3 = ((bf16[4,128,256]{2,1,0:T(8,128)(2,1)}), bf16[4,128,256]{2,1,0:T(8,128)(2,1)S(1)}, u32[]{:S(2)}, u32[]{:S(2)}) async-start(bf16[4,128,256]{2,1,0:T(8,128)(2,1)} %gate_up.1), calls=%async_computation.3 | async-start | bytes 524288 | tf_op jit(solution)/shard_map/all_to_all | solution.py:265
  116.8 13.4 %copy-start.2 = (s32[8,2]{0,1:T(2,128)S(1)}, s32[8,2]{0,1:T(2,128)}, u32[]{:S(2)}) copy-start(s32[8,2]{0,1:T(2,128)} %param.10) | copy-start | bytes 196
  116.8 36.3 %copy-start.3 = (f32[32,2]{0,1:T(2,128)S(1)}, f32[32,2]{0,1:T(2,128)}, u32[]{:S(2)}) copy-start(f32[32,2]{0,1:T(2,128)} %param.9) | copy-start | bytes 772
  126.6 21.2 %all-to-all-start.4 = ((bf16[8,128,256]{2,1,0:T(8,128)(2,1)}), bf16[8,128,256]{2,1,0:T(8,128)(2,1)S(1)}, u32[]{:S(2)}, u32[]{:S(2)}) async-start(bf16[8,128,256]{2,1,0:T(8,128)(2,1)} %down.1), calls=%async_computation.4 | async-start | bytes 1048576 | tf_op jit(solution)/shard_map/all_to_all | solution.py:265
  149.2 14.0 %all-to-all-start.5 = ((bf16[8,32,256]{2,1,0:T(8,128)(2,1)}), bf16[8,32,256]{2,1,0:T(8,128)(2,1)S(1)}, u32[]{:S(2)}, u32[]{:S(2)}) async-start(bf16[8,32,256]{2,1,0:T(8,128)(2,1)} %home.1), calls=%async_computation.5 | async-start | bytes 262144 | tf_op jit(solution)/shard_map/all_to_all | solution.py:265

commit v5 on v3

v5 whole, which is shorter than its diff:
```python
import jax
import jax.numpy as jnp
from jax import lax
from jax.experimental import pallas as pl
from jax.experimental.pallas import tpu as pltpu
from jax.sharding import Mesh, PartitionSpec as P


EXPERTS = 8
MOST = 4
HID = 8
F32 = jnp.float32
BF16 = jnp.bfloat16

GROUP = ("group",)
SQUARE = ("sec", "xlo")


def prep_kernel(x_ref, out_ref, y_ref, sems):
    n, rows, w = x_ref.shape
    rows -= 8
    copies = out_ref.shape[0]
    total = jnp.zeros((rows, w), F32)
    for z in range(n):
        x = x_ref[z, 0:rows, :].astype(F32)
        g = x_ref[z, rows : rows + 1, :].astype(F32)
        total = total + x * x
        y_ref[z * rows : (z + 1) * rows, :] = (x * g).astype(BF16)
    col = jnp.sum(total, axis=1, keepdims=True)
    row = jnp.transpose(jnp.broadcast_to(col, (rows, rows)))[0:8, :]
    hi = row.astype(BF16).astype(F32)
    mid = (row - hi).astype(BF16).astype(F32)
    low = row - hi - mid
    which = lax.broadcasted_iota(jnp.int32, (8, rows), 0)
    parts = jnp.where(which == 0, hi, jnp.where(which == 1, mid, jnp.where(which == 2, low, 0.0)))
    y_ref[n * rows : n * rows + 8, :] = jnp.concatenate([parts, jnp.zeros((8, w - rows), F32)], axis=1).astype(BF16)
    sends = [pltpu.make_async_copy(y_ref, out_ref.at[j], sems.at[j]) for j in range(copies)]
    for send in sends:
        send.start()
    for send in sends:
        send.wait()


def gate_up_kernel(x_ref, g0, u0, g1, u1, act_ref, w_ref, acc_ref, sems):
    _, tall, w = x_ref.shape
    n = HID
    rows = (tall - 8) // n
    deep, ff = g0.shape
    chunks = 4
    per = deep // chunks
    loads = [
        [
            pltpu.make_async_copy(
                ref.at[c * per : (c + 1) * per, :], w_ref.at[i, c * per : (c + 1) * per, :], sems.at[c, i]
            )
            for i, ref in enumerate((g0, u0, g1, u1))
        ]
        for c in range(chunks)
    ]
    for group in loads:
        for load in group:
            load.start()
    scales = []
    for x in range(2):
        parts = [x_ref[2 * s + x, n * rows : n * rows + 8, 0:rows].astype(F32) for s in range(2)]
        both = parts[0] + parts[1]
        total = both[0:1, :] + both[1:2, :] + both[2:3, :]
        inv = 1.0 / jnp.sqrt(total / deep + 1e-05)
        scales.append(jnp.transpose(jnp.broadcast_to(inv, (rows, rows))))
    for c in range(chunks):
        pieces = range(c * per // w, (c + 1) * per // w)
        xs = jnp.concatenate(
            [
                jnp.concatenate(
                    [x_ref[2 * (p // n) + x, (p % n) * rows : (p % n + 1) * rows, :] for p in pieces], axis=1
                )
                for x in range(2)
            ],
            axis=0,
        )
        for load in loads[c]:
            load.wait()
        for k in range(2):
            ws = jnp.concatenate([w_ref[i, c * per : (c + 1) * per, :] for i in (2 * k, 2 * k + 1)], axis=1)
            part = jnp.dot(xs, ws, preferred_element_type=F32)
            if c == 0:
                acc_ref[k] = part
            else:
                acc_ref[k] += part
    for k in range(2):
        for x in range(2):
            block = acc_ref[k, x * rows : (x + 1) * rows, :]
            gate = block[:, 0:ff] * scales[x]
            up = block[:, ff:] * scales[x]
            act = (gate / (1.0 + jnp.exp(-gate)) * up).astype(BF16)
            for s in range(2):
                act_ref[2 * s + x, :, k * ff : (k + 1) * ff] = act


def down_kernel(act_ref, *refs):
    *downs, out_ref, w_ref, acc_ref, y_ref, sems, out_sems = refs
    n, _, w = out_ref.shape
    ff = downs[0].shape[0]
    loads = [pltpu.make_async_copy(ref, w_ref.at[i * ff : (i + 1) * ff], sems.at[i]) for i, ref in enumerate(downs)]
    for load in loads:
        load.start()
    place = lax.axis_index("sec") * 2 + lax.axis_index("xlo")
    sends = []
    for h in range(2):
        act = jnp.concatenate([act_ref[place ^ k] for k in (2 * h, 2 * h + 1)], axis=1)
        for load in loads[4 * h : 4 * h + 4]:
            load.wait()
        for z in range(n):
            part = jnp.dot(
                act, w_ref[4 * h * ff : 4 * (h + 1) * ff, z * w : (z + 1) * w], preferred_element_type=F32
            )
            if h == 0:
                acc_ref[z] = part
                continue
            y_ref[z] = (acc_ref[z] + part).astype(BF16)
            if z % 2:
                sends.append(
                    pltpu.make_async_copy(
                        y_ref.at[z - 1 : z + 1], out_ref.at[z - 1 : z + 1], out_sems.at[z // 2]
                    )
                )
                sends[-1].start()
    for send in sends:
        send.wait()


VM = pl.BlockSpec(memory_space=pltpu.VMEM)
HBM = pl.BlockSpec(memory_space=pltpu.HBM)


def vm(x):
    return pltpu.with_memory_space_constraint(x, pltpu.VMEM)


def hbm(x):
    return pltpu.with_memory_space_constraint(x, pltpu.HBM)


def prepared(x):
    n, rows, w = x.shape
    tall = n * (rows - 8) + 8
    return pl.pallas_call(
        prep_kernel,
        out_shape=pltpu.HBM((4, tall, w), BF16),
        in_specs=[VM],
        out_specs=HBM,
        scratch_shapes=[pltpu.VMEM((tall, w), BF16), pltpu.SemaphoreType.DMA((4,))],
        compiler_params=pltpu.CompilerParams(vmem_limit_bytes=4 << 20),
        name="prep",
    )(vm(x))


def gated(x, weights):
    _, tall, _ = x.shape
    rows = (tall - 8) // HID
    deep, ff = weights[0].shape
    return pl.pallas_call(
        gate_up_kernel,
        out_shape=pltpu.HBM((4, rows, 2 * ff), BF16),
        in_specs=[VM] + [HBM] * 4,
        out_specs=VM,
        scratch_shapes=[
            pltpu.VMEM((4, deep, ff), BF16),
            pltpu.VMEM((2, 2 * rows, 2 * ff), F32),
            pltpu.SemaphoreType.DMA((4, 4)),
        ],
        compiler_params=pltpu.CompilerParams(vmem_limit_bytes=16 << 20),
        name="gate_up",
    )(vm(x), *[hbm(v) for v in weights])


def lowered(act, downs):
    _, rows, _ = act.shape
    ff, wide = downs[0].shape
    shape = (HID, rows, wide // HID)
    return pl.pallas_call(
        down_kernel,
        out_shape=pltpu.HBM(shape, BF16),
        in_specs=[VM] + [HBM] * 8,
        out_specs=HBM,
        scratch_shapes=[
            pltpu.VMEM((8 * ff, wide), BF16),
            pltpu.VMEM(shape, F32),
            pltpu.VMEM(shape, BF16),
            pltpu.SemaphoreType.DMA((8,)),
            pltpu.SemaphoreType.DMA((HID // 2,)),
        ],
        compiler_params=pltpu.CompilerParams(vmem_limit_bytes=16 << 20),
        name="down",
    )(vm(act), *[hbm(v) for v in downs])


def exchange(x, axes):
    return lax.all_to_all(x, axes, split_axis=0, concat_axis=0, tiled=True)


def added(x):
    return jnp.sum(x.astype(F32), axis=0).astype(BF16)


def layer(tokens, norm_gain, route_weight, block_experts, w_gate, w_up, w_down):
    rows, w = tokens.shape
    groups = lax.axis_size("group")
    n_hid = lax.axis_size("hid")
    me = lax.axis_index("group")
    gate0, up0, down0 = w_gate[0], w_up[0], w_down[0]
    sec = lax.axis_index("sec")
    part = down0.shape[1] // 2
    down_away = lax.dynamic_slice_in_dim(down0, (1 - sec) * part, part, 1)

    def sent(x, flip):
        return lax.ppermute(x, SQUARE, [(i, i ^ flip) for i in range(4)])

    def swapped(x):
        return lax.ppermute(x, "core", [(0, 1), (1, 0)])

    away_x = sent(down_away, 3)
    gate1, up1 = swapped(gate0), swapped(up0)

    hit = jnp.any(block_experts == me, axis=1)
    slot_of_block = jnp.maximum(jnp.cumsum(hit.astype(jnp.int32)) - 1, 0)
    slot_ids = jnp.arange(MOST, dtype=jnp.int32)
    match = (slot_of_block[None, :] == slot_ids[:, None]) & hit[None, :]
    block_of_slot = jnp.sum(jnp.where(match, jnp.arange(groups, dtype=jnp.int32)[None, :], 0), axis=1)

    mine = jnp.take(block_experts, me, axis=0, mode="clip")
    named = mine[None, :] == jnp.arange(EXPERTS, dtype=jnp.int32)[:, None]
    factor = jnp.sum(jnp.where(named[:, None, :], route_weight[None], 0.0), axis=2)

    blocks = exchange(jnp.broadcast_to(tokens[None], (groups, rows, w)), GROUP)
    tall = MOST * rows
    picked = jnp.take(blocks, block_of_slot, axis=0, mode="clip").reshape(tall, w)
    picked, down_late = lax.optimization_barrier((picked, down0))
    down_here = lax.dynamic_slice_in_dim(down_late, sec * part, part, 1)
    direct = [down_here, sent(down_here, 1), sent(down_away, 2), away_x]
    downs = [d for piece in direct for d in (piece, swapped(piece))]
    picked = jnp.concatenate([picked, jnp.broadcast_to(norm_gain[None, :], (8, w))], axis=0)
    wide = exchange(jnp.broadcast_to(picked[None], (n_hid, tall + 8, w)), "hid")
    ready = prepared(wide)
    every = exchange(ready, SQUARE)
    act = exchange(gated(every, (gate0, up0, gate1, up1)), SQUARE)
    summed = added(exchange(lowered(act, downs), "hid")).reshape(MOST, rows, w)
    outgoing = jnp.take(summed, slot_of_block, axis=0, mode="clip")
    back = exchange(outgoing, GROUP)
    return jnp.sum(back.astype(F32) * factor[:, :, None], axis=0).astype(BF16)


def solution(mesh):
    devices = mesh.devices.reshape(2, EXPERTS, 2, 2, 8)
    fine = Mesh(devices, ("sec", "group", "xlo", "core", "hid"))
    exp = ("group", "xlo", "core")
    return jax.shard_map(
        layer,
        mesh=fine,
        in_specs=(
            P(exp, ("sec", "hid")),
            P(("sec", "hid")),
            P(exp, None),
            P(),
            P("sec", None, exp + ("hid",)),
            P("sec", None, exp + ("hid",)),
            P("sec", exp + ("hid",), None),
        ),
        out_specs=P(exp, ("sec", "hid")),
        check_vma=False,
    )
```

time: 161 us -> 161 us (level)
  waiting for transfers between devices: 66.7 us -> 69.5 us
  Pallas kernels: 10.8 us -> 8.56 us
    pallas_call x2, Pallas kernels: 9.14 us -> 6.91 us  [the longest x1 3.57 us: gated(): pl.pallas_call(gate_up_kernel, out_shape=pltpu.HBM((4, rows, 2 * ff), BF1...]
    ppermute x3, waiting for transfers between devices: 24.8 us -> 26.9 us  [sent(): return lax.ppermute(x, SQUARE, [(i, i ^ flip) for i in range(4)])]
  transfers between devices with their start and end apart: 14 -> 14, of which waited for: 6 -> 6; matrix products, arithmetic and copies ran while one was open for 2% -> 2% of each run, Pallas kernels for 3% -> 2%
where the time goes in v5:
time: 161 us; the launch traced here: 160 us
  waiting for transfers between devices  69.5 us (43%)
  starting transfers between devices  47.4 us (29%)
  blocking collectives  27 us (17%)
  Pallas kernels  8.56 us (5%)
  local copies, waits for them, and re-layouts  5.79 us (4%)
  other arithmetic  1.96 us (1%)
    all_to_all x5, waiting for transfers between devices, exchange(): return lax.all_to_all(x, axes, split_axis=0, concat_axis=0, tiled=True)  42.6 us
    all_to_all x1, blocking collectives, exchange(): return lax.all_to_all(x, axes, split_axis=0, concat_axis=0, tiled=True)  27 us
    ppermute x3, waiting for transfers between devices, sent(): return lax.ppermute(x, SQUARE, [(i, i ^ flip) for i in range(4)])  26.9 us
    all_to_all x5, starting transfers between devices, exchange(): return lax.all_to_all(x, axes, split_axis=0, concat_axis=0, tiled=True)  25.7 us
    ppermute x6, starting transfers between devices, swapped(): return lax.ppermute(x, 'core', [(0, 1), (1, 0)])  12.5 us
    ppermute x3, starting transfers between devices, sent(): return lax.ppermute(x, SQUARE, [(i, i ^ flip) for i in range(4)])  9.19 us
    pallas_call x1, Pallas kernels, gated(): pl.pallas_call(gate_up_kernel, out_shape=pltpu.HBM((4, rows, 2 * ff), BF1...  3.57 us
    pallas_call x1, Pallas kernels, lowered(): pl.pallas_call(down_kernel, out_shape=pltpu.HBM(shape, BF16), in_specs=[V...  3.34 us
  transfers between devices with their start and end apart: 14, of which 6 were waited for; matrix products, arithmetic and copies ran while one was open for 2% of the time, Pallas kernels for 2%

profile of v5, /device:TPU:8, one launch (start us, length us, event | category | flops | bytes accessed | tf_op | source)
XLA Modules:
  0.0 160.4 jit_solution(7961088354168210239)
XLA Ops:
  1.5 8.7 %all-to-all-start = ((bf16[8,32,256]{2,1,0:T(8,128)(2,1)}), bf16[8,32,256]{2,1,0:T(8,128)(2,1)S(1)}, u32[]{:S(2)}, u32[]{:S(2)}) async-start(bf16[8,32,256]{2,1,0:T(8,128)(2,1)} %broadcast_in_dim.48), calls=%async_computation | async-start | bytes 262144 | tf_op jit(solution)/shard_map/all_to_all | solution.py:199
  11.1 9.2 %all-to-all-done = bf16[8,32,256]{2,1,0:T(8,128)(2,1)S(1)} async-done(((bf16[8,32,256]{2,1,0:T(8,128)(2,1)}), bf16[8,32,256]{2,1,0:T(8,128)(2,1)S(1)}, u32[]{:S(2)}, u32[]{:S(2)}) %all-to-all-start) | async-done | bytes 131104 | tf_op jit(solution)/shard_map/all_to_all | solution.py:199
  21.7 27.0 %all_to_all.30.x_ref = bf16[8,136,256]{2,1,0:T(8,128)(2,1)S(1)} all-to-all(bf16[8,136,256]{2,1,0:T(8,128)(2,1)S(1)} %broadcast_in_dim.74), channel_id=1, replica_groups=mesh['sec'=2,'group'=8,'xlo'=2,'core'=2,'hid'=8] {'hid'}, dimensions={0} | all-to-all | bytes 1114112 | tf_op jit(solution)/shard_map/all_to_all | solution.py:199
  48.7 1.7 %prep.1 = bf16[4,1032,256]{2,1,0:T(8,128)(2,1)} custom-call(bf16[8,136,256]{2,1,0:T(8,128)(2,1)S(1)} %all_to_all.30.x_ref), custom_call_target="tpu_custom_call" | custom-call | tf_op jit(solution)/shard_map/prep/pallas_call | solution.py:147
  50.3 4.9 %all-to-all-start.2 = ((bf16[4,1032,256]{2,1,0:T(8,128)(2,1)}), bf16[4,1032,256]{2,1,0:T(8,128)(2,1)S(1)}, u32[]{:S(2)}, u32[]{:S(2)}) async-start(bf16[4,1032,256]{2,1,0:T(8,128)(2,1)} %prep.1), calls=%async_computation.2 | async-start | bytes 4227072 | tf_op jit(solution)/shard_map/all_to_all | solution.py:199
  55.2 1.9 %collective-permute-start = (bf16[4096,128]{1,0:T(8,128)(2,1)}, bf16[4096,128]{1,0:T(8,128)(2,1)}, u32[]{:S(2)}, u32[]{:S(2)}) collective-permute-start(bf16[4096,128]{1,0:T(8,128)(2,1)} %bitcast.12), channel_id=1, source_target_pairs={{0,8},{8,0},{1,9},{9,1},{2,10},{10,2},{3,11},{11,3},{4,12},{12,4},... | collective-permute-start | bytes 3145736 | tf_op jit(solution)/shard_map/ppermute | solution.py:220
  57.1 2.4 %collective-permute-start.1 = (bf16[4096,128]{1,0:T(8,128)(2,1)}, bf16[4096,128]{1,0:T(8,128)(2,1)}, u32[]{:S(2)}, u32[]{:S(2)}) collective-permute-start(bf16[4096,128]{1,0:T(8,128)(2,1)} %bitcast.14), channel_id=1, source_target_pairs={{0,8},{8,0},{1,9},{9,1},{2,10},{10,2},{3,11},{11,3},{4,12},{12,4},... | collective-permute-start | bytes 3145736 | tf_op jit(solution)/shard_map/ppermute | solution.py:220
  60.4 1.9 %collective-permute-start.5 = (bf16[128,2048]{1,0:T(8,128)(2,1)}, bf16[128,2048]{1,0:T(8,128)(2,1)}, u32[]{:S(2)}, u32[]{:S(2)}) collective-permute-start(bf16[128,2048]{1,0:T(8,128)(2,1)} %dynamic-slice_bitcast_fusion), channel_id=1, source_target_pairs={{0,256},{16,272},{256,0},{272,16},{1,257},{17,273},{257,1},{273,17... | collective-permute-start | bytes 1572872 | tf_op jit(solution)/shard_map/ppermute | solution.py:217
  62.4 4.8 %collective-permute-start.7 = (bf16[128,2048]{1,0:T(8,128)(2,1)}, bf16[128,2048]{1,0:T(8,128)(2,1)}, u32[]{:S(2)}, u32[]{:S(2)}) collective-permute-start(bf16[128,2048]{1,0:T(8,128)(2,1)} %dynamic-slice_bitcast_fusion), channel_id=1, source_target_pairs={{0,272},{16,256},{256,16},{272,0},{1,273},{17,257},{257,17},{273,1... | collective-permute-start | bytes 1572872 | tf_op jit(solution)/shard_map/ppermute | solution.py:217
  68.0 2.5 %collective-permute-start.3 = (bf16[128,2048]{1,0:T(8,128)(2,1)}, bf16[128,2048]{1,0:T(8,128)(2,1)}, u32[]{:S(2)}, u32[]{:S(2)}) collective-permute-start(bf16[128,2048]{1,0:T(8,128)(2,1)} %constant_dynamic-slice_fusion.refs_0_), channel_id=1, source_target_pairs={{0,16},{16,0},{256,272},{272,256},{1,17},{17,1},{257,273},{273,257... | collective-permute-start | bytes 1572872 | tf_op jit(solution)/shard_map/ppermute | solution.py:217
  70.5 20.5 %collective-permute-done.5.refs_4_ = bf16[128,2048]{1,0:T(8,128)(2,1)} collective-permute-done((bf16[128,2048]{1,0:T(8,128)(2,1)}, bf16[128,2048]{1,0:T(8,128)(2,1)}, u32[]{:S(2)}, u32[]{:S(2)}) %collective-permute-start.5) | collective-permute-done | bytes 524320 | tf_op jit(solution)/shard_map/ppermute | solution.py:217
  91.0 1.9 %collective-permute-start.2 = (bf16[128,2048]{1,0:T(8,128)(2,1)}, bf16[128,2048]{1,0:T(8,128)(2,1)}, u32[]{:S(2)}, u32[]{:S(2)}) collective-permute-start(bf16[128,2048]{1,0:T(8,128)(2,1)} %constant_dynamic-slice_fusion.refs_0_), channel_id=1, source_target_pairs={{0,8},{8,0},{1,9},{9,1},{2,10},{10,2},{3,11},{11,3},{4,12},{12,4},... | collective-permute-start | bytes 1572872 | tf_op jit(solution)/shard_map/ppermute | solution.py:220
  92.9 6.4 %collective-permute-done.7.refs_6_ = bf16[128,2048]{1,0:T(8,128)(2,1)} collective-permute-done((bf16[128,2048]{1,0:T(8,128)(2,1)}, bf16[128,2048]{1,0:T(8,128)(2,1)}, u32[]{:S(2)}, u32[]{:S(2)}) %collective-permute-start.7) | collective-permute-done | bytes 524320 | tf_op jit(solution)/shard_map/ppermute | solution.py:217
  99.3 1.9 %collective-permute-start.6 = (bf16[128,2048]{1,0:T(8,128)(2,1)}, bf16[128,2048]{1,0:T(8,128)(2,1)}, u32[]{:S(2)}, u32[]{:S(2)}) collective-permute-start(bf16[128,2048]{1,0:T(8,128)(2,1)} %collective-permute-done.5.refs_4_), channel_id=1, source_target_pairs={{0,8},{8,0},{1,9},{9,1},{2,10},{10,2},{3,11},{11,3},{4,12},{12,4},... | collective-permute-start | bytes 1572872 | tf_op jit(solution)/shard_map/ppermute | solution.py:220
  101.2 2.4 %collective-permute-start.8 = (bf16[128,2048]{1,0:T(8,128)(2,1)}, bf16[128,2048]{1,0:T(8,128)(2,1)}, u32[]{:S(2)}, u32[]{:S(2)}) collective-permute-start(bf16[128,2048]{1,0:T(8,128)(2,1)} %collective-permute-done.7.refs_6_), channel_id=1, source_target_pairs={{0,8},{8,0},{1,9},{9,1},{2,10},{10,2},{3,11},{11,3},{4,12},{12,4},... | collective-permute-start | bytes 1572872 | tf_op jit(solution)/shard_map/ppermute | solution.py:220
  103.6 1.9 %collective-permute-start.4 = (bf16[128,2048]{1,0:T(8,128)(2,1)}, bf16[128,2048]{1,0:T(8,128)(2,1)}, u32[]{:S(2)}, u32[]{:S(2)}) collective-permute-start(bf16[128,2048]{1,0:T(8,128)(2,1)} %collective-permute-done.3.refs_2_), channel_id=1, source_target_pairs={{0,8},{8,0},{1,9},{9,1},{2,10},{10,2},{3,11},{11,3},{4,12},{12,4},... | collective-permute-start | bytes 1572872 | tf_op jit(solution)/shard_map/ppermute | solution.py:220
  105.6 3.6 %gate_up.1 = bf16[4,128,256]{2,1,0:T(8,128)(2,1)} custom-call(bf16[4,1032,256]{2,1,0:T(8,128)(2,1)S(1)} %all-to-all-done.2.x_ref, bf16[4096,128]{1,0:T(8,128)(2,1)} %bitcast.13, bf16[4096,128]{1,0:T(8,128)(2,1)} %bitcast.15, bf16[4096,128]{1,0:T(8,128)(2,1)} %collective-permute-done.g1, bf16[4096,128]{1,0:T(8,128)(2,1)} %collective-permute-done.1.u1), custom_call_target="tpu_custom_call" | custom-call | tf_op jit(solution)/shard_map/gate_up/pallas_call | solution.py:162
  109.2 4.9 %all-to-all-start.3 = ((bf16[4,128,256]{2,1,0:T(8,128)(2,1)}), bf16[4,128,256]{2,1,0:T(8,128)(2,1)S(1)}, u32[]{:S(2)}, u32[]{:S(2)}) async-start(bf16[4,128,256]{2,1,0:T(8,128)(2,1)} %gate_up.1), calls=%async_computation.3 | async-start | bytes 524288 | tf_op jit(solution)/shard_map/all_to_all | solution.py:199
  114.1 5.5 %all-to-all-done.3.act_ref = bf16[4,128,256]{2,1,0:T(8,128)(2,1)S(1)} async-done(((bf16[4,128,256]{2,1,0:T(8,128)(2,1)}), bf16[4,128,256]{2,1,0:T(8,128)(2,1)S(1)}, u32[]{:S(2)}, u32[]{:S(2)}) %all-to-all-start.3) | async-done | bytes 262176 | tf_op jit(solution)/shard_map/all_to_all | solution.py:199
  119.6 3.3 %down.1 = bf16[8,128,256]{2,1,0:T(8,128)(2,1)} custom-call(bf16[4,128,256]{2,1,0:T(8,128)(2,1)S(1)} %all-to-all-done.3.act_ref, bf16[128,2048]{1,0:T(8,128)(2,1)} %constant_dynamic-slice_fusion.refs_0_, bf16[128,2048]{1,0:T(8,128)(2,1)} %collective-permute-done.2.refs_1_, bf16[128,2048]{1,0:T(8,128)(2,1)} %collective-permute-done.3.refs_2_, ...), custom_call_target="tpu_custom_call" | custom-call | tf_op jit(solution)/shard_map/down/pallas_call | solution.py:181
  122.9 3.5 %all-to-all-start.4 = ((bf16[8,128,256]{2,1,0:T(8,128)(2,1)}), bf16[8,128,256]{2,1,0:T(8,128)(2,1)S(1)}, u32[]{:S(2)}, u32[]{:S(2)}) async-start(bf16[8,128,256]{2,1,0:T(8,128)(2,1)} %down.1), calls=%async_computation.4 | async-start | bytes 1048576 | tf_op jit(solution)/shard_map/all_to_all | solution.py:199
  126.7 17.7 %all-to-all-done.4 = bf16[8,128,256]{2,1,0:T(8,128)(2,1)S(1)} async-done(((bf16[8,128,256]{2,1,0:T(8,128)(2,1)}), bf16[8,128,256]{2,1,0:T(8,128)(2,1)S(1)}, u32[]{:S(2)}, u32[]{:S(2)}) %all-to-all-start.4) | async-done | bytes 524320 | tf_op jit(solution)/shard_map/all_to_all | solution.py:199
  145.6 3.8 %all-to-all-start.5 = ((bf16[8,32,256]{2,1,0:T(8,128)(2,1)}), bf16[8,32,256]{2,1,0:T(8,128)(2,1)S(1)}, u32[]{:S(2)}, u32[]{:S(2)}) async-start(bf16[8,32,256]{2,1,0:T(8,128)(2,1)} %gather_fusion.1), calls=%async_computation.5 | async-start | bytes 262144 | tf_op jit(solution)/shard_map/all_to_all | solution.py:199
  149.6 10.1 %all-to-all-done.5 = bf16[8,32,256]{2,1,0:T(8,128)(2,1)S(1)} async-done(((bf16[8,32,256]{2,1,0:T(8,128)(2,1)}), bf16[8,32,256]{2,1,0:T(8,128)(2,1)S(1)}, u32[]{:S(2)}, u32[]{:S(2)}) %all-to-all-start.5) | async-done | bytes 131104 | tf_op jit(solution)/shard_map/all_to_all | solution.py:199
  (34 shorter events, 7.8 us)
Async XLA Ops:
  0.0 20.9 %copy-start = (bf16[1,128,4096]{2,1,0:T(8,128)(2,1)S(1)}, bf16[1,128,4096]{2,1,0:T(8,128)(2,1)}, u32[]{:S(2)}) copy-start(bf16[1,128,4096]{2,1,0:T(8,128)(2,1)} %param.13) | copy-start | bytes 3145732
  1.5 18.9 %all-to-all-start = ((bf16[8,32,256]{2,1,0:T(8,128)(2,1)}), bf16[8,32,256]{2,1,0:T(8,128)(2,1)S(1)}, u32[]{:S(2)}, u32[]{:S(2)}) async-start(bf16[8,32,256]{2,1,0:T(8,128)(2,1)} %broadcast_in_dim.48), calls=%async_computation | async-start | bytes 262144 | tf_op jit(solution)/shard_map/all_to_all | solution.py:199
  50.3 55.3 %all-to-all-start.2 = ((bf16[4,1032,256]{2,1,0:T(8,128)(2,1)}), bf16[4,1032,256]{2,1,0:T(8,128)(2,1)S(1)}, u32[]{:S(2)}, u32[]{:S(2)}) async-start(bf16[4,1032,256]{2,1,0:T(8,128)(2,1)} %prep.1), calls=%async_computation.2 | async-start | bytes 4227072 | tf_op jit(solution)/shard_map/all_to_all | solution.py:199
  55.2 48.4 %collective-permute-start = (bf16[4096,128]{1,0:T(8,128)(2,1)}, bf16[4096,128]{1,0:T(8,128)(2,1)}, u32[]{:S(2)}, u32[]{:S(2)}) collective-permute-start(bf16[4096,128]{1,0:T(8,128)(2,1)} %bitcast.12), channel_id=1, source_target_pairs={{0,8},{8,0},{1,9},{9,1},{2,10},{10,2},{3,11},{11,3},{4,12},{12,4},... | collective-permute-start | bytes 3145736 | tf_op jit(solution)/shard_map/ppermute | solution.py:220
  57.1 48.4 %collective-permute-start.1 = (bf16[4096,128]{1,0:T(8,128)(2,1)}, bf16[4096,128]{1,0:T(8,128)(2,1)}, u32[]{:S(2)}, u32[]{:S(2)}) collective-permute-start(bf16[4096,128]{1,0:T(8,128)(2,1)} %bitcast.14), channel_id=1, source_target_pairs={{0,8},{8,0},{1,9},{9,1},{2,10},{10,2},{3,11},{11,3},{4,12},{12,4},... | collective-permute-start | bytes 3145736 | tf_op jit(solution)/shard_map/ppermute | solution.py:220
  60.4 30.6 %collective-permute-start.5 = (bf16[128,2048]{1,0:T(8,128)(2,1)}, bf16[128,2048]{1,0:T(8,128)(2,1)}, u32[]{:S(2)}, u32[]{:S(2)}) collective-permute-start(bf16[128,2048]{1,0:T(8,128)(2,1)} %dynamic-slice_bitcast_fusion), channel_id=1, source_target_pairs={{0,256},{16,272},{256,0},{272,16},{1,257},{17,273},{257,1},{273,17... | collective-permute-start | bytes 1572872 | tf_op jit(solution)/shard_map/ppermute | solution.py:217
  62.4 36.9 %collective-permute-start.7 = (bf16[128,2048]{1,0:T(8,128)(2,1)}, bf16[128,2048]{1,0:T(8,128)(2,1)}, u32[]{:S(2)}, u32[]{:S(2)}) collective-permute-start(bf16[128,2048]{1,0:T(8,128)(2,1)} %dynamic-slice_bitcast_fusion), channel_id=1, source_target_pairs={{0,272},{16,256},{256,16},{272,0},{1,273},{17,257},{257,17},{273,1... | collective-permute-start | bytes 1572872 | tf_op jit(solution)/shard_map/ppermute | solution.py:217
  68.0 33.2 %collective-permute-start.3 = (bf16[128,2048]{1,0:T(8,128)(2,1)}, bf16[128,2048]{1,0:T(8,128)(2,1)}, u32[]{:S(2)}, u32[]{:S(2)}) collective-permute-start(bf16[128,2048]{1,0:T(8,128)(2,1)} %constant_dynamic-slice_fusion.refs_0_), channel_id=1, source_target_pairs={{0,16},{16,0},{256,272},{272,256},{1,17},{17,1},{257,273},{273,257... | collective-permute-start | bytes 1572872 | tf_op jit(solution)/shard_map/ppermute | solution.py:217
  91.0 23.1 %collective-permute-start.2 = (bf16[128,2048]{1,0:T(8,128)(2,1)}, bf16[128,2048]{1,0:T(8,128)(2,1)}, u32[]{:S(2)}, u32[]{:S(2)}) collective-permute-start(bf16[128,2048]{1,0:T(8,128)(2,1)} %constant_dynamic-slice_fusion.refs_0_), channel_id=1, source_target_pairs={{0,8},{8,0},{1,9},{9,1},{2,10},{10,2},{3,11},{11,3},{4,12},{12,4},... | collective-permute-start | bytes 1572872 | tf_op jit(solution)/shard_map/ppermute | solution.py:220
  99.3 14.8 %collective-permute-start.6 = (bf16[128,2048]{1,0:T(8,128)(2,1)}, bf16[128,2048]{1,0:T(8,128)(2,1)}, u32[]{:S(2)}, u32[]{:S(2)}) collective-permute-start(bf16[128,2048]{1,0:T(8,128)(2,1)} %collective-permute-done.5.refs_4_), channel_id=1, source_target_pairs={{0,8},{8,0},{1,9},{9,1},{2,10},{10,2},{3,11},{11,3},{4,12},{12,4},... | collective-permute-start | bytes 1572872 | tf_op jit(solution)/shard_map/ppermute | solution.py:220
  101.2 12.8 %collective-permute-start.8 = (bf16[128,2048]{1,0:T(8,128)(2,1)}, bf16[128,2048]{1,0:T(8,128)(2,1)}, u32[]{:S(2)}, u32[]{:S(2)}) collective-permute-start(bf16[128,2048]{1,0:T(8,128)(2,1)} %collective-permute-done.7.refs_6_), channel_id=1, source_target_pairs={{0,8},{8,0},{1,9},{9,1},{2,10},{10,2},{3,11},{11,3},{4,12},{12,4},... | collective-permute-start | bytes 1572872 | tf_op jit(solution)/shard_map/ppermute | solution.py:220
  103.6 10.4 %collective-permute-start.4 = (bf16[128,2048]{1,0:T(8,128)(2,1)}, bf16[128,2048]{1,0:T(8,128)(2,1)}, u32[]{:S(2)}, u32[]{:S(2)}) collective-permute-start(bf16[128,2048]{1,0:T(8,128)(2,1)} %collective-permute-done.3.refs_2_), channel_id=1, source_target_pairs={{0,8},{8,0},{1,9},{9,1},{2,10},{10,2},{3,11},{11,3},{4,12},{12,4},... | collective-permute-start | bytes 1572872 | tf_op jit(solution)/shard_map/ppermute | solution.py:220
  109.2 10.4 %all-to-all-start.3 = ((bf16[4,128,256]{2,1,0:T(8,128)(2,1)}), bf16[4,128,256]{2,1,0:T(8,128)(2,1)S(1)}, u32[]{:S(2)}, u32[]{:S(2)}) async-start(bf16[4,128,256]{2,1,0:T(8,128)(2,1)} %gate_up.1), calls=%async_computation.3 | async-start | bytes 524288 | tf_op jit(solution)/shard_map/all_to_all | solution.py:199
  114.0 12.4 %copy-start.1 = (s32[8,2]{0,1:T(2,128)S(1)}, s32[8,2]{0,1:T(2,128)}, u32[]{:S(2)}) copy-start(s32[8,2]{0,1:T(2,128)} %param.10) | copy-start | bytes 196
  122.9 26.6 %copy-start.2 = (f32[32,2]{0,1:T(2,128)S(1)}, f32[32,2]{0,1:T(2,128)}, u32[]{:S(2)}) copy-start(f32[32,2]{0,1:T(2,128)} %param.9) | copy-start | bytes 772
  122.9 21.4 %all-to-all-start.4 = ((bf16[8,128,256]{2,1,0:T(8,128)(2,1)}), bf16[8,128,256]{2,1,0:T(8,128)(2,1)S(1)}, u32[]{:S(2)}, u32[]{:S(2)}) async-start(bf16[8,128,256]{2,1,0:T(8,128)(2,1)} %down.1), calls=%async_computation.4 | async-start | bytes 1048576 | tf_op jit(solution)/shard_map/all_to_all | solution.py:199
  145.6 14.0 %all-to-all-start.5 = ((bf16[8,32,256]{2,1,0:T(8,128)(2,1)}), bf16[8,32,256]{2,1,0:T(8,128)(2,1)S(1)}, u32[]{:S(2)}, u32[]{:S(2)}) async-start(bf16[8,32,256]{2,1,0:T(8,128)(2,1)} %gather_fusion.1), calls=%async_computation.5 | async-start | bytes 262144 | tf_op jit(solution)/shard_map/all_to_all | solution.py:199

commit v6 on v5

--- a/solution.py
+++ b/solution.py
@@ -16,10 +16,9 @@
 SQUARE = ("sec", "xlo")
 
 
-def prep_kernel(x_ref, out_ref, y_ref, sems):
+def prep_kernel(x_ref, y_ref):
     n, rows, w = x_ref.shape
     rows -= 8
-    copies = out_ref.shape[0]
     total = jnp.zeros((rows, w), F32)
     for z in range(n):
         x = x_ref[z, 0:rows, :].astype(F32)
@@ -34,25 +33,29 @@
     which = lax.broadcasted_iota(jnp.int32, (8, rows), 0)
     parts = jnp.where(which == 0, hi, jnp.where(which == 1, mid, jnp.where(which == 2, low, 0.0)))
     y_ref[n * rows : n * rows + 8, :] = jnp.concatenate([parts, jnp.zeros((8, w - rows), F32)], axis=1).astype(BF16)
-    sends = [pltpu.make_async_copy(y_ref, out_ref.at[j], sems.at[j]) for j in range(copies)]
-    for send in sends:
-        send.start()
-    for send in sends:
-        send.wait()
-
-
-def gate_up_kernel(x_ref, g0, u0, g1, u1, act_ref, w_ref, acc_ref, sems):
-    _, tall, w = x_ref.shape
+
+
+def gate_up_kernel(own, far, one, two, g0, u0, g1, u1, act_ref, w_ref, acc_ref, mid_ref, sems, mid_sems):
+    tall, w = own.shape
     n = HID
     rows = (tall - 8) // n
     deep, ff = g0.shape
     chunks = 4
     per = deep // chunks
+    sec, xlo, core = lax.axis_index("sec"), lax.axis_index("xlo"), lax.axis_index("core")
+    moves = [
+        pltpu.make_async_copy(one, mid_ref.at[core], mid_sems.at[0]),
+        pltpu.make_async_copy(two, mid_ref.at[1 - core], mid_sems.at[1]),
+    ]
+    for move in moves:
+        move.start()
+
+    def source(ref, c):
+        return ref.at[pl.ds(pl.multiple_of((sec ^ (c // 2)) * (deep // 2) + (c % 2) * per, per), per), :]
+
     loads = [
         [
-            pltpu.make_async_copy(
-                ref.at[c * per : (c + 1) * per, :], w_ref.at[i, c * per : (c + 1) * per, :], sems.at[c, i]
-            )
+            pltpu.make_async_copy(source(ref, c), w_ref.at[i, c * per : (c + 1) * per, :], sems.at[c, i])
             for i, ref in enumerate((g0, u0, g1, u1))
         ]
         for c in range(chunks)
@@ -60,19 +63,22 @@
     for group in loads:
         for load in group:
             load.start()
+    for move in moves:
+        move.wait()
+    pieces = ((own, mid_ref.at[0]), (mid_ref.at[1], far))
     scales = []
     for x in range(2):
-        parts = [x_ref[2 * s + x, n * rows : n * rows + 8, 0:rows].astype(F32) for s in range(2)]
+        parts = [pieces[s][x][n * rows : n * rows + 8, 0:rows].astype(F32) for s in range(2)]
         both = parts[0] + parts[1]
         total = both[0:1, :] + both[1:2, :] + both[2:3, :]
         inv = 1.0 / jnp.sqrt(total / deep + 1e-05)
         scales.append(jnp.transpose(jnp.broadcast_to(inv, (rows, rows))))
     for c in range(chunks):
-        pieces = range(c * per // w, (c + 1) * per // w)
+        first = c % 2 * per // w
         xs = jnp.concatenate(
             [
                 jnp.concatenate(
-                    [x_ref[2 * (p // n) + x, (p % n) * rows : (p % n + 1) * rows, :] for p in pieces], axis=1
+                    [pieces[c // 2][x][z * rows : (z + 1) * rows, :] for z in range(first, first + per // w)], axis=1
                 )
                 for x in range(2)
             ],
@@ -94,7 +100,7 @@
             up = block[:, ff:] * scales[x]
             act = (gate / (1.0 + jnp.exp(-gate)) * up).astype(BF16)
             for s in range(2):
-                act_ref[2 * s + x, :, k * ff : (k + 1) * ff] = act
+                act_ref[2 * s + (xlo ^ x), :, k * ff : (k + 1) * ff] = act
 
 
 def down_kernel(act_ref, *refs):
@@ -143,35 +149,35 @@
 
 def prepared(x):
     n, rows, w = x.shape
-    tall = n * (rows - 8) + 8
     return pl.pallas_call(
         prep_kernel,
-        out_shape=pltpu.HBM((4, tall, w), BF16),
+        out_shape=jax.ShapeDtypeStruct((n * (rows - 8) + 8, w), BF16),
         in_specs=[VM],
-        out_specs=HBM,
-        scratch_shapes=[pltpu.VMEM((tall, w), BF16), pltpu.SemaphoreType.DMA((4,))],
+        out_specs=VM,
         compiler_params=pltpu.CompilerParams(vmem_limit_bytes=4 << 20),
         name="prep",
     )(vm(x))
 
 
-def gated(x, weights):
-    _, tall, _ = x.shape
+def gated(own, far, one, two, weights):
+    tall, w = own.shape
     rows = (tall - 8) // HID
     deep, ff = weights[0].shape
     return pl.pallas_call(
         gate_up_kernel,
         out_shape=pltpu.HBM((4, rows, 2 * ff), BF16),
-        in_specs=[VM] + [HBM] * 4,
+        in_specs=[VM] * 2 + [HBM] * 6,
         out_specs=VM,
         scratch_shapes=[
             pltpu.VMEM((4, deep, ff), BF16),
             pltpu.VMEM((2, 2 * rows, 2 * ff), F32),
+            pltpu.VMEM((2, tall, w), BF16),
             pltpu.SemaphoreType.DMA((4, 4)),
+            pltpu.SemaphoreType.DMA((2,)),
         ],
         compiler_params=pltpu.CompilerParams(vmem_limit_bytes=16 << 20),
         name="gate_up",
-    )(vm(x), *[hbm(v) for v in weights])
+    )(vm(own), vm(far), *[hbm(v) for v in (one, two, *weights)])
 
 
 def lowered(act, downs):
@@ -203,6 +209,12 @@
     return jnp.sum(x.astype(F32), axis=0).astype(BF16)
 
 
+def turned(x, turn):
+    devices = [(place, core) for place in range(4) for core in range(2)]
+    pairs = [(p * 2 + c, (p ^ (1 if c == turn else 2)) * 2 + c) for p, c in devices]
+    return lax.ppermute(x, (*SQUARE, "core"), pairs)
+
+
 def layer(tokens, norm_gain, route_weight, block_experts, w_gate, w_up, w_down):
     rows, w = tokens.shape
     groups = lax.axis_size("group")
@@ -241,9 +253,11 @@
     downs = [d for piece in direct for d in (piece, swapped(piece))]
     picked = jnp.concatenate([picked, jnp.broadcast_to(norm_gain[None, :], (8, w))], axis=0)
     wide = exchange(jnp.broadcast_to(picked[None], (n_hid, tall + 8, w)), "hid")
-    ready = prepared(wide)
-    every = exchange(ready, SQUARE)
-    act = exchange(gated(every, (gate0, up0, gate1, up1)), SQUARE)
+    own = prepared(wide)
+    one = turned(own, 0)
+    two = turned(own, 1)
+    far = turned(one, 1)
+    act = exchange(gated(own, far, one, two, (gate0, up0, gate1, up1)), SQUARE)
     summed = added(exchange(lowered(act, downs), "hid")).reshape(MOST, rows, w)
     outgoing = jnp.take(summed, slot_of_block, axis=0, mode="clip")
     back = exchange(outgoing, GROUP)

time: 161 us -> 144 us (0.89)
  blocking collectives: 27 us -> 0 us
  starting transfers between devices: 47.4 us -> 61.8 us
  waiting for transfers between devices: 69.5 us -> 63.7 us
    all_to_all x1 -> x0, blocking collectives: 27 us -> none  [exchange(): return lax.all_to_all(x, axes, split_axis=0, concat_axis=0, tiled=True)]
    ppermute x3, waiting for transfers between devices: 26.9 us -> 14.8 us  [sent(): return lax.ppermute(x, SQUARE, [(i, i ^ flip) for i in range(4)])]
    ppermute x0 -> x3, starting transfers between devices: none -> 8.96 us  [turned(): return lax.ppermute(x, (*SQUARE, 'core'), pairs)]
    all_to_all x5, starting transfers between devices: 25.7 us -> 30.7 us  [exchange(): return lax.all_to_all(x, axes, split_axis=0, concat_axis=0, tiled=True)]
    all_to_all x5, waiting for transfers between devices: 42.6 us -> 47.3 us  [exchange(): return lax.all_to_all(x, axes, split_axis=0, concat_axis=0, tiled=True)]
    unnamed x6 -> x16, local copies, waits for them, and re-layouts: 0.01 us -> 1.95 us
  transfers between devices with their start and end apart: 14 -> 17, of which waited for: 6 -> 8; matrix products, arithmetic and copies ran while one was open for 2% -> 1% of each run, Pallas kernels for 2% -> 4%
where the time goes in v6:
time: 144 us; the launch traced here: 143 us
  waiting for transfers between devices  63.7 us (44%)
  starting transfers between devices  61.8 us (43%)
  Pallas kernels  8.58 us (6%)
  local copies, waits for them, and re-layouts  7.08 us (5%)
    all_to_all x5, waiting for transfers between devices, exchange(): return lax.all_to_all(x, axes, split_axis=0, concat_axis=0, tiled=True)  47.3 us
    all_to_all x5, starting transfers between devices, exchange(): return lax.all_to_all(x, axes, split_axis=0, concat_axis=0, tiled=True)  30.7 us
    ppermute x3, waiting for transfers between devices, sent(): return lax.ppermute(x, SQUARE, [(i, i ^ flip) for i in range(4)])  14.8 us
    ppermute x6, starting transfers between devices, swapped(): return lax.ppermute(x, 'core', [(0, 1), (1, 0)])  13 us
    ppermute x3, starting transfers between devices, sent(): return lax.ppermute(x, SQUARE, [(i, i ^ flip) for i in range(4)])  9.19 us
    ppermute x3, starting transfers between devices, turned(): return lax.ppermute(x, (*SQUARE, 'core'), pairs)  8.96 us
    pallas_call x1, Pallas kernels, gated(): pl.pallas_call(gate_up_kernel, out_shape=pltpu.HBM((4, rows, 2 * ff), BF1...  4.99 us
    pallas_call x1, Pallas kernels, lowered(): pl.pallas_call(down_kernel, out_shape=pltpu.HBM(shape, BF16), in_specs=[V...  3.35 us
  transfers between devices with their start and end apart: 17, of which 8 were waited for; matrix products, arithmetic and copies ran while one was open for 1% of the time, Pallas kernels for 4%

profile of v6, /device:TPU:8, one launch (start us, length us, event | category | flops | bytes accessed | tf_op | source)
XLA Modules:
  0.0 142.7 jit_solution(9184564763292234448)
XLA Ops:
  1.5 8.7 %all-to-all-start = ((bf16[8,32,256]{2,1,0:T(8,128)(2,1)}), bf16[8,32,256]{2,1,0:T(8,128)(2,1)S(1)}, u32[]{:S(2)}, u32[]{:S(2)}) async-start(bf16[8,32,256]{2,1,0:T(8,128)(2,1)} %broadcast_in_dim.48), calls=%async_computation | async-start | bytes 262144 | tf_op jit(solution)/shard_map/all_to_all | solution.py:205
  11.2 9.2 %all-to-all-done = bf16[8,32,256]{2,1,0:T(8,128)(2,1)S(1)} async-done(((bf16[8,32,256]{2,1,0:T(8,128)(2,1)}), bf16[8,32,256]{2,1,0:T(8,128)(2,1)S(1)}, u32[]{:S(2)}, u32[]{:S(2)}) %all-to-all-start) | async-done | bytes 131104 | tf_op jit(solution)/shard_map/all_to_all | solution.py:205
  22.5 10.4 %all-to-all-start.1 = ((bf16[8,136,256]{2,1,0:T(8,128)(2,1)}), bf16[8,136,256]{2,1,0:T(8,128)(2,1)S(1)}, u32[]{:S(2)}, u32[]{:S(2)}) async-start(bf16[8,136,256]{2,1,0:T(8,128)(2,1)} %broadcast_in_dim.74), calls=%async_computation.1 | async-start | bytes 1114112 | tf_op jit(solution)/shard_map/all_to_all | solution.py:205
  33.8 3.3 %collective-permute-start.10 = (bf16[128,2048]{1,0:T(8,128)(2,1)}, bf16[128,2048]{1,0:T(8,128)(2,1)}, u32[]{:S(2)}, u32[]{:S(2)}) collective-permute-start(bf16[128,2048]{1,0:T(8,128)(2,1)} %dynamic-slice_bitcast_fusion), channel_id=1, source_target_pairs={{0,272},{16,256},{256,16},{272,0},{1,273},{17,257},{257,17},{273,1... | collective-permute-start | bytes 1572872 | tf_op jit(solution)/shard_map/ppermute | solution.py:229
  37.0 2.6 %collective-permute-start.8 = (bf16[128,2048]{1,0:T(8,128)(2,1)}, bf16[128,2048]{1,0:T(8,128)(2,1)}, u32[]{:S(2)}, u32[]{:S(2)}) collective-permute-start(bf16[128,2048]{1,0:T(8,128)(2,1)} %dynamic-slice_bitcast_fusion), channel_id=1, source_target_pairs={{0,256},{16,272},{256,0},{272,16},{1,257},{17,273},{257,1},{273,17... | collective-permute-start | bytes 1572872 | tf_op jit(solution)/shard_map/ppermute | solution.py:229
  39.7 1.9 %collective-permute-start.3 = (bf16[4096,128]{1,0:T(8,128)(2,1)S(1)}, bf16[4096,128]{1,0:T(8,128)(2,1)}, u32[]{:S(2)}, u32[]{:S(2)}) collective-permute-start(bf16[4096,128]{1,0:T(8,128)(2,1)S(1)} %bitcast.13), channel_id=1, source_target_pairs={{0,8},{8,0},{1,9},{9,1},{2,10},{10,2},{3,11},{11,3},{4,12},{12,4},... | collective-permute-start | bytes 3145736 | tf_op jit(solution)/shard_map/ppermute | solution.py:232
  41.6 2.4 %collective-permute-start.4 = (bf16[4096,128]{1,0:T(8,128)(2,1)}, bf16[4096,128]{1,0:T(8,128)(2,1)}, u32[]{:S(2)}, u32[]{:S(2)}) collective-permute-start(bf16[4096,128]{1,0:T(8,128)(2,1)} %bitcast.5.u0), channel_id=1, source_target_pairs={{0,8},{8,0},{1,9},{9,1},{2,10},{10,2},{3,11},{11,3},{4,12},{12,4},... | collective-permute-start | bytes 3145736 | tf_op jit(solution)/shard_map/ppermute | solution.py:232
  44.0 5.8 %all-to-all-done.1.x_ref = bf16[8,136,256]{2,1,0:T(8,128)(2,1)S(1)} async-done(((bf16[8,136,256]{2,1,0:T(8,128)(2,1)}), bf16[8,136,256]{2,1,0:T(8,128)(2,1)S(1)}, u32[]{:S(2)}, u32[]{:S(2)}) %all-to-all-start.1) | async-done | bytes 557088 | tf_op jit(solution)/shard_map/all_to_all | solution.py:205
  50.1 2.5 %collective-permute-start = (bf16[1032,256]{1,0:T(8,128)(2,1)S(1)}, bf16[1032,256]{1,0:T(8,128)(2,1)}, u32[]{:S(2)}, u32[]{:S(2)}) collective-permute-start(bf16[1032,256]{1,0:T(8,128)(2,1)S(1)} %prep.1.own), channel_id=1, source_target_pairs={{0,16},{8,264},{16,0},{24,280},{256,272},{264,8},{272,256},{280,24... | collective-permute-start | bytes 1585160 | tf_op jit(solution)/shard_map/ppermute | solution.py:215
  52.6 3.2 %collective-permute-start.2 = (bf16[1032,256]{1,0:T(8,128)(2,1)S(1)}, bf16[1032,256]{1,0:T(8,128)(2,1)S(1)}, u32[]{:S(2)}, u32[]{:S(2)}) collective-permute-start(bf16[1032,256]{1,0:T(8,128)(2,1)S(1)} %prep.1.own), channel_id=1, source_target_pairs={{0,256},{8,24},{16,272},{24,8},{256,0},{264,280},{272,16},{280,264... | collective-permute-start | bytes 1585160 | tf_op jit(solution)/shard_map/ppermute | solution.py:215
  55.9 6.1 %collective-permute-done.8.refs_4_ = bf16[128,2048]{1,0:T(8,128)(2,1)} collective-permute-done((bf16[128,2048]{1,0:T(8,128)(2,1)}, bf16[128,2048]{1,0:T(8,128)(2,1)}, u32[]{:S(2)}, u32[]{:S(2)}) %collective-permute-start.8) | collective-permute-done | bytes 524320 | tf_op jit(solution)/shard_map/ppermute | solution.py:229
  62.0 3.3 %collective-permute-start.6 = (bf16[128,2048]{1,0:T(8,128)(2,1)S(1)}, bf16[128,2048]{1,0:T(8,128)(2,1)}, u32[]{:S(2)}, u32[]{:S(2)}) collective-permute-start(bf16[128,2048]{1,0:T(8,128)(2,1)S(1)} %constant_dynamic-slice_fusion.refs_0_), channel_id=1, source_target_pairs={{0,16},{16,0},{256,272},{272,256},{1,17},{17,1},{257,273},{273,257... | collective-permute-start | bytes 1572872 | tf_op jit(solution)/shard_map/ppermute | solution.py:229
  67.0 3.2 %collective-permute-start.1 = (bf16[1032,256]{1,0:T(8,128)(2,1)}, bf16[1032,256]{1,0:T(8,128)(2,1)S(1)}, u32[]{:S(2)}, u32[]{:S(2)}) collective-permute-start(bf16[1032,256]{1,0:T(8,128)(2,1)} %collective-permute-done.one), channel_id=1, source_target_pairs={{0,256},{8,24},{16,272},{24,8},{256,0},{264,280},{272,16},{280,264... | collective-permute-start | bytes 1585160 | tf_op jit(solution)/shard_map/ppermute | solution.py:215
  70.2 8.6 %collective-permute-done.6.refs_2_ = bf16[128,2048]{1,0:T(8,128)(2,1)} collective-permute-done((bf16[128,2048]{1,0:T(8,128)(2,1)S(1)}, bf16[128,2048]{1,0:T(8,128)(2,1)}, u32[]{:S(2)}, u32[]{:S(2)}) %collective-permute-start.6) | collective-permute-done | bytes 524320 | tf_op jit(solution)/shard_map/ppermute | solution.py:229
  80.7 2.4 %collective-permute-start.11 = (bf16[128,2048]{1,0:T(8,128)(2,1)}, bf16[128,2048]{1,0:T(8,128)(2,1)S(1)}, u32[]{:S(2)}, u32[]{:S(2)}) collective-permute-start(bf16[128,2048]{1,0:T(8,128)(2,1)} %collective-permute-done.10.refs_6_), channel_id=1, source_target_pairs={{0,8},{8,0},{1,9},{9,1},{2,10},{10,2},{3,11},{11,3},{4,12},{12,4},... | collective-permute-start | bytes 1572872 | tf_op jit(solution)/shard_map/ppermute | solution.py:232
  85.1 2.4 %collective-permute-start.7 = (bf16[128,2048]{1,0:T(8,128)(2,1)}, bf16[128,2048]{1,0:T(8,128)(2,1)}, u32[]{:S(2)}, u32[]{:S(2)}) collective-permute-start(bf16[128,2048]{1,0:T(8,128)(2,1)} %collective-permute-done.6.refs_2_), channel_id=1, source_target_pairs={{0,8},{8,0},{1,9},{9,1},{2,10},{10,2},{3,11},{11,3},{4,12},{12,4},... | collective-permute-start | bytes 1572872 | tf_op jit(solution)/shard_map/ppermute | solution.py:232
  87.6 5.0 %gate_up.1 = bf16[4,128,256]{2,1,0:T(8,128)(2,1)} custom-call(bf16[1032,256]{1,0:T(8,128)(2,1)S(1)} %prep.1.own, bf16[1032,256]{1,0:T(8,128)(2,1)S(1)} %collective-permute-done.1.far, bf16[1032,256]{1,0:T(8,128)(2,1)} %collective-permute-done.one, bf16[1032,256]{1,0:T(8,128)(2,1)} %copy-done.3, bf16[4096,128]{1,0:T(8,128)(2,1)} %bitcast.12, ...), custom_call_target="tpu_custom_call" | custom-call | tf_op jit(solution)/shard_map/gate_up/pallas_call | solution.py:166
  92.6 4.7 %all-to-all-start.2 = ((bf16[4,128,256]{2,1,0:T(8,128)(2,1)}), bf16[4,128,256]{2,1,0:T(8,128)(2,1)S(1)}, u32[]{:S(2)}, u32[]{:S(2)}) async-start(bf16[4,128,256]{2,1,0:T(8,128)(2,1)} %gate_up.1), calls=%async_computation.2 | async-start | bytes 524288 | tf_op jit(solution)/shard_map/all_to_all | solution.py:205
  97.3 5.0 %all-to-all-done.2.act_ref = bf16[4,128,256]{2,1,0:T(8,128)(2,1)S(1)} async-done(((bf16[4,128,256]{2,1,0:T(8,128)(2,1)}), bf16[4,128,256]{2,1,0:T(8,128)(2,1)S(1)}, u32[]{:S(2)}, u32[]{:S(2)}) %all-to-all-start.2) | async-done | bytes 262176 | tf_op jit(solution)/shard_map/all_to_all | solution.py:205
  102.4 3.3 %down.1 = bf16[8,128,256]{2,1,0:T(8,128)(2,1)} custom-call(bf16[4,128,256]{2,1,0:T(8,128)(2,1)S(1)} %all-to-all-done.2.act_ref, bf16[128,2048]{1,0:T(8,128)(2,1)} %copy-done.1, bf16[128,2048]{1,0:T(8,128)(2,1)} %collective-permute-done.5.refs_1_, bf16[128,2048]{1,0:T(8,128)(2,1)} %collective-permute-done.6.refs_2_, ...), custom_call_target="tpu_custom_call" | custom-call | tf_op jit(solution)/shard_map/down/pallas_call | solution.py:187
  105.7 3.5 %all-to-all-start.3 = ((bf16[8,128,256]{2,1,0:T(8,128)(2,1)}), bf16[8,128,256]{2,1,0:T(8,128)(2,1)S(1)}, u32[]{:S(2)}, u32[]{:S(2)}) async-start(bf16[8,128,256]{2,1,0:T(8,128)(2,1)} %down.1), calls=%async_computation.3 | async-start | bytes 1048576 | tf_op jit(solution)/shard_map/all_to_all | solution.py:205
  109.4 17.5 %all-to-all-done.3 = bf16[8,128,256]{2,1,0:T(8,128)(2,1)S(1)} async-done(((bf16[8,128,256]{2,1,0:T(8,128)(2,1)}), bf16[8,128,256]{2,1,0:T(8,128)(2,1)S(1)}, u32[]{:S(2)}, u32[]{:S(2)}) %all-to-all-start.3) | async-done | bytes 524320 | tf_op jit(solution)/shard_map/all_to_all | solution.py:205
  128.2 3.4 %all-to-all-start.4 = ((bf16[8,32,256]{2,1,0:T(8,128)(2,1)}), bf16[8,32,256]{2,1,0:T(8,128)(2,1)S(1)}, u32[]{:S(2)}, u32[]{:S(2)}) async-start(bf16[8,32,256]{2,1,0:T(8,128)(2,1)} %gather_fusion.1), calls=%async_computation.4 | async-start | bytes 262144 | tf_op jit(solution)/shard_map/all_to_all | solution.py:205
  132.3 9.7 %all-to-all-done.4 = bf16[8,32,256]{2,1,0:T(8,128)(2,1)S(1)} async-done(((bf16[8,32,256]{2,1,0:T(8,128)(2,1)}), bf16[8,32,256]{2,1,0:T(8,128)(2,1)S(1)}, u32[]{:S(2)}, u32[]{:S(2)}) %all-to-all-start.4) | async-done | bytes 131104 | tf_op jit(solution)/shard_map/all_to_all | solution.py:205
  (49 shorter events, 14.1 us)
Async XLA Ops:
  0.0 20.9 %copy-start = (bf16[1,128,4096]{2,1,0:T(8,128)(2,1)S(1)}, bf16[1,128,4096]{2,1,0:T(8,128)(2,1)}, u32[]{:S(2)}) copy-start(bf16[1,128,4096]{2,1,0:T(8,128)(2,1)} %param.13) | copy-start | bytes 3145732
  1.5 18.9 %all-to-all-start = ((bf16[8,32,256]{2,1,0:T(8,128)(2,1)}), bf16[8,32,256]{2,1,0:T(8,128)(2,1)S(1)}, u32[]{:S(2)}, u32[]{:S(2)}) async-start(bf16[8,32,256]{2,1,0:T(8,128)(2,1)} %broadcast_in_dim.48), calls=%async_computation | async-start | bytes 262144 | tf_op jit(solution)/shard_map/all_to_all | solution.py:205
  10.1 0.7 copy-start.5
  22.5 17.2 %copy-start.2 = (bf16[1,4096,128]{2,1,0:T(8,128)(2,1)S(1)}, bf16[1,4096,128]{2,1,0:T(8,128)(2,1)}, u32[]{:S(2)}) copy-start(bf16[1,4096,128]{2,1,0:T(8,128)(2,1)} %param.11) | copy-start | bytes 3145732
  22.5 27.3 %all-to-all-start.1 = ((bf16[8,136,256]{2,1,0:T(8,128)(2,1)}), bf16[8,136,256]{2,1,0:T(8,128)(2,1)S(1)}, u32[]{:S(2)}, u32[]{:S(2)}) async-start(bf16[8,136,256]{2,1,0:T(8,128)(2,1)} %broadcast_in_dim.74), calls=%async_computation.1 | async-start | bytes 1114112 | tf_op jit(solution)/shard_map/all_to_all | solution.py:205
  33.8 18.8 %collective-permute-start.10 = (bf16[128,2048]{1,0:T(8,128)(2,1)}, bf16[128,2048]{1,0:T(8,128)(2,1)}, u32[]{:S(2)}, u32[]{:S(2)}) collective-permute-start(bf16[128,2048]{1,0:T(8,128)(2,1)} %dynamic-slice_bitcast_fusion), channel_id=1, source_target_pairs={{0,272},{16,256},{256,16},{272,0},{1,273},{17,257},{257,17},{273,1... | collective-permute-start | bytes 1572872 | tf_op jit(solution)/shard_map/ppermute | solution.py:229
  37.0 25.0 %collective-permute-start.8 = (bf16[128,2048]{1,0:T(8,128)(2,1)}, bf16[128,2048]{1,0:T(8,128)(2,1)}, u32[]{:S(2)}, u32[]{:S(2)}) collective-permute-start(bf16[128,2048]{1,0:T(8,128)(2,1)} %dynamic-slice_bitcast_fusion), channel_id=1, source_target_pairs={{0,256},{16,272},{256,0},{272,16},{1,257},{17,273},{257,1},{273,17... | collective-permute-start | bytes 1572872 | tf_op jit(solution)/shard_map/ppermute | solution.py:229
  39.7 41.1 %collective-permute-start.3 = (bf16[4096,128]{1,0:T(8,128)(2,1)S(1)}, bf16[4096,128]{1,0:T(8,128)(2,1)}, u32[]{:S(2)}, u32[]{:S(2)}) collective-permute-start(bf16[4096,128]{1,0:T(8,128)(2,1)S(1)} %bitcast.13), channel_id=1, source_target_pairs={{0,8},{8,0},{1,9},{9,1},{2,10},{10,2},{3,11},{11,3},{4,12},{12,4},... | collective-permute-start | bytes 3145736 | tf_op jit(solution)/shard_map/ppermute | solution.py:232
  41.6 41.6 %collective-permute-start.4 = (bf16[4096,128]{1,0:T(8,128)(2,1)}, bf16[4096,128]{1,0:T(8,128)(2,1)}, u32[]{:S(2)}, u32[]{:S(2)}) collective-permute-start(bf16[4096,128]{1,0:T(8,128)(2,1)} %bitcast.5.u0), channel_id=1, source_target_pairs={{0,8},{8,0},{1,9},{9,1},{2,10},{10,2},{3,11},{11,3},{4,12},{12,4},... | collective-permute-start | bytes 3145736 | tf_op jit(solution)/shard_map/ppermute | solution.py:232
  50.1 16.9 %collective-permute-start = (bf16[1032,256]{1,0:T(8,128)(2,1)S(1)}, bf16[1032,256]{1,0:T(8,128)(2,1)}, u32[]{:S(2)}, u32[]{:S(2)}) collective-permute-start(bf16[1032,256]{1,0:T(8,128)(2,1)S(1)} %prep.1.own), channel_id=1, source_target_pairs={{0,16},{8,264},{16,0},{24,280},{256,272},{264,8},{272,256},{280,24... | collective-permute-start | bytes 1585160 | tf_op jit(solution)/shard_map/ppermute | solution.py:215
  52.6 32.5 %collective-permute-start.2 = (bf16[1032,256]{1,0:T(8,128)(2,1)S(1)}, bf16[1032,256]{1,0:T(8,128)(2,1)S(1)}, u32[]{:S(2)}, u32[]{:S(2)}) collective-permute-start(bf16[1032,256]{1,0:T(8,128)(2,1)S(1)} %prep.1.own), channel_id=1, source_target_pairs={{0,256},{8,24},{16,272},{24,8},{256,0},{264,280},{272,16},{280,264... | collective-permute-start | bytes 1585160 | tf_op jit(solution)/shard_map/ppermute | solution.py:215
  55.9 36.7 %copy-start.1 = (bf16[128,2048]{1,0:T(8,128)(2,1)}, bf16[128,2048]{1,0:T(8,128)(2,1)S(1)}, u32[]{:S(2)}) copy-start(bf16[128,2048]{1,0:T(8,128)(2,1)S(1)} %constant_dynamic-slice_fusion.refs_0_) | copy-start | bytes 1572868
  62.0 16.8 %collective-permute-start.6 = (bf16[128,2048]{1,0:T(8,128)(2,1)S(1)}, bf16[128,2048]{1,0:T(8,128)(2,1)}, u32[]{:S(2)}, u32[]{:S(2)}) collective-permute-start(bf16[128,2048]{1,0:T(8,128)(2,1)S(1)} %constant_dynamic-slice_fusion.refs_0_), channel_id=1, source_target_pairs={{0,16},{16,0},{256,272},{272,256},{1,17},{17,1},{257,273},{273,257... | collective-permute-start | bytes 1572872 | tf_op jit(solution)/shard_map/ppermute | solution.py:229
  67.0 20.6 %collective-permute-start.1 = (bf16[1032,256]{1,0:T(8,128)(2,1)}, bf16[1032,256]{1,0:T(8,128)(2,1)S(1)}, u32[]{:S(2)}, u32[]{:S(2)}) collective-permute-start(bf16[1032,256]{1,0:T(8,128)(2,1)} %collective-permute-done.one), channel_id=1, source_target_pairs={{0,256},{8,24},{16,272},{24,8},{256,0},{264,280},{272,16},{280,264... | collective-permute-start | bytes 1585160 | tf_op jit(solution)/shard_map/ppermute | solution.py:215
  78.8 18.5 %collective-permute-start.5 = (bf16[128,2048]{1,0:T(8,128)(2,1)S(1)}, bf16[128,2048]{1,0:T(8,128)(2,1)}, u32[]{:S(2)}, u32[]{:S(2)}) collective-permute-start(bf16[128,2048]{1,0:T(8,128)(2,1)S(1)} %constant_dynamic-slice_fusion.refs_0_), channel_id=1, source_target_pairs={{0,8},{8,0},{1,9},{9,1},{2,10},{10,2},{3,11},{11,3},{4,12},{12,4},... | collective-permute-start | bytes 1572872 | tf_op jit(solution)/shard_map/ppermute | solution.py:232
  80.7 16.6 %collective-permute-start.11 = (bf16[128,2048]{1,0:T(8,128)(2,1)}, bf16[128,2048]{1,0:T(8,128)(2,1)S(1)}, u32[]{:S(2)}, u32[]{:S(2)}) collective-permute-start(bf16[128,2048]{1,0:T(8,128)(2,1)} %collective-permute-done.10.refs_6_), channel_id=1, source_target_pairs={{0,8},{8,0},{1,9},{9,1},{2,10},{10,2},{3,11},{11,3},{4,12},{12,4},... | collective-permute-start | bytes 1572872 | tf_op jit(solution)/shard_map/ppermute | solution.py:232
  83.2 14.1 %collective-permute-start.9 = (bf16[128,2048]{1,0:T(8,128)(2,1)}, bf16[128,2048]{1,0:T(8,128)(2,1)}, u32[]{:S(2)}, u32[]{:S(2)}) collective-permute-start(bf16[128,2048]{1,0:T(8,128)(2,1)} %collective-permute-done.8.refs_4_), channel_id=1, source_target_pairs={{0,8},{8,0},{1,9},{9,1},{2,10},{10,2},{3,11},{11,3},{4,12},{12,4},... | collective-permute-start | bytes 1572872 | tf_op jit(solution)/shard_map/ppermute | solution.py:232
  85.1 2.4 %copy-start.3 = (bf16[1032,256]{1,0:T(8,128)(2,1)}, bf16[1032,256]{1,0:T(8,128)(2,1)S(1)}, u32[]{:S(2)}) copy-start(bf16[1032,256]{1,0:T(8,128)(2,1)S(1)} %collective-permute-done.2.two) | copy-start | bytes 1585156
  85.1 12.2 %collective-permute-start.7 = (bf16[128,2048]{1,0:T(8,128)(2,1)}, bf16[128,2048]{1,0:T(8,128)(2,1)}, u32[]{:S(2)}, u32[]{:S(2)}) collective-permute-start(bf16[128,2048]{1,0:T(8,128)(2,1)} %collective-permute-done.6.refs_2_), channel_id=1, source_target_pairs={{0,8},{8,0},{1,9},{9,1},{2,10},{10,2},{3,11},{11,3},{4,12},{12,4},... | collective-permute-start | bytes 1572872 | tf_op jit(solution)/shard_map/ppermute | solution.py:232
  92.6 9.8 %all-to-all-start.2 = ((bf16[4,128,256]{2,1,0:T(8,128)(2,1)}), bf16[4,128,256]{2,1,0:T(8,128)(2,1)S(1)}, u32[]{:S(2)}, u32[]{:S(2)}) async-start(bf16[4,128,256]{2,1,0:T(8,128)(2,1)} %gate_up.1), calls=%async_computation.2 | async-start | bytes 524288 | tf_op jit(solution)/shard_map/all_to_all | solution.py:205
  97.3 5.1 %copy-start.4 = (bf16[128,2048]{1,0:T(8,128)(2,1)}, bf16[128,2048]{1,0:T(8,128)(2,1)S(1)}, u32[]{:S(2)}) copy-start(bf16[128,2048]{1,0:T(8,128)(2,1)S(1)} %collective-permute-done.11.refs_7_) | copy-start | bytes 1572868
  105.7 21.2 %all-to-all-start.3 = ((bf16[8,128,256]{2,1,0:T(8,128)(2,1)}), bf16[8,128,256]{2,1,0:T(8,128)(2,1)S(1)}, u32[]{:S(2)}, u32[]{:S(2)}) async-start(bf16[8,128,256]{2,1,0:T(8,128)(2,1)} %down.1), calls=%async_computation.3 | async-start | bytes 1048576 | tf_op jit(solution)/shard_map/all_to_all | solution.py:205
  128.2 13.8 %all-to-all-start.4 = ((bf16[8,32,256]{2,1,0:T(8,128)(2,1)}), bf16[8,32,256]{2,1,0:T(8,128)(2,1)S(1)}, u32[]{:S(2)}, u32[]{:S(2)}) async-start(bf16[8,32,256]{2,1,0:T(8,128)(2,1)} %gather_fusion.1), calls=%async_computation.4 | async-start | bytes 262144 | tf_op jit(solution)/shard_map/all_to_all | solution.py:205
  131.6 0.7 copy-start.6
  (1 other events, 0.7 us)

commit v7 on v5

--- a/solution.py
+++ b/solution.py
@@ -129,6 +129,46 @@
         send.wait()
 
 
+def routed(experts_ref, me):
+    count = jnp.int32(0)
+    block_of_slot = [jnp.int32(0)] * MOST
+    slot_of_block = []
+    for b in range(experts_ref.shape[1]):
+        hit = (experts_ref[0, b] == me) | (experts_ref[1, b] == me)
+        block_of_slot = [jnp.where(hit & (count == k), b, old) for k, old in enumerate(block_of_slot)]
+        slot_of_block.append(jnp.minimum(count, MOST - 1))
+        count = count + jnp.where(hit, 1, 0)
+    return block_of_slot, slot_of_block
+
+
+def sent_all(sends):
+    for send in sends:
+        send.start()
+    for send in sends:
+        send.wait()
+
+
+def pick_kernel(experts_ref, x_ref, gain_ref, out_ref, y_ref, sems):
+    _, rows, w = x_ref.shape
+    block_of_slot, _ = routed(experts_ref, lax.axis_index("group"))
+    for k, block in enumerate(block_of_slot):
+        y_ref[k * rows : (k + 1) * rows, :] = x_ref[block]
+    y_ref[MOST * rows :, :] = jnp.broadcast_to(gain_ref[...].astype(F32), (8, w)).astype(BF16)
+    sent_all([pltpu.make_async_copy(y_ref, out_ref.at[j], sems.at[j]) for j in range(out_ref.shape[0])])
+
+
+def home_kernel(experts_ref, x_ref, out_ref, y_ref, sems):
+    blocks, rows, _ = out_ref.shape
+    _, slot_of_block = routed(experts_ref, lax.axis_index("group"))
+    for k in range(MOST):
+        total = x_ref[0, k * rows : (k + 1) * rows, :].astype(F32)
+        for z in range(1, x_ref.shape[0]):
+            total = total + x_ref[z, k * rows : (k + 1) * rows, :].astype(F32)
+        y_ref[k] = total.astype(BF16)
+    sent_all([pltpu.make_async_copy(y_ref.at[slot_of_block[b]], out_ref.at[b], sems.at[b]) for b in range(blocks)])
+
+
+SM = pl.BlockSpec(memory_space=pltpu.SMEM)
 VM = pl.BlockSpec(memory_space=pltpu.VMEM)
 HBM = pl.BlockSpec(memory_space=pltpu.HBM)
 
@@ -195,19 +235,41 @@
     )(vm(act), *[hbm(v) for v in downs])
 
 
+def picked_rows(block_experts, blocks, norm_gain, copies):
+    _, rows, w = blocks.shape
+    tall = MOST * rows + 8
+    return pl.pallas_call(
+        pick_kernel,
+        out_shape=pltpu.HBM((copies, tall, w), BF16),
+        in_specs=[SM, VM, VM],
+        out_specs=HBM,
+        scratch_shapes=[pltpu.VMEM((tall, w), BF16), pltpu.SemaphoreType.DMA((copies,))],
+        compiler_params=pltpu.CompilerParams(vmem_limit_bytes=1 << 20),
+    )(block_experts.T, vm(blocks), norm_gain[None, :])
+
+
+def homed(block_experts, parts):
+    _, tall, w = parts.shape
+    shape = (block_experts.shape[0], tall // MOST, w)
+    return pl.pallas_call(
+        home_kernel,
+        out_shape=pltpu.HBM(shape, BF16),
+        in_specs=[SM, VM],
+        out_specs=HBM,
+        scratch_shapes=[pltpu.VMEM((MOST, *shape[1:]), BF16), pltpu.SemaphoreType.DMA((shape[0],))],
+        compiler_params=pltpu.CompilerParams(vmem_limit_bytes=2 << 20),
+        name="home",
+    )(block_experts.T, vm(parts))
+
+
 def exchange(x, axes):
     return lax.all_to_all(x, axes, split_axis=0, concat_axis=0, tiled=True)
-
-
-def added(x):
-    return jnp.sum(x.astype(F32), axis=0).astype(BF16)
 
 
 def layer(tokens, norm_gain, route_weight, block_experts, w_gate, w_up, w_down):
     rows, w = tokens.shape
     groups = lax.axis_size("group")
     n_hid = lax.axis_size("hid")
-    me = lax.axis_index("group")
     gate0, up0, down0 = w_gate[0], w_up[0], w_down[0]
     sec = lax.axis_index("sec")
     part = down0.shape[1] // 2
@@ -222,31 +284,21 @@
     away_x = sent(down_away, 3)
     gate1, up1 = swapped(gate0), swapped(up0)
 
-    hit = jnp.any(block_experts == me, axis=1)
-    slot_of_block = jnp.maximum(jnp.cumsum(hit.astype(jnp.int32)) - 1, 0)
-    slot_ids = jnp.arange(MOST, dtype=jnp.int32)
-    match = (slot_of_block[None, :] == slot_ids[:, None]) & hit[None, :]
-    block_of_slot = jnp.sum(jnp.where(match, jnp.arange(groups, dtype=jnp.int32)[None, :], 0), axis=1)
-
-    mine = jnp.take(block_experts, me, axis=0, mode="clip")
+    mine = jnp.take(block_experts, lax.axis_index("group"), axis=0, mode="clip")
     named = mine[None, :] == jnp.arange(EXPERTS, dtype=jnp.int32)[:, None]
     factor = jnp.sum(jnp.where(named[:, None, :], route_weight[None], 0.0), axis=2)
 
     blocks = exchange(jnp.broadcast_to(tokens[None], (groups, rows, w)), GROUP)
-    tall = MOST * rows
-    picked = jnp.take(blocks, block_of_slot, axis=0, mode="clip").reshape(tall, w)
-    picked, down_late = lax.optimization_barrier((picked, down0))
+    wide = picked_rows(block_experts, blocks, norm_gain, n_hid)
+    blocks, down_late = lax.optimization_barrier((blocks, down0))
     down_here = lax.dynamic_slice_in_dim(down_late, sec * part, part, 1)
     direct = [down_here, sent(down_here, 1), sent(down_away, 2), away_x]
     downs = [d for piece in direct for d in (piece, swapped(piece))]
-    picked = jnp.concatenate([picked, jnp.broadcast_to(norm_gain[None, :], (8, w))], axis=0)
-    wide = exchange(jnp.broadcast_to(picked[None], (n_hid, tall + 8, w)), "hid")
+    wide = exchange(wide, "hid")
     ready = prepared(wide)
     every = exchange(ready, SQUARE)
     act = exchange(gated(every, (gate0, up0, gate1, up1)), SQUARE)
-    summed = added(exchange(lowered(act, downs), "hid")).reshape(MOST, rows, w)
-    outgoing = jnp.take(summed, slot_of_block, axis=0, mode="clip")
-    back = exchange(outgoing, GROUP)
+    back = exchange(homed(block_experts, exchange(lowered(act, downs), "hid")), GROUP)
     return jnp.sum(back.astype(F32) * factor[:, :, None], axis=0).astype(BF16)
 
 

time: 161 us -> 162 us (level)
  Pallas kernels: 8.56 us -> 11.4 us
    pallas_call x0 -> x2, Pallas kernels: none -> 2.81 us  [the longest x1 1.48 us: picked_rows(): pl.pallas_call(pick_kernel, out_shape=pltpu.HBM((copies, tall, w), BF16),...]
    gather x3 -> x1, local copies, waits for them, and re-layouts: 1.93 us -> 0.18 us  [layer(): mine = jnp.take(block_experts, lax.axis_index('group'), axis=0, mode='clip')]
where the time goes in v7:
time: 162 us
  waiting for transfers between devices  69.8 us (43%)
  starting transfers between devices  47.4 us (29%)
  blocking collectives  27.2 us (17%)
  Pallas kernels  11.4 us (7%)
  local copies, waits for them, and re-layouts  4.69 us (3%)
    all_to_all x5, waiting for transfers between devices, exchange(): return lax.all_to_all(x, axes, split_axis=0, concat_axis=0, tiled=True)  42.9 us
    all_to_all x1, blocking collectives, exchange(): return lax.all_to_all(x, axes, split_axis=0, concat_axis=0, tiled=True)  27.2 us
    ppermute x3, waiting for transfers between devices, sent(): return lax.ppermute(x, SQUARE, [(i, i ^ flip) for i in range(4)])  26.9 us
    all_to_all x5, starting transfers between devices, exchange(): return lax.all_to_all(x, axes, split_axis=0, concat_axis=0, tiled=True)  25.7 us
    ppermute x6, starting transfers between devices, swapped(): return lax.ppermute(x, 'core', [(0, 1), (1, 0)])  12.5 us
    ppermute x3, starting transfers between devices, sent(): return lax.ppermute(x, SQUARE, [(i, i ^ flip) for i in range(4)])  9.19 us
    pallas_call x1, Pallas kernels, gated(): pl.pallas_call(gate_up_kernel, out_shape=pltpu.HBM((4, rows, 2 * ff), BF1...  3.59 us
    pallas_call x1, Pallas kernels, lowered(): pl.pallas_call(down_kernel, out_shape=pltpu.HBM(shape, BF16), in_specs=[V...  3.34 us
  transfers between devices with their start and end apart: 14, of which 6 were waited for; matrix products, arithmetic and copies ran while one was open for 2% of the time, Pallas kernels for 2%

profile of v7, /device:TPU:8, one launch (start us, length us, event | category | flops | bytes accessed | tf_op | source)
XLA Modules:
  0.0 161.6 jit_solution(7353052184357014465)
XLA Ops:
  1.5 8.7 %all-to-all-start = ((bf16[8,32,256]{2,1,0:T(8,128)(2,1)}), bf16[8,32,256]{2,1,0:T(8,128)(2,1)S(1)}, u32[]{:S(2)}, u32[]{:S(2)}) async-start(bf16[8,32,256]{2,1,0:T(8,128)(2,1)} %broadcast_in_dim.38), calls=%async_computation | async-start | bytes 262144 | tf_op jit(solution)/shard_map/all_to_all | solution.py:266
  10.8 9.6 %all-to-all-done.x_ref = bf16[8,32,256]{2,1,0:T(8,128)(2,1)S(1)} async-done(((bf16[8,32,256]{2,1,0:T(8,128)(2,1)}), bf16[8,32,256]{2,1,0:T(8,128)(2,1)S(1)}, u32[]{:S(2)}, u32[]{:S(2)}) %all-to-all-start) | async-done | bytes 131104 | tf_op jit(solution)/shard_map/all_to_all | solution.py:266
  22.6 27.2 %all_to_all.30.x_ref = bf16[8,136,256]{2,1,0:T(8,128)(2,1)S(1)} all-to-all(bf16[8,136,256]{2,1,0:T(8,128)(2,1)} %shard_map.73), channel_id=1, replica_groups=mesh['sec'=2,'group'=8,'xlo'=2,'core'=2,'hid'=8] {'hid'}, dimensions={0} | all-to-all | bytes 1114112 | tf_op jit(solution)/shard_map/all_to_all | solution.py:266
  49.8 1.6 %prep.1 = bf16[4,1032,256]{2,1,0:T(8,128)(2,1)} custom-call(bf16[8,136,256]{2,1,0:T(8,128)(2,1)S(1)} %all_to_all.30.x_ref), custom_call_target="tpu_custom_call" | custom-call | tf_op jit(solution)/shard_map/prep/pallas_call | solution.py:187
  51.4 4.9 %all-to-all-start.2 = ((bf16[4,1032,256]{2,1,0:T(8,128)(2,1)}), bf16[4,1032,256]{2,1,0:T(8,128)(2,1)S(1)}, u32[]{:S(2)}, u32[]{:S(2)}) async-start(bf16[4,1032,256]{2,1,0:T(8,128)(2,1)} %prep.1), calls=%async_computation.2 | async-start | bytes 4227072 | tf_op jit(solution)/shard_map/all_to_all | solution.py:266
  56.3 1.9 %collective-permute-start = (bf16[4096,128]{1,0:T(8,128)(2,1)}, bf16[4096,128]{1,0:T(8,128)(2,1)}, u32[]{:S(2)}, u32[]{:S(2)}) collective-permute-start(bf16[4096,128]{1,0:T(8,128)(2,1)} %bitcast.9), channel_id=1, source_target_pairs={{0,8},{8,0},{1,9},{9,1},{2,10},{10,2},{3,11},{11,3},{4,12},{12,4},... | collective-permute-start | bytes 3145736 | tf_op jit(solution)/shard_map/ppermute | solution.py:282
  58.3 2.4 %collective-permute-start.1 = (bf16[4096,128]{1,0:T(8,128)(2,1)}, bf16[4096,128]{1,0:T(8,128)(2,1)}, u32[]{:S(2)}, u32[]{:S(2)}) collective-permute-start(bf16[4096,128]{1,0:T(8,128)(2,1)} %bitcast.11), channel_id=1, source_target_pairs={{0,8},{8,0},{1,9},{9,1},{2,10},{10,2},{3,11},{11,3},{4,12},{12,4},... | collective-permute-start | bytes 3145736 | tf_op jit(solution)/shard_map/ppermute | solution.py:282
  61.5 1.9 %collective-permute-start.5 = (bf16[128,2048]{1,0:T(8,128)(2,1)}, bf16[128,2048]{1,0:T(8,128)(2,1)}, u32[]{:S(2)}, u32[]{:S(2)}) collective-permute-start(bf16[128,2048]{1,0:T(8,128)(2,1)} %dynamic-slice_bitcast_fusion), channel_id=1, source_target_pairs={{0,256},{16,272},{256,0},{272,16},{1,257},{17,273},{257,1},{273,17... | collective-permute-start | bytes 1572872 | tf_op jit(solution)/shard_map/ppermute | solution.py:279
  63.5 4.8 %collective-permute-start.7 = (bf16[128,2048]{1,0:T(8,128)(2,1)}, bf16[128,2048]{1,0:T(8,128)(2,1)}, u32[]{:S(2)}, u32[]{:S(2)}) collective-permute-start(bf16[128,2048]{1,0:T(8,128)(2,1)} %dynamic-slice_bitcast_fusion), channel_id=1, source_target_pairs={{0,272},{16,256},{256,16},{272,0},{1,273},{17,257},{257,17},{273,1... | collective-permute-start | bytes 1572872 | tf_op jit(solution)/shard_map/ppermute | solution.py:279
  69.1 2.5 %collective-permute-start.3 = (bf16[128,2048]{1,0:T(8,128)(2,1)}, bf16[128,2048]{1,0:T(8,128)(2,1)}, u32[]{:S(2)}, u32[]{:S(2)}) collective-permute-start(bf16[128,2048]{1,0:T(8,128)(2,1)} %constant_dynamic-slice_fusion.refs_0_), channel_id=1, source_target_pairs={{0,16},{16,0},{256,272},{272,256},{1,17},{17,1},{257,273},{273,257... | collective-permute-start | bytes 1572872 | tf_op jit(solution)/shard_map/ppermute | solution.py:279
  71.6 20.5 %collective-permute-done.5.refs_4_ = bf16[128,2048]{1,0:T(8,128)(2,1)} collective-permute-done((bf16[128,2048]{1,0:T(8,128)(2,1)}, bf16[128,2048]{1,0:T(8,128)(2,1)}, u32[]{:S(2)}, u32[]{:S(2)}) %collective-permute-start.5) | collective-permute-done | bytes 524320 | tf_op jit(solution)/shard_map/ppermute | solution.py:279
  92.1 1.9 %collective-permute-start.2 = (bf16[128,2048]{1,0:T(8,128)(2,1)}, bf16[128,2048]{1,0:T(8,128)(2,1)}, u32[]{:S(2)}, u32[]{:S(2)}) collective-permute-start(bf16[128,2048]{1,0:T(8,128)(2,1)} %constant_dynamic-slice_fusion.refs_0_), channel_id=1, source_target_pairs={{0,8},{8,0},{1,9},{9,1},{2,10},{10,2},{3,11},{11,3},{4,12},{12,4},... | collective-permute-start | bytes 1572872 | tf_op jit(solution)/shard_map/ppermute | solution.py:282
  94.0 6.4 %collective-permute-done.7.refs_6_ = bf16[128,2048]{1,0:T(8,128)(2,1)} collective-permute-done((bf16[128,2048]{1,0:T(8,128)(2,1)}, bf16[128,2048]{1,0:T(8,128)(2,1)}, u32[]{:S(2)}, u32[]{:S(2)}) %collective-permute-start.7) | collective-permute-done | bytes 524320 | tf_op jit(solution)/shard_map/ppermute | solution.py:279
  100.4 1.9 %collective-permute-start.6 = (bf16[128,2048]{1,0:T(8,128)(2,1)}, bf16[128,2048]{1,0:T(8,128)(2,1)}, u32[]{:S(2)}, u32[]{:S(2)}) collective-permute-start(bf16[128,2048]{1,0:T(8,128)(2,1)} %collective-permute-done.5.refs_4_), channel_id=1, source_target_pairs={{0,8},{8,0},{1,9},{9,1},{2,10},{10,2},{3,11},{11,3},{4,12},{12,4},... | collective-permute-start | bytes 1572872 | tf_op jit(solution)/shard_map/ppermute | solution.py:282
  102.3 2.4 %collective-permute-start.8 = (bf16[128,2048]{1,0:T(8,128)(2,1)}, bf16[128,2048]{1,0:T(8,128)(2,1)}, u32[]{:S(2)}, u32[]{:S(2)}) collective-permute-start(bf16[128,2048]{1,0:T(8,128)(2,1)} %collective-permute-done.7.refs_6_), channel_id=1, source_target_pairs={{0,8},{8,0},{1,9},{9,1},{2,10},{10,2},{3,11},{11,3},{4,12},{12,4},... | collective-permute-start | bytes 1572872 | tf_op jit(solution)/shard_map/ppermute | solution.py:282
  104.8 1.9 %collective-permute-start.4 = (bf16[128,2048]{1,0:T(8,128)(2,1)}, bf16[128,2048]{1,0:T(8,128)(2,1)}, u32[]{:S(2)}, u32[]{:S(2)}) collective-permute-start(bf16[128,2048]{1,0:T(8,128)(2,1)} %collective-permute-done.3.refs_2_), channel_id=1, source_target_pairs={{0,8},{8,0},{1,9},{9,1},{2,10},{10,2},{3,11},{11,3},{4,12},{12,4},... | collective-permute-start | bytes 1572872 | tf_op jit(solution)/shard_map/ppermute | solution.py:282
  106.7 3.6 %gate_up.1 = bf16[4,128,256]{2,1,0:T(8,128)(2,1)} custom-call(bf16[4,1032,256]{2,1,0:T(8,128)(2,1)S(1)} %all-to-all-done.2.x_ref, bf16[4096,128]{1,0:T(8,128)(2,1)} %bitcast.10, bf16[4096,128]{1,0:T(8,128)(2,1)} %bitcast.12, bf16[4096,128]{1,0:T(8,128)(2,1)} %collective-permute-done.g1, bf16[4096,128]{1,0:T(8,128)(2,1)} %collective-permute-done.1.u1), custom_call_target="tpu_custom_call" | custom-call | tf_op jit(solution)/shard_map/gate_up/pallas_call | solution.py:202
  110.3 4.9 %all-to-all-start.3 = ((bf16[4,128,256]{2,1,0:T(8,128)(2,1)}), bf16[4,128,256]{2,1,0:T(8,128)(2,1)S(1)}, u32[]{:S(2)}, u32[]{:S(2)}) async-start(bf16[4,128,256]{2,1,0:T(8,128)(2,1)} %gate_up.1), calls=%async_computation.3 | async-start | bytes 524288 | tf_op jit(solution)/shard_map/all_to_all | solution.py:266
  115.2 5.5 %all-to-all-done.3.act_ref = bf16[4,128,256]{2,1,0:T(8,128)(2,1)S(1)} async-done(((bf16[4,128,256]{2,1,0:T(8,128)(2,1)}), bf16[4,128,256]{2,1,0:T(8,128)(2,1)S(1)}, u32[]{:S(2)}, u32[]{:S(2)}) %all-to-all-start.3) | async-done | bytes 262176 | tf_op jit(solution)/shard_map/all_to_all | solution.py:266
  120.7 3.3 %down.1 = bf16[8,128,256]{2,1,0:T(8,128)(2,1)} custom-call(bf16[4,128,256]{2,1,0:T(8,128)(2,1)S(1)} %all-to-all-done.3.act_ref, bf16[128,2048]{1,0:T(8,128)(2,1)} %constant_dynamic-slice_fusion.refs_0_, bf16[128,2048]{1,0:T(8,128)(2,1)} %collective-permute-done.2.refs_1_, bf16[128,2048]{1,0:T(8,128)(2,1)} %collective-permute-done.3.refs_2_, ...), custom_call_target="tpu_custom_call" | custom-call | tf_op jit(solution)/shard_map/down/pallas_call | solution.py:221
  124.1 3.5 %all-to-all-start.4 = ((bf16[8,128,256]{2,1,0:T(8,128)(2,1)}), bf16[8,128,256]{2,1,0:T(8,128)(2,1)S(1)}, u32[]{:S(2)}, u32[]{:S(2)}) async-start(bf16[8,128,256]{2,1,0:T(8,128)(2,1)} %down.1), calls=%async_computation.4 | async-start | bytes 1048576 | tf_op jit(solution)/shard_map/all_to_all | solution.py:266
  127.8 17.7 %all-to-all-done.4.x_ref = bf16[8,128,256]{2,1,0:T(8,128)(2,1)S(1)} async-done(((bf16[8,128,256]{2,1,0:T(8,128)(2,1)}), bf16[8,128,256]{2,1,0:T(8,128)(2,1)S(1)}, u32[]{:S(2)}, u32[]{:S(2)}) %all-to-all-start.4) | async-done | bytes 524320 | tf_op jit(solution)/shard_map/all_to_all | solution.py:266
  146.8 3.8 %all-to-all-start.5 = ((bf16[8,32,256]{2,1,0:T(8,128)(2,1)}), bf16[8,32,256]{2,1,0:T(8,128)(2,1)S(1)}, u32[]{:S(2)}, u32[]{:S(2)}) async-start(bf16[8,32,256]{2,1,0:T(8,128)(2,1)} %home.1), calls=%async_computation.5 | async-start | bytes 262144 | tf_op jit(solution)/shard_map/all_to_all | solution.py:266
  150.8 10.1 %all-to-all-done.5 = bf16[8,32,256]{2,1,0:T(8,128)(2,1)S(1)} async-done(((bf16[8,32,256]{2,1,0:T(8,128)(2,1)}), bf16[8,32,256]{2,1,0:T(8,128)(2,1)S(1)}, u32[]{:S(2)}, u32[]{:S(2)}) %all-to-all-start.5) | async-done | bytes 131104 | tf_op jit(solution)/shard_map/all_to_all | solution.py:266
  (26 shorter events, 8.4 us)
Async XLA Ops:
  0.0 60.7 %copy-start = (bf16[1,128,4096]{2,1,0:T(8,128)(2,1)S(1)}, bf16[1,128,4096]{2,1,0:T(8,128)(2,1)}, u32[]{:S(2)}) copy-start(bf16[1,128,4096]{2,1,0:T(8,128)(2,1)} %param.13) | copy-start | bytes 3145732
  1.5 18.9 %all-to-all-start = ((bf16[8,32,256]{2,1,0:T(8,128)(2,1)}), bf16[8,32,256]{2,1,0:T(8,128)(2,1)S(1)}, u32[]{:S(2)}, u32[]{:S(2)}) async-start(bf16[8,32,256]{2,1,0:T(8,128)(2,1)} %broadcast_in_dim.38), calls=%async_computation | async-start | bytes 262144 | tf_op jit(solution)/shard_map/all_to_all | solution.py:266
  20.4 0.7 copy-start.1
  51.4 55.3 %all-to-all-start.2 = ((bf16[4,1032,256]{2,1,0:T(8,128)(2,1)}), bf16[4,1032,256]{2,1,0:T(8,128)(2,1)S(1)}, u32[]{:S(2)}, u32[]{:S(2)}) async-start(bf16[4,1032,256]{2,1,0:T(8,128)(2,1)} %prep.1), calls=%async_computation.2 | async-start | bytes 4227072 | tf_op jit(solution)/shard_map/all_to_all | solution.py:266
  56.3 48.4 %collective-permute-start = (bf16[4096,128]{1,0:T(8,128)(2,1)}, bf16[4096,128]{1,0:T(8,128)(2,1)}, u32[]{:S(2)}, u32[]{:S(2)}) collective-permute-start(bf16[4096,128]{1,0:T(8,128)(2,1)} %bitcast.9), channel_id=1, source_target_pairs={{0,8},{8,0},{1,9},{9,1},{2,10},{10,2},{3,11},{11,3},{4,12},{12,4},... | collective-permute-start | bytes 3145736 | tf_op jit(solution)/shard_map/ppermute | solution.py:282
  58.3 48.4 %collective-permute-start.1 = (bf16[4096,128]{1,0:T(8,128)(2,1)}, bf16[4096,128]{1,0:T(8,128)(2,1)}, u32[]{:S(2)}, u32[]{:S(2)}) collective-permute-start(bf16[4096,128]{1,0:T(8,128)(2,1)} %bitcast.11), channel_id=1, source_target_pairs={{0,8},{8,0},{1,9},{9,1},{2,10},{10,2},{3,11},{11,3},{4,12},{12,4},... | collective-permute-start | bytes 3145736 | tf_op jit(solution)/shard_map/ppermute | solution.py:282
  61.5 30.6 %collective-permute-start.5 = (bf16[128,2048]{1,0:T(8,128)(2,1)}, bf16[128,2048]{1,0:T(8,128)(2,1)}, u32[]{:S(2)}, u32[]{:S(2)}) collective-permute-start(bf16[128,2048]{1,0:T(8,128)(2,1)} %dynamic-slice_bitcast_fusion), channel_id=1, source_target_pairs={{0,256},{16,272},{256,0},{272,16},{1,257},{17,273},{257,1},{273,17... | collective-permute-start | bytes 1572872 | tf_op jit(solution)/shard_map/ppermute | solution.py:279
  63.5 36.9 %collective-permute-start.7 = (bf16[128,2048]{1,0:T(8,128)(2,1)}, bf16[128,2048]{1,0:T(8,128)(2,1)}, u32[]{:S(2)}, u32[]{:S(2)}) collective-permute-start(bf16[128,2048]{1,0:T(8,128)(2,1)} %dynamic-slice_bitcast_fusion), channel_id=1, source_target_pairs={{0,272},{16,256},{256,16},{272,0},{1,273},{17,257},{257,17},{273,1... | collective-permute-start | bytes 1572872 | tf_op jit(solution)/shard_map/ppermute | solution.py:279
  69.1 33.2 %collective-permute-start.3 = (bf16[128,2048]{1,0:T(8,128)(2,1)}, bf16[128,2048]{1,0:T(8,128)(2,1)}, u32[]{:S(2)}, u32[]{:S(2)}) collective-permute-start(bf16[128,2048]{1,0:T(8,128)(2,1)} %constant_dynamic-slice_fusion.refs_0_), channel_id=1, source_target_pairs={{0,16},{16,0},{256,272},{272,256},{1,17},{17,1},{257,273},{273,257... | collective-permute-start | bytes 1572872 | tf_op jit(solution)/shard_map/ppermute | solution.py:279
  92.1 23.1 %collective-permute-start.2 = (bf16[128,2048]{1,0:T(8,128)(2,1)}, bf16[128,2048]{1,0:T(8,128)(2,1)}, u32[]{:S(2)}, u32[]{:S(2)}) collective-permute-start(bf16[128,2048]{1,0:T(8,128)(2,1)} %constant_dynamic-slice_fusion.refs_0_), channel_id=1, source_target_pairs={{0,8},{8,0},{1,9},{9,1},{2,10},{10,2},{3,11},{11,3},{4,12},{12,4},... | collective-permute-start | bytes 1572872 | tf_op jit(solution)/shard_map/ppermute | solution.py:282
  100.4 14.8 %collective-permute-start.6 = (bf16[128,2048]{1,0:T(8,128)(2,1)}, bf16[128,2048]{1,0:T(8,128)(2,1)}, u32[]{:S(2)}, u32[]{:S(2)}) collective-permute-start(bf16[128,2048]{1,0:T(8,128)(2,1)} %collective-permute-done.5.refs_4_), channel_id=1, source_target_pairs={{0,8},{8,0},{1,9},{9,1},{2,10},{10,2},{3,11},{11,3},{4,12},{12,4},... | collective-permute-start | bytes 1572872 | tf_op jit(solution)/shard_map/ppermute | solution.py:282
  102.3 12.9 %collective-permute-start.8 = (bf16[128,2048]{1,0:T(8,128)(2,1)}, bf16[128,2048]{1,0:T(8,128)(2,1)}, u32[]{:S(2)}, u32[]{:S(2)}) collective-permute-start(bf16[128,2048]{1,0:T(8,128)(2,1)} %collective-permute-done.7.refs_6_), channel_id=1, source_target_pairs={{0,8},{8,0},{1,9},{9,1},{2,10},{10,2},{3,11},{11,3},{4,12},{12,4},... | collective-permute-start | bytes 1572872 | tf_op jit(solution)/shard_map/ppermute | solution.py:282
  104.8 10.4 %collective-permute-start.4 = (bf16[128,2048]{1,0:T(8,128)(2,1)}, bf16[128,2048]{1,0:T(8,128)(2,1)}, u32[]{:S(2)}, u32[]{:S(2)}) collective-permute-start(bf16[128,2048]{1,0:T(8,128)(2,1)} %collective-permute-done.3.refs_2_), channel_id=1, source_target_pairs={{0,8},{8,0},{1,9},{9,1},{2,10},{10,2},{3,11},{11,3},{4,12},{12,4},... | collective-permute-start | bytes 1572872 | tf_op jit(solution)/shard_map/ppermute | solution.py:282
  110.3 10.4 %all-to-all-start.3 = ((bf16[4,128,256]{2,1,0:T(8,128)(2,1)}), bf16[4,128,256]{2,1,0:T(8,128)(2,1)S(1)}, u32[]{:S(2)}, u32[]{:S(2)}) async-start(bf16[4,128,256]{2,1,0:T(8,128)(2,1)} %gate_up.1), calls=%async_computation.3 | async-start | bytes 524288 | tf_op jit(solution)/shard_map/all_to_all | solution.py:266
  115.2 12.4 %copy-start.2 = (s32[8,2]{0,1:T(2,128)S(1)}, s32[8,2]{0,1:T(2,128)}, u32[]{:S(2)}) copy-start(s32[8,2]{0,1:T(2,128)} %param.10) | copy-start | bytes 196
  115.2 35.5 %copy-start.3 = (f32[32,2]{0,1:T(2,128)S(1)}, f32[32,2]{0,1:T(2,128)}, u32[]{:S(2)}) copy-start(f32[32,2]{0,1:T(2,128)} %param.9) | copy-start | bytes 772
  124.1 21.4 %all-to-all-start.4 = ((bf16[8,128,256]{2,1,0:T(8,128)(2,1)}), bf16[8,128,256]{2,1,0:T(8,128)(2,1)S(1)}, u32[]{:S(2)}, u32[]{:S(2)}) async-start(bf16[8,128,256]{2,1,0:T(8,128)(2,1)} %down.1), calls=%async_computation.4 | async-start | bytes 1048576 | tf_op jit(solution)/shard_map/all_to_all | solution.py:266
  146.8 14.0 %all-to-all-start.5 = ((bf16[8,32,256]{2,1,0:T(8,128)(2,1)}), bf16[8,32,256]{2,1,0:T(8,128)(2,1)S(1)}, u32[]{:S(2)}, u32[]{:S(2)}) async-start(bf16[8,32,256]{2,1,0:T(8,128)(2,1)} %home.1), calls=%async_computation.5 | async-start | bytes 262144 | tf_op jit(solution)/shard_map/all_to_all | solution.py:266

commit v8 on v7

--- a/solution.py
+++ b/solution.py
@@ -148,12 +148,17 @@
         send.wait()
 
 
-def pick_kernel(experts_ref, x_ref, gain_ref, out_ref, y_ref, sems):
+def pick_kernel(experts_hbm, x_ref, gain_hbm, out_ref, y_ref, experts_ref, gain_ref, sems):
     _, rows, w = x_ref.shape
+    loads = [
+        pltpu.make_async_copy(experts_hbm, experts_ref, sems.at[out_ref.shape[0]]),
+        pltpu.make_async_copy(gain_hbm, gain_ref, sems.at[out_ref.shape[0] + 1]),
+    ]
+    sent_all(loads)
+    y_ref[MOST * rows :, :] = jnp.broadcast_to(gain_ref[...].astype(F32)[None, :], (8, w)).astype(BF16)
     block_of_slot, _ = routed(experts_ref, lax.axis_index("group"))
     for k, block in enumerate(block_of_slot):
         y_ref[k * rows : (k + 1) * rows, :] = x_ref[block]
-    y_ref[MOST * rows :, :] = jnp.broadcast_to(gain_ref[...].astype(F32), (8, w)).astype(BF16)
     sent_all([pltpu.make_async_copy(y_ref, out_ref.at[j], sems.at[j]) for j in range(out_ref.shape[0])])
 
 
@@ -241,11 +246,16 @@
     return pl.pallas_call(
         pick_kernel,
         out_shape=pltpu.HBM((copies, tall, w), BF16),
-        in_specs=[SM, VM, VM],
+        in_specs=[HBM, VM, HBM],
         out_specs=HBM,
-        scratch_shapes=[pltpu.VMEM((tall, w), BF16), pltpu.SemaphoreType.DMA((copies,))],
+        scratch_shapes=[
+            pltpu.VMEM((tall, w), BF16),
+            pltpu.SMEM(block_experts.shape[::-1], jnp.int32),
+            pltpu.VMEM((w,), BF16),
+            pltpu.SemaphoreType.DMA((copies + 2,)),
+        ],
         compiler_params=pltpu.CompilerParams(vmem_limit_bytes=1 << 20),
-    )(block_experts.T, vm(blocks), norm_gain[None, :])
+    )(hbm(block_experts.T), vm(blocks), hbm(norm_gain))
 
 
 def homed(block_experts, parts):

time: 162 us -> 161 us (level)
  blocking collectives: 27.2 us -> 45.9 us
  waiting for transfers between devices: 69.8 us -> 60.2 us
  starting transfers between devices: 47.4 us -> 38.7 us
  local copies, waits for them, and re-layouts: 4.69 us -> 2.7 us
    all_to_all x1 -> x2, blocking collectives: 27.2 us -> 45.9 us  [exchange(): return lax.all_to_all(x, axes, split_axis=0, concat_axis=0, tiled=True)]
    all_to_all x5 -> x4, waiting for transfers between devices: 42.9 us -> 33.3 us  [exchange(): return lax.all_to_all(x, axes, split_axis=0, concat_axis=0, tiled=True)]
    all_to_all x5 -> x4, starting transfers between devices: 25.7 us -> 17 us  [exchange(): return lax.all_to_all(x, axes, split_axis=0, concat_axis=0, tiled=True)]
  transfers between devices with their start and end apart: 14 -> 13, of which waited for: 6 -> 5; matrix products, arithmetic and copies ran while one was open for 2% -> 1% of each run, Pallas kernels for 2% -> 2%
where the time goes in v8:
time: 161 us; the launch traced here: 160 us
  waiting for transfers between devices  60.2 us (37%)
  blocking collectives  45.9 us (29%)
  starting transfers between devices  38.7 us (24%)
  Pallas kernels  11.5 us (7%)
  local copies, waits for them, and re-layouts  2.7 us (2%)
    all_to_all x2, blocking collectives, exchange(): return lax.all_to_all(x, axes, split_axis=0, concat_axis=0, tiled=True)  45.9 us
    all_to_all x4, waiting for transfers between devices, exchange(): return lax.all_to_all(x, axes, split_axis=0, concat_axis=0, tiled=True)  33.3 us
    ppermute x3, waiting for transfers between devices, sent(): return lax.ppermute(x, SQUARE, [(i, i ^ flip) for i in range(4)])  26.9 us
    all_to_all x4, starting transfers between devices, exchange(): return lax.all_to_all(x, axes, split_axis=0, concat_axis=0, tiled=True)  17 us
    ppermute x6, starting transfers between devices, swapped(): return lax.ppermute(x, 'core', [(0, 1), (1, 0)])  12.5 us
    ppermute x3, starting transfers between devices, sent(): return lax.ppermute(x, SQUARE, [(i, i ^ flip) for i in range(4)])  9.19 us
    pallas_call x1, Pallas kernels, gated(): pl.pallas_call(gate_up_kernel, out_shape=pltpu.HBM((4, rows, 2 * ff), BF1...  3.59 us
    pallas_call x1, Pallas kernels, lowered(): pl.pallas_call(down_kernel, out_shape=pltpu.HBM(shape, BF16), in_specs=[V...  3.34 us
  transfers between devices with their start and end apart: 13, of which 5 were waited for; matrix products, arithmetic and copies ran while one was open for 1% of the time, Pallas kernels for 2%

profile of v8, /device:TPU:8, one launch (start us, length us, event | category | flops | bytes accessed | tf_op | source)
XLA Modules:
  0.0 160.2 jit_solution(4902421381974471)
XLA Ops:
  0.8 18.7 %all_to_all.30.x_ref = bf16[8,32,256]{2,1,0:T(8,128)(2,1)S(1)} all-to-all(bf16[8,32,256]{2,1,0:T(8,128)(2,1)S(1)} %broadcast_in_dim.35), channel_id=1, replica_groups=mesh['sec'=2,'group'=8,'xlo'=2,'core'=2,'hid'=8] {'group'}, dimensions={0} | all-to-all | bytes 262144 | tf_op jit(solution)/shard_map/all_to_all | solution.py:276
  19.5 1.6 %shard_map.73 = bf16[8,136,256]{2,1,0:T(8,128)(2,1)} custom-call(s32[2,8]{1,0:T(2,128)} %bitcast.7, bf16[8,32,256]{2,1,0:T(8,128)(2,1)S(1)} %all_to_all.30.x_ref, bf16[256]{0:T(256)(128)(2,1)} %gain_hbm.1), custom_call_target="tpu_custom_call" | custom-call | tf_op jit(solution)/shard_map/pallas_call | solution.py:246
  21.2 27.2 %all_to_all.31.x_ref = bf16[8,136,256]{2,1,0:T(8,128)(2,1)S(1)} all-to-all(bf16[8,136,256]{2,1,0:T(8,128)(2,1)} %shard_map.73), channel_id=1, replica_groups=mesh['sec'=2,'group'=8,'xlo'=2,'core'=2,'hid'=8] {'hid'}, dimensions={0} | all-to-all | bytes 1114112 | tf_op jit(solution)/shard_map/all_to_all | solution.py:276
  48.4 1.6 %prep.1 = bf16[4,1032,256]{2,1,0:T(8,128)(2,1)} custom-call(bf16[8,136,256]{2,1,0:T(8,128)(2,1)S(1)} %all_to_all.31.x_ref), custom_call_target="tpu_custom_call" | custom-call | tf_op jit(solution)/shard_map/prep/pallas_call | solution.py:192
  50.1 4.9 %all-to-all-start.2 = ((bf16[4,1032,256]{2,1,0:T(8,128)(2,1)}), bf16[4,1032,256]{2,1,0:T(8,128)(2,1)S(1)}, u32[]{:S(2)}, u32[]{:S(2)}) async-start(bf16[4,1032,256]{2,1,0:T(8,128)(2,1)} %prep.1), calls=%async_computation.2 | async-start | bytes 4227072 | tf_op jit(solution)/shard_map/all_to_all | solution.py:276
  55.0 1.9 %collective-permute-start = (bf16[4096,128]{1,0:T(8,128)(2,1)}, bf16[4096,128]{1,0:T(8,128)(2,1)}, u32[]{:S(2)}, u32[]{:S(2)}) collective-permute-start(bf16[4096,128]{1,0:T(8,128)(2,1)} %bitcast.9), channel_id=1, source_target_pairs={{0,8},{8,0},{1,9},{9,1},{2,10},{10,2},{3,11},{11,3},{4,12},{12,4},... | collective-permute-start | bytes 3145736 | tf_op jit(solution)/shard_map/ppermute | solution.py:292
  56.9 2.4 %collective-permute-start.1 = (bf16[4096,128]{1,0:T(8,128)(2,1)}, bf16[4096,128]{1,0:T(8,128)(2,1)}, u32[]{:S(2)}, u32[]{:S(2)}) collective-permute-start(bf16[4096,128]{1,0:T(8,128)(2,1)} %bitcast.11), channel_id=1, source_target_pairs={{0,8},{8,0},{1,9},{9,1},{2,10},{10,2},{3,11},{11,3},{4,12},{12,4},... | collective-permute-start | bytes 3145736 | tf_op jit(solution)/shard_map/ppermute | solution.py:292
  60.2 1.9 %collective-permute-start.5 = (bf16[128,2048]{1,0:T(8,128)(2,1)}, bf16[128,2048]{1,0:T(8,128)(2,1)}, u32[]{:S(2)}, u32[]{:S(2)}) collective-permute-start(bf16[128,2048]{1,0:T(8,128)(2,1)} %dynamic-slice_bitcast_fusion), channel_id=1, source_target_pairs={{0,256},{16,272},{256,0},{272,16},{1,257},{17,273},{257,1},{273,17... | collective-permute-start | bytes 1572872 | tf_op jit(solution)/shard_map/ppermute | solution.py:289
  62.1 4.8 %collective-permute-start.7 = (bf16[128,2048]{1,0:T(8,128)(2,1)}, bf16[128,2048]{1,0:T(8,128)(2,1)}, u32[]{:S(2)}, u32[]{:S(2)}) collective-permute-start(bf16[128,2048]{1,0:T(8,128)(2,1)} %dynamic-slice_bitcast_fusion), channel_id=1, source_target_pairs={{0,272},{16,256},{256,16},{272,0},{1,273},{17,257},{257,17},{273,1... | collective-permute-start | bytes 1572872 | tf_op jit(solution)/shard_map/ppermute | solution.py:289
  67.8 2.5 %collective-permute-start.3 = (bf16[128,2048]{1,0:T(8,128)(2,1)}, bf16[128,2048]{1,0:T(8,128)(2,1)}, u32[]{:S(2)}, u32[]{:S(2)}) collective-permute-start(bf16[128,2048]{1,0:T(8,128)(2,1)} %constant_dynamic-slice_fusion.refs_0_), channel_id=1, source_target_pairs={{0,16},{16,0},{256,272},{272,256},{1,17},{17,1},{257,273},{273,257... | collective-permute-start | bytes 1572872 | tf_op jit(solution)/shard_map/ppermute | solution.py:289
  70.2 20.5 %collective-permute-done.5.refs_4_ = bf16[128,2048]{1,0:T(8,128)(2,1)} collective-permute-done((bf16[128,2048]{1,0:T(8,128)(2,1)}, bf16[128,2048]{1,0:T(8,128)(2,1)}, u32[]{:S(2)}, u32[]{:S(2)}) %collective-permute-start.5) | collective-permute-done | bytes 524320 | tf_op jit(solution)/shard_map/ppermute | solution.py:289
  90.7 1.9 %collective-permute-start.2 = (bf16[128,2048]{1,0:T(8,128)(2,1)}, bf16[128,2048]{1,0:T(8,128)(2,1)}, u32[]{:S(2)}, u32[]{:S(2)}) collective-permute-start(bf16[128,2048]{1,0:T(8,128)(2,1)} %constant_dynamic-slice_fusion.refs_0_), channel_id=1, source_target_pairs={{0,8},{8,0},{1,9},{9,1},{2,10},{10,2},{3,11},{11,3},{4,12},{12,4},... | collective-permute-start | bytes 1572872 | tf_op jit(solution)/shard_map/ppermute | solution.py:292
  92.6 6.4 %collective-permute-done.7.refs_6_ = bf16[128,2048]{1,0:T(8,128)(2,1)} collective-permute-done((bf16[128,2048]{1,0:T(8,128)(2,1)}, bf16[128,2048]{1,0:T(8,128)(2,1)}, u32[]{:S(2)}, u32[]{:S(2)}) %collective-permute-start.7) | collective-permute-done | bytes 524320 | tf_op jit(solution)/shard_map/ppermute | solution.py:289
  99.0 1.9 %collective-permute-start.6 = (bf16[128,2048]{1,0:T(8,128)(2,1)}, bf16[128,2048]{1,0:T(8,128)(2,1)}, u32[]{:S(2)}, u32[]{:S(2)}) collective-permute-start(bf16[128,2048]{1,0:T(8,128)(2,1)} %collective-permute-done.5.refs_4_), channel_id=1, source_target_pairs={{0,8},{8,0},{1,9},{9,1},{2,10},{10,2},{3,11},{11,3},{4,12},{12,4},... | collective-permute-start | bytes 1572872 | tf_op jit(solution)/shard_map/ppermute | solution.py:292
  101.0 2.4 %collective-permute-start.8 = (bf16[128,2048]{1,0:T(8,128)(2,1)}, bf16[128,2048]{1,0:T(8,128)(2,1)}, u32[]{:S(2)}, u32[]{:S(2)}) collective-permute-start(bf16[128,2048]{1,0:T(8,128)(2,1)} %collective-permute-done.7.refs_6_), channel_id=1, source_target_pairs={{0,8},{8,0},{1,9},{9,1},{2,10},{10,2},{3,11},{11,3},{4,12},{12,4},... | collective-permute-start | bytes 1572872 | tf_op jit(solution)/shard_map/ppermute | solution.py:292
  103.4 1.9 %collective-permute-start.4 = (bf16[128,2048]{1,0:T(8,128)(2,1)}, bf16[128,2048]{1,0:T(8,128)(2,1)}, u32[]{:S(2)}, u32[]{:S(2)}) collective-permute-start(bf16[128,2048]{1,0:T(8,128)(2,1)} %collective-permute-done.3.refs_2_), channel_id=1, source_target_pairs={{0,8},{8,0},{1,9},{9,1},{2,10},{10,2},{3,11},{11,3},{4,12},{12,4},... | collective-permute-start | bytes 1572872 | tf_op jit(solution)/shard_map/ppermute | solution.py:292
  105.3 3.6 %gate_up.1 = bf16[4,128,256]{2,1,0:T(8,128)(2,1)} custom-call(bf16[4,1032,256]{2,1,0:T(8,128)(2,1)S(1)} %all-to-all-done.2.x_ref, bf16[4096,128]{1,0:T(8,128)(2,1)} %bitcast.10, bf16[4096,128]{1,0:T(8,128)(2,1)} %bitcast.12, bf16[4096,128]{1,0:T(8,128)(2,1)} %collective-permute-done.g1, bf16[4096,128]{1,0:T(8,128)(2,1)} %collective-permute-done.1.u1), custom_call_target="tpu_custom_call" | custom-call | tf_op jit(solution)/shard_map/gate_up/pallas_call | solution.py:207
  108.9 4.9 %all-to-all-start.3 = ((bf16[4,128,256]{2,1,0:T(8,128)(2,1)}), bf16[4,128,256]{2,1,0:T(8,128)(2,1)S(1)}, u32[]{:S(2)}, u32[]{:S(2)}) async-start(bf16[4,128,256]{2,1,0:T(8,128)(2,1)} %gate_up.1), calls=%async_computation.3 | async-start | bytes 524288 | tf_op jit(solution)/shard_map/all_to_all | solution.py:276
  113.8 5.5 %all-to-all-done.3.act_ref = bf16[4,128,256]{2,1,0:T(8,128)(2,1)S(1)} async-done(((bf16[4,128,256]{2,1,0:T(8,128)(2,1)}), bf16[4,128,256]{2,1,0:T(8,128)(2,1)S(1)}, u32[]{:S(2)}, u32[]{:S(2)}) %all-to-all-start.3) | async-done | bytes 262176 | tf_op jit(solution)/shard_map/all_to_all | solution.py:276
  119.3 3.3 %down.1 = bf16[8,128,256]{2,1,0:T(8,128)(2,1)} custom-call(bf16[4,128,256]{2,1,0:T(8,128)(2,1)S(1)} %all-to-all-done.3.act_ref, bf16[128,2048]{1,0:T(8,128)(2,1)} %constant_dynamic-slice_fusion.refs_0_, bf16[128,2048]{1,0:T(8,128)(2,1)} %collective-permute-done.2.refs_1_, bf16[128,2048]{1,0:T(8,128)(2,1)} %collective-permute-done.3.refs_2_, ...), custom_call_target="tpu_custom_call" | custom-call | tf_op jit(solution)/shard_map/down/pallas_call | solution.py:226
  122.7 3.5 %all-to-all-start.4 = ((bf16[8,128,256]{2,1,0:T(8,128)(2,1)}), bf16[8,128,256]{2,1,0:T(8,128)(2,1)S(1)}, u32[]{:S(2)}, u32[]{:S(2)}) async-start(bf16[8,128,256]{2,1,0:T(8,128)(2,1)} %down.1), calls=%async_computation.4 | async-start | bytes 1048576 | tf_op jit(solution)/shard_map/all_to_all | solution.py:276
  126.4 17.7 %all-to-all-done.4.x_ref = bf16[8,128,256]{2,1,0:T(8,128)(2,1)S(1)} async-done(((bf16[8,128,256]{2,1,0:T(8,128)(2,1)}), bf16[8,128,256]{2,1,0:T(8,128)(2,1)S(1)}, u32[]{:S(2)}, u32[]{:S(2)}) %all-to-all-start.4) | async-done | bytes 524320 | tf_op jit(solution)/shard_map/all_to_all | solution.py:276
  145.5 3.8 %all-to-all-start.5 = ((bf16[8,32,256]{2,1,0:T(8,128)(2,1)}), bf16[8,32,256]{2,1,0:T(8,128)(2,1)S(1)}, u32[]{:S(2)}, u32[]{:S(2)}) async-start(bf16[8,32,256]{2,1,0:T(8,128)(2,1)} %home.1), calls=%async_computation.5 | async-start | bytes 262144 | tf_op jit(solution)/shard_map/all_to_all | solution.py:276
  149.4 10.1 %all-to-all-done.5 = bf16[8,32,256]{2,1,0:T(8,128)(2,1)S(1)} async-done(((bf16[8,32,256]{2,1,0:T(8,128)(2,1)}), bf16[8,32,256]{2,1,0:T(8,128)(2,1)S(1)}, u32[]{:S(2)}, u32[]{:S(2)}) %all-to-all-start.5) | async-done | bytes 131104 | tf_op jit(solution)/shard_map/all_to_all | solution.py:276
  (22 shorter events, 4.9 us)
Async XLA Ops:
  0.0 59.3 %copy-start = (bf16[1,128,4096]{2,1,0:T(8,128)(2,1)S(1)}, bf16[1,128,4096]{2,1,0:T(8,128)(2,1)}, u32[]{:S(2)}) copy-start(bf16[1,128,4096]{2,1,0:T(8,128)(2,1)} %param.13) | copy-start | bytes 3145732
  50.1 55.3 %all-to-all-start.2 = ((bf16[4,1032,256]{2,1,0:T(8,128)(2,1)}), bf16[4,1032,256]{2,1,0:T(8,128)(2,1)S(1)}, u32[]{:S(2)}, u32[]{:S(2)}) async-start(bf16[4,1032,256]{2,1,0:T(8,128)(2,1)} %prep.1), calls=%async_computation.2 | async-start | bytes 4227072 | tf_op jit(solution)/shard_map/all_to_all | solution.py:276
  55.0 48.4 %collective-permute-start = (bf16[4096,128]{1,0:T(8,128)(2,1)}, bf16[4096,128]{1,0:T(8,128)(2,1)}, u32[]{:S(2)}, u32[]{:S(2)}) collective-permute-start(bf16[4096,128]{1,0:T(8,128)(2,1)} %bitcast.9), channel_id=1, source_target_pairs={{0,8},{8,0},{1,9},{9,1},{2,10},{10,2},{3,11},{11,3},{4,12},{12,4},... | collective-permute-start | bytes 3145736 | tf_op jit(solution)/shard_map/ppermute | solution.py:292
  56.9 48.4 %collective-permute-start.1 = (bf16[4096,128]{1,0:T(8,128)(2,1)}, bf16[4096,128]{1,0:T(8,128)(2,1)}, u32[]{:S(2)}, u32[]{:S(2)}) collective-permute-start(bf16[4096,128]{1,0:T(8,128)(2,1)} %bitcast.11), channel_id=1, source_target_pairs={{0,8},{8,0},{1,9},{9,1},{2,10},{10,2},{3,11},{11,3},{4,12},{12,4},... | collective-permute-start | bytes 3145736 | tf_op jit(solution)/shard_map/ppermute | solution.py:292
  60.2 30.6 %collective-permute-start.5 = (bf16[128,2048]{1,0:T(8,128)(2,1)}, bf16[128,2048]{1,0:T(8,128)(2,1)}, u32[]{:S(2)}, u32[]{:S(2)}) collective-permute-start(bf16[128,2048]{1,0:T(8,128)(2,1)} %dynamic-slice_bitcast_fusion), channel_id=1, source_target_pairs={{0,256},{16,272},{256,0},{272,16},{1,257},{17,273},{257,1},{273,17... | collective-permute-start | bytes 1572872 | tf_op jit(solution)/shard_map/ppermute | solution.py:289
  62.1 36.9 %collective-permute-start.7 = (bf16[128,2048]{1,0:T(8,128)(2,1)}, bf16[128,2048]{1,0:T(8,128)(2,1)}, u32[]{:S(2)}, u32[]{:S(2)}) collective-permute-start(bf16[128,2048]{1,0:T(8,128)(2,1)} %dynamic-slice_bitcast_fusion), channel_id=1, source_target_pairs={{0,272},{16,256},{256,16},{272,0},{1,273},{17,257},{257,17},{273,1... | collective-permute-start | bytes 1572872 | tf_op jit(solution)/shard_map/ppermute | solution.py:289
  67.8 33.2 %collective-permute-start.3 = (bf16[128,2048]{1,0:T(8,128)(2,1)}, bf16[128,2048]{1,0:T(8,128)(2,1)}, u32[]{:S(2)}, u32[]{:S(2)}) collective-permute-start(bf16[128,2048]{1,0:T(8,128)(2,1)} %constant_dynamic-slice_fusion.refs_0_), channel_id=1, source_target_pairs={{0,16},{16,0},{256,272},{272,256},{1,17},{17,1},{257,273},{273,257... | collective-permute-start | bytes 1572872 | tf_op jit(solution)/shard_map/ppermute | solution.py:289
  90.7 23.1 %collective-permute-start.2 = (bf16[128,2048]{1,0:T(8,128)(2,1)}, bf16[128,2048]{1,0:T(8,128)(2,1)}, u32[]{:S(2)}, u32[]{:S(2)}) collective-permute-start(bf16[128,2048]{1,0:T(8,128)(2,1)} %constant_dynamic-slice_fusion.refs_0_), channel_id=1, source_target_pairs={{0,8},{8,0},{1,9},{9,1},{2,10},{10,2},{3,11},{11,3},{4,12},{12,4},... | collective-permute-start | bytes 1572872 | tf_op jit(solution)/shard_map/ppermute | solution.py:292
  99.0 14.8 %collective-permute-start.6 = (bf16[128,2048]{1,0:T(8,128)(2,1)}, bf16[128,2048]{1,0:T(8,128)(2,1)}, u32[]{:S(2)}, u32[]{:S(2)}) collective-permute-start(bf16[128,2048]{1,0:T(8,128)(2,1)} %collective-permute-done.5.refs_4_), channel_id=1, source_target_pairs={{0,8},{8,0},{1,9},{9,1},{2,10},{10,2},{3,11},{11,3},{4,12},{12,4},... | collective-permute-start | bytes 1572872 | tf_op jit(solution)/shard_map/ppermute | solution.py:292
  101.0 12.9 %collective-permute-start.8 = (bf16[128,2048]{1,0:T(8,128)(2,1)}, bf16[128,2048]{1,0:T(8,128)(2,1)}, u32[]{:S(2)}, u32[]{:S(2)}) collective-permute-start(bf16[128,2048]{1,0:T(8,128)(2,1)} %collective-permute-done.7.refs_6_), channel_id=1, source_target_pairs={{0,8},{8,0},{1,9},{9,1},{2,10},{10,2},{3,11},{11,3},{4,12},{12,4},... | collective-permute-start | bytes 1572872 | tf_op jit(solution)/shard_map/ppermute | solution.py:292
  103.4 10.4 %collective-permute-start.4 = (bf16[128,2048]{1,0:T(8,128)(2,1)}, bf16[128,2048]{1,0:T(8,128)(2,1)}, u32[]{:S(2)}, u32[]{:S(2)}) collective-permute-start(bf16[128,2048]{1,0:T(8,128)(2,1)} %collective-permute-done.3.refs_2_), channel_id=1, source_target_pairs={{0,8},{8,0},{1,9},{9,1},{2,10},{10,2},{3,11},{11,3},{4,12},{12,4},... | collective-permute-start | bytes 1572872 | tf_op jit(solution)/shard_map/ppermute | solution.py:292
  108.9 10.4 %all-to-all-start.3 = ((bf16[4,128,256]{2,1,0:T(8,128)(2,1)}), bf16[4,128,256]{2,1,0:T(8,128)(2,1)S(1)}, u32[]{:S(2)}, u32[]{:S(2)}) async-start(bf16[4,128,256]{2,1,0:T(8,128)(2,1)} %gate_up.1), calls=%async_computation.3 | async-start | bytes 524288 | tf_op jit(solution)/shard_map/all_to_all | solution.py:276
  113.8 12.4 %copy-start.1 = (s32[8,2]{0,1:T(2,128)S(1)}, s32[8,2]{0,1:T(2,128)}, u32[]{:S(2)}) copy-start(s32[8,2]{0,1:T(2,128)} %param.10) | copy-start | bytes 196
  113.8 35.5 %copy-start.2 = (f32[32,2]{0,1:T(2,128)S(1)}, f32[32,2]{0,1:T(2,128)}, u32[]{:S(2)}) copy-start(f32[32,2]{0,1:T(2,128)} %param.9) | copy-start | bytes 772
  122.7 21.4 %all-to-all-start.4 = ((bf16[8,128,256]{2,1,0:T(8,128)(2,1)}), bf16[8,128,256]{2,1,0:T(8,128)(2,1)S(1)}, u32[]{:S(2)}, u32[]{:S(2)}) async-start(bf16[8,128,256]{2,1,0:T(8,128)(2,1)} %down.1), calls=%async_computation.4 | async-start | bytes 1048576 | tf_op jit(solution)/shard_map/all_to_all | solution.py:276
  145.5 14.0 %all-to-all-start.5 = ((bf16[8,32,256]{2,1,0:T(8,128)(2,1)}), bf16[8,32,256]{2,1,0:T(8,128)(2,1)S(1)}, u32[]{:S(2)}, u32[]{:S(2)}) async-start(bf16[8,32,256]{2,1,0:T(8,128)(2,1)} %home.1), calls=%async_computation.5 | async-start | bytes 262144 | tf_op jit(solution)/shard_map/all_to_all | solution.py:276

commit v9 on v8

--- a/solution.py
+++ b/solution.py
@@ -16,14 +16,19 @@
 SQUARE = ("sec", "xlo")
 
 
+def place_of(z):
+    return (z + 1) % HID
+
+
 def prep_kernel(x_ref, out_ref, y_ref, sems):
     n, rows, w = x_ref.shape
     rows -= 8
     copies = out_ref.shape[0]
     total = jnp.zeros((rows, w), F32)
     for z in range(n):
-        x = x_ref[z, 0:rows, :].astype(F32)
-        g = x_ref[z, rows : rows + 1, :].astype(F32)
+        k = place_of(z)
+        x = x_ref[k, 0:rows, :].astype(F32)
+        g = x_ref[k, rows : rows + 1, :].astype(F32)
         total = total + x * x
         y_ref[z * rows : (z + 1) * rows, :] = (x * g).astype(BF16)
     col = jnp.sum(total, axis=1, keepdims=True)
@@ -117,14 +122,10 @@
             if h == 0:
                 acc_ref[z] = part
                 continue
-            y_ref[z] = (acc_ref[z] + part).astype(BF16)
-            if z % 2:
-                sends.append(
-                    pltpu.make_async_copy(
-                        y_ref.at[z - 1 : z + 1], out_ref.at[z - 1 : z + 1], out_sems.at[z // 2]
-                    )
-                )
-                sends[-1].start()
+            k = place_of(z)
+            y_ref[k] = (acc_ref[z] + part).astype(BF16)
+            sends.append(pltpu.make_async_copy(y_ref.at[k], out_ref.at[k], out_sems.at[k]))
+            sends[-1].start()
     for send in sends:
         send.wait()
 
@@ -233,7 +234,7 @@
             pltpu.VMEM(shape, F32),
             pltpu.VMEM(shape, BF16),
             pltpu.SemaphoreType.DMA((8,)),
-            pltpu.SemaphoreType.DMA((HID // 2,)),
+            pltpu.SemaphoreType.DMA((HID,)),
         ],
         compiler_params=pltpu.CompilerParams(vmem_limit_bytes=16 << 20),
         name="down",
@@ -272,8 +273,11 @@
     )(block_experts.T, vm(parts))
 
 
-def exchange(x, axes):
-    return lax.all_to_all(x, axes, split_axis=0, concat_axis=0, tiled=True)
+def exchange(x, axes, listing=None):
+    return lax.all_to_all(x, axes, split_axis=0, concat_axis=0, axis_index_groups=listing, tiled=True)
+
+
+COLUMN = [sorted(range(HID), key=place_of)]
 
 
 def layer(tokens, norm_gain, route_weight, block_experts, w_gate, w_up, w_down):
@@ -304,11 +308,11 @@
     down_here = lax.dynamic_slice_in_dim(down_late, sec * part, part, 1)
     direct = [down_here, sent(down_here, 1), sent(down_away, 2), away_x]
     downs = [d for piece in direct for d in (piece, swapped(piece))]
-    wide = exchange(wide, "hid")
+    wide = exchange(wide, "hid", COLUMN)
     ready = prepared(wide)
     every = exchange(ready, SQUARE)
     act = exchange(gated(every, (gate0, up0, gate1, up1)), SQUARE)
-    back = exchange(homed(block_experts, exchange(lowered(act, downs), "hid")), GROUP)
+    back = exchange(homed(block_experts, exchange(lowered(act, downs), "hid", COLUMN)), GROUP)
     return jnp.sum(back.astype(F32) * factor[:, :, None], axis=0).astype(BF16)
 
 

time: 161 us -> 160 us (level)
  waiting for transfers between devices: 60.2 us -> 57 us
  starting transfers between devices: 38.7 us -> 41.1 us
    all_to_all x4, waiting for transfers between devices: 33.3 us -> 29.6 us  [exchange(): lax.all_to_all(x, axes, split_axis=0, concat_axis=0, axis_index_groups=li...]
    all_to_all x4, starting transfers between devices: 17 us -> 19.5 us  [exchange(): lax.all_to_all(x, axes, split_axis=0, concat_axis=0, axis_index_groups=li...]
where the time goes in v9:
time: 160 us; the launch traced here: 159 us
  waiting for transfers between devices  57 us (36%)
  blocking collectives  45.3 us (28%)
  starting transfers between devices  41.1 us (26%)
  Pallas kernels  11.6 us (7%)
  local copies, waits for them, and re-layouts  2.7 us (2%)
    all_to_all x2, blocking collectives, exchange(): lax.all_to_all(x, axes, split_axis=0, concat_axis=0, axis_index_groups=li...  45.3 us
    all_to_all x4, waiting for transfers between devices, exchange(): lax.all_to_all(x, axes, split_axis=0, concat_axis=0, axis_index_groups=li...  29.6 us
    ppermute x3, waiting for transfers between devices, sent(): return lax.ppermute(x, SQUARE, [(i, i ^ flip) for i in range(4)])  27.4 us
    all_to_all x4, starting transfers between devices, exchange(): lax.all_to_all(x, axes, split_axis=0, concat_axis=0, axis_index_groups=li...  19.5 us
    ppermute x6, starting transfers between devices, swapped(): return lax.ppermute(x, 'core', [(0, 1), (1, 0)])  12.5 us
    ppermute x3, starting transfers between devices, sent(): return lax.ppermute(x, SQUARE, [(i, i ^ flip) for i in range(4)])  9.19 us
    pallas_call x1, Pallas kernels, gated(): pl.pallas_call(gate_up_kernel, out_shape=pltpu.HBM((4, rows, 2 * ff), BF1...  3.59 us
    pallas_call x1, Pallas kernels, lowered(): pl.pallas_call(down_kernel, out_shape=pltpu.HBM(shape, BF16), in_specs=[V...  3.39 us
  transfers between devices with their start and end apart: 13, of which 5 were waited for; matrix products, arithmetic and copies ran while one was open for 1% of the time, Pallas kernels for 2%

profile of v9, /device:TPU:8, one launch (start us, length us, event | category | flops | bytes accessed | tf_op | source)
XLA Modules:
  0.0 158.8 jit_solution(14084363345033715702)
XLA Ops:
  0.8 18.7 %all_to_all.30.x_ref = bf16[8,32,256]{2,1,0:T(8,128)(2,1)S(1)} all-to-all(bf16[8,32,256]{2,1,0:T(8,128)(2,1)S(1)} %broadcast_in_dim.35), channel_id=1, replica_groups=mesh['sec'=2,'group'=8,'xlo'=2,'core'=2,'hid'=8] {'group'}, dimensions={0} | all-to-all | bytes 262144 | tf_op jit(solution)/shard_map/all_to_all | solution.py:277
  19.5 1.6 %shard_map.73 = bf16[8,136,256]{2,1,0:T(8,128)(2,1)} custom-call(s32[2,8]{1,0:T(2,128)} %bitcast.7, bf16[8,32,256]{2,1,0:T(8,128)(2,1)S(1)} %all_to_all.30.x_ref, bf16[256]{0:T(256)(128)(2,1)} %gain_hbm.1), custom_call_target="tpu_custom_call" | custom-call | tf_op jit(solution)/shard_map/pallas_call | solution.py:247
  21.2 26.6 %all_to_all.31.x_ref = bf16[8,136,256]{2,1,0:T(8,128)(2,1)S(1)} all-to-all(bf16[8,136,256]{2,1,0:T(8,128)(2,1)} %shard_map.73), channel_id=1, replica_groups={{7,0,1,2,3,4,5,6},{15,8,9,10,11,12,13,14},{23,16,17,18,19,20,21,22},{31..., dimensions={0} | all-to-all | bytes 1114112 | tf_op jit(solution)/shard_map/all_to_all | solution.py:277
  47.8 1.6 %prep.1 = bf16[4,1032,256]{2,1,0:T(8,128)(2,1)} custom-call(bf16[8,136,256]{2,1,0:T(8,128)(2,1)S(1)} %all_to_all.31.x_ref), custom_call_target="tpu_custom_call" | custom-call | tf_op jit(solution)/shard_map/prep/pallas_call | solution.py:193
  49.4 4.9 %all-to-all-start.2 = ((bf16[4,1032,256]{2,1,0:T(8,128)(2,1)}), bf16[4,1032,256]{2,1,0:T(8,128)(2,1)S(1)}, u32[]{:S(2)}, u32[]{:S(2)}) async-start(bf16[4,1032,256]{2,1,0:T(8,128)(2,1)} %prep.1), calls=%async_computation.2 | async-start | bytes 4227072 | tf_op jit(solution)/shard_map/all_to_all | solution.py:277
  54.4 1.9 %collective-permute-start = (bf16[4096,128]{1,0:T(8,128)(2,1)}, bf16[4096,128]{1,0:T(8,128)(2,1)}, u32[]{:S(2)}, u32[]{:S(2)}) collective-permute-start(bf16[4096,128]{1,0:T(8,128)(2,1)} %bitcast.9), channel_id=1, source_target_pairs={{0,8},{8,0},{1,9},{9,1},{2,10},{10,2},{3,11},{11,3},{4,12},{12,4},... | collective-permute-start | bytes 3145736 | tf_op jit(solution)/shard_map/ppermute | solution.py:296
  56.3 2.4 %collective-permute-start.1 = (bf16[4096,128]{1,0:T(8,128)(2,1)}, bf16[4096,128]{1,0:T(8,128)(2,1)}, u32[]{:S(2)}, u32[]{:S(2)}) collective-permute-start(bf16[4096,128]{1,0:T(8,128)(2,1)} %bitcast.11), channel_id=1, source_target_pairs={{0,8},{8,0},{1,9},{9,1},{2,10},{10,2},{3,11},{11,3},{4,12},{12,4},... | collective-permute-start | bytes 3145736 | tf_op jit(solution)/shard_map/ppermute | solution.py:296
  59.5 1.9 %collective-permute-start.5 = (bf16[128,2048]{1,0:T(8,128)(2,1)}, bf16[128,2048]{1,0:T(8,128)(2,1)}, u32[]{:S(2)}, u32[]{:S(2)}) collective-permute-start(bf16[128,2048]{1,0:T(8,128)(2,1)} %dynamic-slice_bitcast_fusion), channel_id=1, source_target_pairs={{0,256},{16,272},{256,0},{272,16},{1,257},{17,273},{257,1},{273,17... | collective-permute-start | bytes 1572872 | tf_op jit(solution)/shard_map/ppermute | solution.py:293
  61.5 4.8 %collective-permute-start.7 = (bf16[128,2048]{1,0:T(8,128)(2,1)}, bf16[128,2048]{1,0:T(8,128)(2,1)}, u32[]{:S(2)}, u32[]{:S(2)}) collective-permute-start(bf16[128,2048]{1,0:T(8,128)(2,1)} %dynamic-slice_bitcast_fusion), channel_id=1, source_target_pairs={{0,272},{16,256},{256,16},{272,0},{1,273},{17,257},{257,17},{273,1... | collective-permute-start | bytes 1572872 | tf_op jit(solution)/shard_map/ppermute | solution.py:293
  67.2 2.5 %collective-permute-start.3 = (bf16[128,2048]{1,0:T(8,128)(2,1)}, bf16[128,2048]{1,0:T(8,128)(2,1)}, u32[]{:S(2)}, u32[]{:S(2)}) collective-permute-start(bf16[128,2048]{1,0:T(8,128)(2,1)} %constant_dynamic-slice_fusion.refs_0_), channel_id=1, source_target_pairs={{0,16},{16,0},{256,272},{272,256},{1,17},{17,1},{257,273},{273,257... | collective-permute-start | bytes 1572872 | tf_op jit(solution)/shard_map/ppermute | solution.py:293
  69.6 20.5 %collective-permute-done.5.refs_4_ = bf16[128,2048]{1,0:T(8,128)(2,1)} collective-permute-done((bf16[128,2048]{1,0:T(8,128)(2,1)}, bf16[128,2048]{1,0:T(8,128)(2,1)}, u32[]{:S(2)}, u32[]{:S(2)}) %collective-permute-start.5) | collective-permute-done | bytes 524320 | tf_op jit(solution)/shard_map/ppermute | solution.py:293
  90.1 1.9 %collective-permute-start.2 = (bf16[128,2048]{1,0:T(8,128)(2,1)}, bf16[128,2048]{1,0:T(8,128)(2,1)}, u32[]{:S(2)}, u32[]{:S(2)}) collective-permute-start(bf16[128,2048]{1,0:T(8,128)(2,1)} %constant_dynamic-slice_fusion.refs_0_), channel_id=1, source_target_pairs={{0,8},{8,0},{1,9},{9,1},{2,10},{10,2},{3,11},{11,3},{4,12},{12,4},... | collective-permute-start | bytes 1572872 | tf_op jit(solution)/shard_map/ppermute | solution.py:296
  92.0 6.9 %collective-permute-done.7.refs_6_ = bf16[128,2048]{1,0:T(8,128)(2,1)} collective-permute-done((bf16[128,2048]{1,0:T(8,128)(2,1)}, bf16[128,2048]{1,0:T(8,128)(2,1)}, u32[]{:S(2)}, u32[]{:S(2)}) %collective-permute-start.7) | collective-permute-done | bytes 524320 | tf_op jit(solution)/shard_map/ppermute | solution.py:293
  98.9 1.9 %collective-permute-start.6 = (bf16[128,2048]{1,0:T(8,128)(2,1)}, bf16[128,2048]{1,0:T(8,128)(2,1)}, u32[]{:S(2)}, u32[]{:S(2)}) collective-permute-start(bf16[128,2048]{1,0:T(8,128)(2,1)} %collective-permute-done.5.refs_4_), channel_id=1, source_target_pairs={{0,8},{8,0},{1,9},{9,1},{2,10},{10,2},{3,11},{11,3},{4,12},{12,4},... | collective-permute-start | bytes 1572872 | tf_op jit(solution)/shard_map/ppermute | solution.py:296
  100.8 2.4 %collective-permute-start.8 = (bf16[128,2048]{1,0:T(8,128)(2,1)}, bf16[128,2048]{1,0:T(8,128)(2,1)}, u32[]{:S(2)}, u32[]{:S(2)}) collective-permute-start(bf16[128,2048]{1,0:T(8,128)(2,1)} %collective-permute-done.7.refs_6_), channel_id=1, source_target_pairs={{0,8},{8,0},{1,9},{9,1},{2,10},{10,2},{3,11},{11,3},{4,12},{12,4},... | collective-permute-start | bytes 1572872 | tf_op jit(solution)/shard_map/ppermute | solution.py:296
  103.3 1.9 %collective-permute-start.4 = (bf16[128,2048]{1,0:T(8,128)(2,1)}, bf16[128,2048]{1,0:T(8,128)(2,1)}, u32[]{:S(2)}, u32[]{:S(2)}) collective-permute-start(bf16[128,2048]{1,0:T(8,128)(2,1)} %collective-permute-done.3.refs_2_), channel_id=1, source_target_pairs={{0,8},{8,0},{1,9},{9,1},{2,10},{10,2},{3,11},{11,3},{4,12},{12,4},... | collective-permute-start | bytes 1572872 | tf_op jit(solution)/shard_map/ppermute | solution.py:296
  105.2 3.6 %gate_up.1 = bf16[4,128,256]{2,1,0:T(8,128)(2,1)} custom-call(bf16[4,1032,256]{2,1,0:T(8,128)(2,1)S(1)} %all-to-all-done.2.x_ref, bf16[4096,128]{1,0:T(8,128)(2,1)} %bitcast.10, bf16[4096,128]{1,0:T(8,128)(2,1)} %bitcast.12, bf16[4096,128]{1,0:T(8,128)(2,1)} %collective-permute-done.g1, bf16[4096,128]{1,0:T(8,128)(2,1)} %collective-permute-done.1.u1), custom_call_target="tpu_custom_call" | custom-call | tf_op jit(solution)/shard_map/gate_up/pallas_call | solution.py:208
  108.8 4.9 %all-to-all-start.3 = ((bf16[4,128,256]{2,1,0:T(8,128)(2,1)}), bf16[4,128,256]{2,1,0:T(8,128)(2,1)S(1)}, u32[]{:S(2)}, u32[]{:S(2)}) async-start(bf16[4,128,256]{2,1,0:T(8,128)(2,1)} %gate_up.1), calls=%async_computation.3 | async-start | bytes 524288 | tf_op jit(solution)/shard_map/all_to_all | solution.py:277
  113.7 5.5 %all-to-all-done.3.act_ref = bf16[4,128,256]{2,1,0:T(8,128)(2,1)S(1)} async-done(((bf16[4,128,256]{2,1,0:T(8,128)(2,1)}), bf16[4,128,256]{2,1,0:T(8,128)(2,1)S(1)}, u32[]{:S(2)}, u32[]{:S(2)}) %all-to-all-start.3) | async-done | bytes 262176 | tf_op jit(solution)/shard_map/all_to_all | solution.py:277
  119.2 3.4 %down.1 = bf16[8,128,256]{2,1,0:T(8,128)(2,1)} custom-call(bf16[4,128,256]{2,1,0:T(8,128)(2,1)S(1)} %all-to-all-done.3.act_ref, bf16[128,2048]{1,0:T(8,128)(2,1)} %constant_dynamic-slice_fusion.refs_0_, bf16[128,2048]{1,0:T(8,128)(2,1)} %collective-permute-done.2.refs_1_, bf16[128,2048]{1,0:T(8,128)(2,1)} %collective-permute-done.3.refs_2_, ...), custom_call_target="tpu_custom_call" | custom-call | tf_op jit(solution)/shard_map/down/pallas_call | solution.py:227
  122.6 6.0 %all-to-all-start.4 = ((bf16[8,128,256]{2,1,0:T(8,128)(2,1)}), bf16[8,128,256]{2,1,0:T(8,128)(2,1)S(1)}, u32[]{:S(2)}, u32[]{:S(2)}) async-start(bf16[8,128,256]{2,1,0:T(8,128)(2,1)} %down.1), calls=%async_computation.4 | async-start | bytes 1048576 | tf_op jit(solution)/shard_map/all_to_all | solution.py:277
  128.8 13.9 %all-to-all-done.4.x_ref = bf16[8,128,256]{2,1,0:T(8,128)(2,1)S(1)} async-done(((bf16[8,128,256]{2,1,0:T(8,128)(2,1)}), bf16[8,128,256]{2,1,0:T(8,128)(2,1)S(1)}, u32[]{:S(2)}, u32[]{:S(2)}) %all-to-all-start.4) | async-done | bytes 524320 | tf_op jit(solution)/shard_map/all_to_all | solution.py:277
  144.1 3.7 %all-to-all-start.5 = ((bf16[8,32,256]{2,1,0:T(8,128)(2,1)}), bf16[8,32,256]{2,1,0:T(8,128)(2,1)S(1)}, u32[]{:S(2)}, u32[]{:S(2)}) async-start(bf16[8,32,256]{2,1,0:T(8,128)(2,1)} %home.1), calls=%async_computation.5 | async-start | bytes 262144 | tf_op jit(solution)/shard_map/all_to_all | solution.py:277
  148.0 10.1 %all-to-all-done.5 = bf16[8,32,256]{2,1,0:T(8,128)(2,1)S(1)} async-done(((bf16[8,32,256]{2,1,0:T(8,128)(2,1)}), bf16[8,32,256]{2,1,0:T(8,128)(2,1)S(1)}, u32[]{:S(2)}, u32[]{:S(2)}) %all-to-all-start.5) | async-done | bytes 131104 | tf_op jit(solution)/shard_map/all_to_all | solution.py:277
  (22 shorter events, 4.9 us)
Async XLA Ops:
  0.0 58.7 %copy-start = (bf16[1,128,4096]{2,1,0:T(8,128)(2,1)S(1)}, bf16[1,128,4096]{2,1,0:T(8,128)(2,1)}, u32[]{:S(2)}) copy-start(bf16[1,128,4096]{2,1,0:T(8,128)(2,1)} %param.13) | copy-start | bytes 3145732
  49.4 55.8 %all-to-all-start.2 = ((bf16[4,1032,256]{2,1,0:T(8,128)(2,1)}), bf16[4,1032,256]{2,1,0:T(8,128)(2,1)S(1)}, u32[]{:S(2)}, u32[]{:S(2)}) async-start(bf16[4,1032,256]{2,1,0:T(8,128)(2,1)} %prep.1), calls=%async_computation.2 | async-start | bytes 4227072 | tf_op jit(solution)/shard_map/all_to_all | solution.py:277
  54.4 48.9 %collective-permute-start = (bf16[4096,128]{1,0:T(8,128)(2,1)}, bf16[4096,128]{1,0:T(8,128)(2,1)}, u32[]{:S(2)}, u32[]{:S(2)}) collective-permute-start(bf16[4096,128]{1,0:T(8,128)(2,1)} %bitcast.9), channel_id=1, source_target_pairs={{0,8},{8,0},{1,9},{9,1},{2,10},{10,2},{3,11},{11,3},{4,12},{12,4},... | collective-permute-start | bytes 3145736 | tf_op jit(solution)/shard_map/ppermute | solution.py:296
  56.3 48.9 %collective-permute-start.1 = (bf16[4096,128]{1,0:T(8,128)(2,1)}, bf16[4096,128]{1,0:T(8,128)(2,1)}, u32[]{:S(2)}, u32[]{:S(2)}) collective-permute-start(bf16[4096,128]{1,0:T(8,128)(2,1)} %bitcast.11), channel_id=1, source_target_pairs={{0,8},{8,0},{1,9},{9,1},{2,10},{10,2},{3,11},{11,3},{4,12},{12,4},... | collective-permute-start | bytes 3145736 | tf_op jit(solution)/shard_map/ppermute | solution.py:296
  59.5 30.6 %collective-permute-start.5 = (bf16[128,2048]{1,0:T(8,128)(2,1)}, bf16[128,2048]{1,0:T(8,128)(2,1)}, u32[]{:S(2)}, u32[]{:S(2)}) collective-permute-start(bf16[128,2048]{1,0:T(8,128)(2,1)} %dynamic-slice_bitcast_fusion), channel_id=1, source_target_pairs={{0,256},{16,272},{256,0},{272,16},{1,257},{17,273},{257,1},{273,17... | collective-permute-start | bytes 1572872 | tf_op jit(solution)/shard_map/ppermute | solution.py:293
  61.5 37.4 %collective-permute-start.7 = (bf16[128,2048]{1,0:T(8,128)(2,1)}, bf16[128,2048]{1,0:T(8,128)(2,1)}, u32[]{:S(2)}, u32[]{:S(2)}) collective-permute-start(bf16[128,2048]{1,0:T(8,128)(2,1)} %dynamic-slice_bitcast_fusion), channel_id=1, source_target_pairs={{0,272},{16,256},{256,16},{272,0},{1,273},{17,257},{257,17},{273,1... | collective-permute-start | bytes 1572872 | tf_op jit(solution)/shard_map/ppermute | solution.py:293
  67.2 33.7 %collective-permute-start.3 = (bf16[128,2048]{1,0:T(8,128)(2,1)}, bf16[128,2048]{1,0:T(8,128)(2,1)}, u32[]{:S(2)}, u32[]{:S(2)}) collective-permute-start(bf16[128,2048]{1,0:T(8,128)(2,1)} %constant_dynamic-slice_fusion.refs_0_), channel_id=1, source_target_pairs={{0,16},{16,0},{256,272},{272,256},{1,17},{17,1},{257,273},{273,257... | collective-permute-start | bytes 1572872 | tf_op jit(solution)/shard_map/ppermute | solution.py:293
  90.1 23.6 %collective-permute-start.2 = (bf16[128,2048]{1,0:T(8,128)(2,1)}, bf16[128,2048]{1,0:T(8,128)(2,1)}, u32[]{:S(2)}, u32[]{:S(2)}) collective-permute-start(bf16[128,2048]{1,0:T(8,128)(2,1)} %constant_dynamic-slice_fusion.refs_0_), channel_id=1, source_target_pairs={{0,8},{8,0},{1,9},{9,1},{2,10},{10,2},{3,11},{11,3},{4,12},{12,4},... | collective-permute-start | bytes 1572872 | tf_op jit(solution)/shard_map/ppermute | solution.py:296
  98.9 14.8 %collective-permute-start.6 = (bf16[128,2048]{1,0:T(8,128)(2,1)}, bf16[128,2048]{1,0:T(8,128)(2,1)}, u32[]{:S(2)}, u32[]{:S(2)}) collective-permute-start(bf16[128,2048]{1,0:T(8,128)(2,1)} %collective-permute-done.5.refs_4_), channel_id=1, source_target_pairs={{0,8},{8,0},{1,9},{9,1},{2,10},{10,2},{3,11},{11,3},{4,12},{12,4},... | collective-permute-start | bytes 1572872 | tf_op jit(solution)/shard_map/ppermute | solution.py:296
  100.8 12.9 %collective-permute-start.8 = (bf16[128,2048]{1,0:T(8,128)(2,1)}, bf16[128,2048]{1,0:T(8,128)(2,1)}, u32[]{:S(2)}, u32[]{:S(2)}) collective-permute-start(bf16[128,2048]{1,0:T(8,128)(2,1)} %collective-permute-done.7.refs_6_), channel_id=1, source_target_pairs={{0,8},{8,0},{1,9},{9,1},{2,10},{10,2},{3,11},{11,3},{4,12},{12,4},... | collective-permute-start | bytes 1572872 | tf_op jit(solution)/shard_map/ppermute | solution.py:296
  103.3 10.4 %collective-permute-start.4 = (bf16[128,2048]{1,0:T(8,128)(2,1)}, bf16[128,2048]{1,0:T(8,128)(2,1)}, u32[]{:S(2)}, u32[]{:S(2)}) collective-permute-start(bf16[128,2048]{1,0:T(8,128)(2,1)} %collective-permute-done.3.refs_2_), channel_id=1, source_target_pairs={{0,8},{8,0},{1,9},{9,1},{2,10},{10,2},{3,11},{11,3},{4,12},{12,4},... | collective-permute-start | bytes 1572872 | tf_op jit(solution)/shard_map/ppermute | solution.py:296
  108.8 10.4 %all-to-all-start.3 = ((bf16[4,128,256]{2,1,0:T(8,128)(2,1)}), bf16[4,128,256]{2,1,0:T(8,128)(2,1)S(1)}, u32[]{:S(2)}, u32[]{:S(2)}) async-start(bf16[4,128,256]{2,1,0:T(8,128)(2,1)} %gate_up.1), calls=%async_computation.3 | async-start | bytes 524288 | tf_op jit(solution)/shard_map/all_to_all | solution.py:277
  113.7 14.9 %copy-start.1 = (s32[8,2]{0,1:T(2,128)S(1)}, s32[8,2]{0,1:T(2,128)}, u32[]{:S(2)}) copy-start(s32[8,2]{0,1:T(2,128)} %param.10) | copy-start | bytes 196
  113.7 34.2 %copy-start.2 = (f32[32,2]{0,1:T(2,128)S(1)}, f32[32,2]{0,1:T(2,128)}, u32[]{:S(2)}) copy-start(f32[32,2]{0,1:T(2,128)} %param.9) | copy-start | bytes 772
  122.6 20.1 %all-to-all-start.4 = ((bf16[8,128,256]{2,1,0:T(8,128)(2,1)}), bf16[8,128,256]{2,1,0:T(8,128)(2,1)S(1)}, u32[]{:S(2)}, u32[]{:S(2)}) async-start(bf16[8,128,256]{2,1,0:T(8,128)(2,1)} %down.1), calls=%async_computation.4 | async-start | bytes 1048576 | tf_op jit(solution)/shard_map/all_to_all | solution.py:277
  144.1 14.0 %all-to-all-start.5 = ((bf16[8,32,256]{2,1,0:T(8,128)(2,1)}), bf16[8,32,256]{2,1,0:T(8,128)(2,1)S(1)}, u32[]{:S(2)}, u32[]{:S(2)}) async-start(bf16[8,32,256]{2,1,0:T(8,128)(2,1)} %home.1), calls=%async_computation.5 | async-start | bytes 262144 | tf_op jit(solution)/shard_map/all_to_all | solution.py:277

commit v10 on v9

--- a/solution.py
+++ b/solution.py
@@ -12,7 +12,8 @@
 F32 = jnp.float32
 BF16 = jnp.bfloat16
 
-GROUP = ("group",)
+FAR = 5
+GROUP = "group"
 SQUARE = ("sec", "xlo")
 
 
@@ -159,7 +160,7 @@
     y_ref[MOST * rows :, :] = jnp.broadcast_to(gain_ref[...].astype(F32)[None, :], (8, w)).astype(BF16)
     block_of_slot, _ = routed(experts_ref, lax.axis_index("group"))
     for k, block in enumerate(block_of_slot):
-        y_ref[k * rows : (k + 1) * rows, :] = x_ref[block]
+        y_ref[k * rows : (k + 1) * rows, :] = x_ref[block ^ FAR]
     sent_all([pltpu.make_async_copy(y_ref, out_ref.at[j], sems.at[j]) for j in range(out_ref.shape[0])])
 
 
@@ -171,7 +172,9 @@
         for z in range(1, x_ref.shape[0]):
             total = total + x_ref[z, k * rows : (k + 1) * rows, :].astype(F32)
         y_ref[k] = total.astype(BF16)
-    sent_all([pltpu.make_async_copy(y_ref.at[slot_of_block[b]], out_ref.at[b], sems.at[b]) for b in range(blocks)])
+    sent_all(
+        [pltpu.make_async_copy(y_ref.at[slot_of_block[b]], out_ref.at[b ^ FAR], sems.at[b]) for b in range(blocks)]
+    )
 
 
 SM = pl.BlockSpec(memory_space=pltpu.SMEM)
@@ -277,6 +280,7 @@
     return lax.all_to_all(x, axes, split_axis=0, concat_axis=0, axis_index_groups=listing, tiled=True)
 
 
+ACROSS = [[g ^ FAR for g in range(EXPERTS)]]
 COLUMN = [sorted(range(HID), key=place_of)]
 
 
@@ -299,10 +303,10 @@
     gate1, up1 = swapped(gate0), swapped(up0)
 
     mine = jnp.take(block_experts, lax.axis_index("group"), axis=0, mode="clip")
-    named = mine[None, :] == jnp.arange(EXPERTS, dtype=jnp.int32)[:, None]
+    named = mine[None, :] == (jnp.arange(EXPERTS, dtype=jnp.int32) ^ FAR)[:, None]
     factor = jnp.sum(jnp.where(named[:, None, :], route_weight[None], 0.0), axis=2)
 
-    blocks = exchange(jnp.broadcast_to(tokens[None], (groups, rows, w)), GROUP)
+    blocks = exchange(jnp.broadcast_to(tokens[None], (groups, rows, w)), GROUP, ACROSS)
     wide = picked_rows(block_experts, blocks, norm_gain, n_hid)
     blocks, down_late = lax.optimization_barrier((blocks, down0))
     down_here = lax.dynamic_slice_in_dim(down_late, sec * part, part, 1)
@@ -312,7 +316,7 @@
     ready = prepared(wide)
     every = exchange(ready, SQUARE)
     act = exchange(gated(every, (gate0, up0, gate1, up1)), SQUARE)
-    back = exchange(homed(block_experts, exchange(lowered(act, downs), "hid", COLUMN)), GROUP)
+    back = exchange(homed(block_experts, exchange(lowered(act, downs), "hid", COLUMN)), GROUP, ACROSS)
     return jnp.sum(back.astype(F32) * factor[:, :, None], axis=0).astype(BF16)
 
 

time: 160 us -> 157 us (0.981)
  the two profiles are of different devices: /device:TPU:8 before, /device:TPU:6 now
where the time goes in v10:
time: 157 us; the launch traced here: 156 us
  waiting for transfers between devices  52.3 us (33%)
  starting transfers between devices  47.2 us (30%)
  blocking collectives  40.9 us (26%)
  Pallas kernels  11.6 us (7%)
  local copies, waits for them, and re-layouts  2.7 us (2%)
    all_to_all x2, blocking collectives, exchange(): lax.all_to_all(x, axes, split_axis=0, concat_axis=0, axis_index_groups=li...  40.9 us
    ppermute x3, waiting for transfers between devices, sent(): return lax.ppermute(x, SQUARE, [(i, i ^ flip) for i in range(4)])  27.5 us
    all_to_all x4, starting transfers between devices, exchange(): lax.all_to_all(x, axes, split_axis=0, concat_axis=0, axis_index_groups=li...  25.5 us
    all_to_all x4, waiting for transfers between devices, exchange(): lax.all_to_all(x, axes, split_axis=0, concat_axis=0, axis_index_groups=li...  24.7 us
    ppermute x6, starting transfers between devices, swapped(): return lax.ppermute(x, 'core', [(0, 1), (1, 0)])  12.5 us
    ppermute x3, starting transfers between devices, sent(): return lax.ppermute(x, SQUARE, [(i, i ^ flip) for i in range(4)])  9.19 us
    pallas_call x1, Pallas kernels, gated(): pl.pallas_call(gate_up_kernel, out_shape=pltpu.HBM((4, rows, 2 * ff), BF1...  3.59 us
    pallas_call x1, Pallas kernels, lowered(): pl.pallas_call(down_kernel, out_shape=pltpu.HBM(shape, BF16), in_specs=[V...  3.39 us
  transfers between devices with their start and end apart: 13, of which 5 were waited for; matrix products, arithmetic and copies ran while one was open for 1% of the time, Pallas kernels for 2%

profile of v10, /device:TPU:6, one launch (start us, length us, event | category | flops | bytes accessed | tf_op | source)
XLA Modules:
  0.0 155.7 jit_solution(6610531434357484544)
XLA Ops:
  0.8 14.1 %all_to_all.30.x_ref = bf16[8,32,256]{2,1,0:T(8,128)(2,1)S(1)} all-to-all(bf16[8,32,256]{2,1,0:T(8,128)(2,1)S(1)} %broadcast_in_dim.35), channel_id=1, replica_groups={{160,128,224,192,32,0,96,64},{161,129,225,193,33,1,97,65},{162,130,226,..., dimensions={0} | all-to-all | bytes 262144 | tf_op jit(solution)/shard_map/all_to_all | solution.py:280
  14.9 1.6 %shard_map.73 = bf16[8,136,256]{2,1,0:T(8,128)(2,1)} custom-call(s32[2,8]{1,0:T(2,128)} %bitcast.7, bf16[8,32,256]{2,1,0:T(8,128)(2,1)S(1)} %all_to_all.30.x_ref, bf16[256]{0:T(256)(128)(2,1)} %gain_hbm.1), custom_call_target="tpu_custom_call" | custom-call | tf_op jit(solution)/shard_map/pallas_call | solution.py:250
  16.6 26.8 %all_to_all.31.x_ref = bf16[8,136,256]{2,1,0:T(8,128)(2,1)S(1)} all-to-all(bf16[8,136,256]{2,1,0:T(8,128)(2,1)} %shard_map.73), channel_id=1, replica_groups={{7,0,1,2,3,4,5,6},{15,8,9,10,11,12,13,14},{23,16,17,18,19,20,21,22},{31..., dimensions={0} | all-to-all | bytes 1114112 | tf_op jit(solution)/shard_map/all_to_all | solution.py:280
  43.4 1.6 %prep.1 = bf16[4,1032,256]{2,1,0:T(8,128)(2,1)} custom-call(bf16[8,136,256]{2,1,0:T(8,128)(2,1)S(1)} %all_to_all.31.x_ref), custom_call_target="tpu_custom_call" | custom-call | tf_op jit(solution)/shard_map/prep/pallas_call | solution.py:196
  45.0 4.8 %all-to-all-start.2 = ((bf16[4,1032,256]{2,1,0:T(8,128)(2,1)}), bf16[4,1032,256]{2,1,0:T(8,128)(2,1)S(1)}, u32[]{:S(2)}, u32[]{:S(2)}) async-start(bf16[4,1032,256]{2,1,0:T(8,128)(2,1)} %prep.1), calls=%async_computation.2 | async-start | bytes 4227072 | tf_op jit(solution)/shard_map/all_to_all | solution.py:280
  49.8 1.9 %collective-permute-start = (bf16[4096,128]{1,0:T(8,128)(2,1)}, bf16[4096,128]{1,0:T(8,128)(2,1)}, u32[]{:S(2)}, u32[]{:S(2)}) collective-permute-start(bf16[4096,128]{1,0:T(8,128)(2,1)} %bitcast.9), channel_id=1, source_target_pairs={{0,8},{8,0},{1,9},{9,1},{2,10},{10,2},{3,11},{11,3},{4,12},{12,4},... | collective-permute-start | bytes 3145736 | tf_op jit(solution)/shard_map/ppermute | solution.py:300
  51.7 2.4 %collective-permute-start.1 = (bf16[4096,128]{1,0:T(8,128)(2,1)}, bf16[4096,128]{1,0:T(8,128)(2,1)}, u32[]{:S(2)}, u32[]{:S(2)}) collective-permute-start(bf16[4096,128]{1,0:T(8,128)(2,1)} %bitcast.11), channel_id=1, source_target_pairs={{0,8},{8,0},{1,9},{9,1},{2,10},{10,2},{3,11},{11,3},{4,12},{12,4},... | collective-permute-start | bytes 3145736 | tf_op jit(solution)/shard_map/ppermute | solution.py:300
  55.0 3.4 %collective-permute-start.5 = (bf16[128,2048]{1,0:T(8,128)(2,1)}, bf16[128,2048]{1,0:T(8,128)(2,1)}, u32[]{:S(2)}, u32[]{:S(2)}) collective-permute-start(bf16[128,2048]{1,0:T(8,128)(2,1)} %dynamic-slice_bitcast_fusion), channel_id=1, source_target_pairs={{0,256},{16,272},{256,0},{272,16},{1,257},{17,273},{257,1},{273,17... | collective-permute-start | bytes 1572872 | tf_op jit(solution)/shard_map/ppermute | solution.py:297
  58.4 2.0 %collective-permute-start.7 = (bf16[128,2048]{1,0:T(8,128)(2,1)}, bf16[128,2048]{1,0:T(8,128)(2,1)}, u32[]{:S(2)}, u32[]{:S(2)}) collective-permute-start(bf16[128,2048]{1,0:T(8,128)(2,1)} %dynamic-slice_bitcast_fusion), channel_id=1, source_target_pairs={{0,272},{16,256},{256,16},{272,0},{1,273},{17,257},{257,17},{273,1... | collective-permute-start | bytes 1572872 | tf_op jit(solution)/shard_map/ppermute | solution.py:297
  61.2 3.9 %collective-permute-start.3 = (bf16[128,2048]{1,0:T(8,128)(2,1)}, bf16[128,2048]{1,0:T(8,128)(2,1)}, u32[]{:S(2)}, u32[]{:S(2)}) collective-permute-start(bf16[128,2048]{1,0:T(8,128)(2,1)} %constant_dynamic-slice_fusion.refs_0_), channel_id=1, source_target_pairs={{0,16},{16,0},{256,272},{272,256},{1,17},{17,1},{257,273},{273,257... | collective-permute-start | bytes 1572872 | tf_op jit(solution)/shard_map/ppermute | solution.py:297
  65.1 21.9 %collective-permute-done.5.refs_4_ = bf16[128,2048]{1,0:T(8,128)(2,1)} collective-permute-done((bf16[128,2048]{1,0:T(8,128)(2,1)}, bf16[128,2048]{1,0:T(8,128)(2,1)}, u32[]{:S(2)}, u32[]{:S(2)}) %collective-permute-start.5) | collective-permute-done | bytes 524320 | tf_op jit(solution)/shard_map/ppermute | solution.py:297
  87.0 1.9 %collective-permute-start.2 = (bf16[128,2048]{1,0:T(8,128)(2,1)}, bf16[128,2048]{1,0:T(8,128)(2,1)}, u32[]{:S(2)}, u32[]{:S(2)}) collective-permute-start(bf16[128,2048]{1,0:T(8,128)(2,1)} %constant_dynamic-slice_fusion.refs_0_), channel_id=1, source_target_pairs={{0,8},{8,0},{1,9},{9,1},{2,10},{10,2},{3,11},{11,3},{4,12},{12,4},... | collective-permute-start | bytes 1572872 | tf_op jit(solution)/shard_map/ppermute | solution.py:300
  88.9 5.6 %collective-permute-done.7.refs_6_ = bf16[128,2048]{1,0:T(8,128)(2,1)} collective-permute-done((bf16[128,2048]{1,0:T(8,128)(2,1)}, bf16[128,2048]{1,0:T(8,128)(2,1)}, u32[]{:S(2)}, u32[]{:S(2)}) %collective-permute-start.7) | collective-permute-done | bytes 524320 | tf_op jit(solution)/shard_map/ppermute | solution.py:297
  94.5 1.9 %collective-permute-start.6 = (bf16[128,2048]{1,0:T(8,128)(2,1)}, bf16[128,2048]{1,0:T(8,128)(2,1)}, u32[]{:S(2)}, u32[]{:S(2)}) collective-permute-start(bf16[128,2048]{1,0:T(8,128)(2,1)} %collective-permute-done.5.refs_4_), channel_id=1, source_target_pairs={{0,8},{8,0},{1,9},{9,1},{2,10},{10,2},{3,11},{11,3},{4,12},{12,4},... | collective-permute-start | bytes 1572872 | tf_op jit(solution)/shard_map/ppermute | solution.py:300
  96.4 2.4 %collective-permute-start.8 = (bf16[128,2048]{1,0:T(8,128)(2,1)}, bf16[128,2048]{1,0:T(8,128)(2,1)}, u32[]{:S(2)}, u32[]{:S(2)}) collective-permute-start(bf16[128,2048]{1,0:T(8,128)(2,1)} %collective-permute-done.7.refs_6_), channel_id=1, source_target_pairs={{0,8},{8,0},{1,9},{9,1},{2,10},{10,2},{3,11},{11,3},{4,12},{12,4},... | collective-permute-start | bytes 1572872 | tf_op jit(solution)/shard_map/ppermute | solution.py:300
  98.9 1.9 %collective-permute-start.4 = (bf16[128,2048]{1,0:T(8,128)(2,1)}, bf16[128,2048]{1,0:T(8,128)(2,1)}, u32[]{:S(2)}, u32[]{:S(2)}) collective-permute-start(bf16[128,2048]{1,0:T(8,128)(2,1)} %collective-permute-done.3.refs_2_), channel_id=1, source_target_pairs={{0,8},{8,0},{1,9},{9,1},{2,10},{10,2},{3,11},{11,3},{4,12},{12,4},... | collective-permute-start | bytes 1572872 | tf_op jit(solution)/shard_map/ppermute | solution.py:300
  100.8 3.6 %gate_up.1 = bf16[4,128,256]{2,1,0:T(8,128)(2,1)} custom-call(bf16[4,1032,256]{2,1,0:T(8,128)(2,1)S(1)} %all-to-all-done.2.x_ref, bf16[4096,128]{1,0:T(8,128)(2,1)} %bitcast.10, bf16[4096,128]{1,0:T(8,128)(2,1)} %bitcast.12, bf16[4096,128]{1,0:T(8,128)(2,1)} %collective-permute-done.g1, bf16[4096,128]{1,0:T(8,128)(2,1)} %collective-permute-done.1.u1), custom_call_target="tpu_custom_call" | custom-call | tf_op jit(solution)/shard_map/gate_up/pallas_call | solution.py:211
  104.4 4.8 %all-to-all-start.3 = ((bf16[4,128,256]{2,1,0:T(8,128)(2,1)}), bf16[4,128,256]{2,1,0:T(8,128)(2,1)S(1)}, u32[]{:S(2)}, u32[]{:S(2)}) async-start(bf16[4,128,256]{2,1,0:T(8,128)(2,1)} %gate_up.1), calls=%async_computation.3 | async-start | bytes 524288 | tf_op jit(solution)/shard_map/all_to_all | solution.py:280
  109.3 5.5 %all-to-all-done.3.act_ref = bf16[4,128,256]{2,1,0:T(8,128)(2,1)S(1)} async-done(((bf16[4,128,256]{2,1,0:T(8,128)(2,1)}), bf16[4,128,256]{2,1,0:T(8,128)(2,1)S(1)}, u32[]{:S(2)}, u32[]{:S(2)}) %all-to-all-start.3) | async-done | bytes 262176 | tf_op jit(solution)/shard_map/all_to_all | solution.py:280
  114.8 3.4 %down.1 = bf16[8,128,256]{2,1,0:T(8,128)(2,1)} custom-call(bf16[4,128,256]{2,1,0:T(8,128)(2,1)S(1)} %all-to-all-done.3.act_ref, bf16[128,2048]{1,0:T(8,128)(2,1)} %constant_dynamic-slice_fusion.refs_0_, bf16[128,2048]{1,0:T(8,128)(2,1)} %collective-permute-done.2.refs_1_, bf16[128,2048]{1,0:T(8,128)(2,1)} %collective-permute-done.3.refs_2_, ...), custom_call_target="tpu_custom_call" | custom-call | tf_op jit(solution)/shard_map/down/pallas_call | solution.py:230
  118.2 6.0 %all-to-all-start.4 = ((bf16[8,128,256]{2,1,0:T(8,128)(2,1)}), bf16[8,128,256]{2,1,0:T(8,128)(2,1)S(1)}, u32[]{:S(2)}, u32[]{:S(2)}) async-start(bf16[8,128,256]{2,1,0:T(8,128)(2,1)} %down.1), calls=%async_computation.4 | async-start | bytes 1048576 | tf_op jit(solution)/shard_map/all_to_all | solution.py:280
  124.4 13.6 %all-to-all-done.4.x_ref = bf16[8,128,256]{2,1,0:T(8,128)(2,1)S(1)} async-done(((bf16[8,128,256]{2,1,0:T(8,128)(2,1)}), bf16[8,128,256]{2,1,0:T(8,128)(2,1)S(1)}, u32[]{:S(2)}, u32[]{:S(2)}) %all-to-all-start.4) | async-done | bytes 524320 | tf_op jit(solution)/shard_map/all_to_all | solution.py:280
  139.4 9.9 %all-to-all-start.5 = ((bf16[8,32,256]{2,1,0:T(8,128)(2,1)}), bf16[8,32,256]{2,1,0:T(8,128)(2,1)S(1)}, u32[]{:S(2)}, u32[]{:S(2)}) async-start(bf16[8,32,256]{2,1,0:T(8,128)(2,1)} %home.1), calls=%async_computation.5 | async-start | bytes 262144 | tf_op jit(solution)/shard_map/all_to_all | solution.py:280
  149.4 5.6 %all-to-all-done.5 = bf16[8,32,256]{2,1,0:T(8,128)(2,1)S(1)} async-done(((bf16[8,32,256]{2,1,0:T(8,128)(2,1)}), bf16[8,32,256]{2,1,0:T(8,128)(2,1)S(1)}, u32[]{:S(2)}, u32[]{:S(2)}) %all-to-all-start.5) | async-done | bytes 131104 | tf_op jit(solution)/shard_map/all_to_all | solution.py:280
  (23 shorter events, 4.9 us)
Async XLA Ops:
  0.0 54.2 %copy-start = (bf16[1,128,4096]{2,1,0:T(8,128)(2,1)S(1)}, bf16[1,128,4096]{2,1,0:T(8,128)(2,1)}, u32[]{:S(2)}) copy-start(bf16[1,128,4096]{2,1,0:T(8,128)(2,1)} %param.13) | copy-start | bytes 3145732
  45.0 55.8 %all-to-all-start.2 = ((bf16[4,1032,256]{2,1,0:T(8,128)(2,1)}), bf16[4,1032,256]{2,1,0:T(8,128)(2,1)S(1)}, u32[]{:S(2)}, u32[]{:S(2)}) async-start(bf16[4,1032,256]{2,1,0:T(8,128)(2,1)} %prep.1), calls=%async_computation.2 | async-start | bytes 4227072 | tf_op jit(solution)/shard_map/all_to_all | solution.py:280
  49.8 49.0 %collective-permute-start = (bf16[4096,128]{1,0:T(8,128)(2,1)}, bf16[4096,128]{1,0:T(8,128)(2,1)}, u32[]{:S(2)}, u32[]{:S(2)}) collective-permute-start(bf16[4096,128]{1,0:T(8,128)(2,1)} %bitcast.9), channel_id=1, source_target_pairs={{0,8},{8,0},{1,9},{9,1},{2,10},{10,2},{3,11},{11,3},{4,12},{12,4},... | collective-permute-start | bytes 3145736 | tf_op jit(solution)/shard_map/ppermute | solution.py:300
  51.7 49.1 %collective-permute-start.1 = (bf16[4096,128]{1,0:T(8,128)(2,1)}, bf16[4096,128]{1,0:T(8,128)(2,1)}, u32[]{:S(2)}, u32[]{:S(2)}) collective-permute-start(bf16[4096,128]{1,0:T(8,128)(2,1)} %bitcast.11), channel_id=1, source_target_pairs={{0,8},{8,0},{1,9},{9,1},{2,10},{10,2},{3,11},{11,3},{4,12},{12,4},... | collective-permute-start | bytes 3145736 | tf_op jit(solution)/shard_map/ppermute | solution.py:300
  55.0 32.0 %collective-permute-start.5 = (bf16[128,2048]{1,0:T(8,128)(2,1)}, bf16[128,2048]{1,0:T(8,128)(2,1)}, u32[]{:S(2)}, u32[]{:S(2)}) collective-permute-start(bf16[128,2048]{1,0:T(8,128)(2,1)} %dynamic-slice_bitcast_fusion), channel_id=1, source_target_pairs={{0,256},{16,272},{256,0},{272,16},{1,257},{17,273},{257,1},{273,17... | collective-permute-start | bytes 1572872 | tf_op jit(solution)/shard_map/ppermute | solution.py:297
  58.4 36.1 %collective-permute-start.7 = (bf16[128,2048]{1,0:T(8,128)(2,1)}, bf16[128,2048]{1,0:T(8,128)(2,1)}, u32[]{:S(2)}, u32[]{:S(2)}) collective-permute-start(bf16[128,2048]{1,0:T(8,128)(2,1)} %dynamic-slice_bitcast_fusion), channel_id=1, source_target_pairs={{0,272},{16,256},{256,16},{272,0},{1,273},{17,257},{257,17},{273,1... | collective-permute-start | bytes 1572872 | tf_op jit(solution)/shard_map/ppermute | solution.py:297
  61.2 35.2 %collective-permute-start.3 = (bf16[128,2048]{1,0:T(8,128)(2,1)}, bf16[128,2048]{1,0:T(8,128)(2,1)}, u32[]{:S(2)}, u32[]{:S(2)}) collective-permute-start(bf16[128,2048]{1,0:T(8,128)(2,1)} %constant_dynamic-slice_fusion.refs_0_), channel_id=1, source_target_pairs={{0,16},{16,0},{256,272},{272,256},{1,17},{17,1},{257,273},{273,257... | collective-permute-start | bytes 1572872 | tf_op jit(solution)/shard_map/ppermute | solution.py:297
  87.0 22.3 %collective-permute-start.2 = (bf16[128,2048]{1,0:T(8,128)(2,1)}, bf16[128,2048]{1,0:T(8,128)(2,1)}, u32[]{:S(2)}, u32[]{:S(2)}) collective-permute-start(bf16[128,2048]{1,0:T(8,128)(2,1)} %constant_dynamic-slice_fusion.refs_0_), channel_id=1, source_target_pairs={{0,8},{8,0},{1,9},{9,1},{2,10},{10,2},{3,11},{11,3},{4,12},{12,4},... | collective-permute-start | bytes 1572872 | tf_op jit(solution)/shard_map/ppermute | solution.py:300
  94.5 14.8 %collective-permute-start.6 = (bf16[128,2048]{1,0:T(8,128)(2,1)}, bf16[128,2048]{1,0:T(8,128)(2,1)}, u32[]{:S(2)}, u32[]{:S(2)}) collective-permute-start(bf16[128,2048]{1,0:T(8,128)(2,1)} %collective-permute-done.5.refs_4_), channel_id=1, source_target_pairs={{0,8},{8,0},{1,9},{9,1},{2,10},{10,2},{3,11},{11,3},{4,12},{12,4},... | collective-permute-start | bytes 1572872 | tf_op jit(solution)/shard_map/ppermute | solution.py:300
  96.4 12.8 %collective-permute-start.8 = (bf16[128,2048]{1,0:T(8,128)(2,1)}, bf16[128,2048]{1,0:T(8,128)(2,1)}, u32[]{:S(2)}, u32[]{:S(2)}) collective-permute-start(bf16[128,2048]{1,0:T(8,128)(2,1)} %collective-permute-done.7.refs_6_), channel_id=1, source_target_pairs={{0,8},{8,0},{1,9},{9,1},{2,10},{10,2},{3,11},{11,3},{4,12},{12,4},... | collective-permute-start | bytes 1572872 | tf_op jit(solution)/shard_map/ppermute | solution.py:300
  98.9 10.4 %collective-permute-start.4 = (bf16[128,2048]{1,0:T(8,128)(2,1)}, bf16[128,2048]{1,0:T(8,128)(2,1)}, u32[]{:S(2)}, u32[]{:S(2)}) collective-permute-start(bf16[128,2048]{1,0:T(8,128)(2,1)} %collective-permute-done.3.refs_2_), channel_id=1, source_target_pairs={{0,8},{8,0},{1,9},{9,1},{2,10},{10,2},{3,11},{11,3},{4,12},{12,4},... | collective-permute-start | bytes 1572872 | tf_op jit(solution)/shard_map/ppermute | solution.py:300
  104.4 10.4 %all-to-all-start.3 = ((bf16[4,128,256]{2,1,0:T(8,128)(2,1)}), bf16[4,128,256]{2,1,0:T(8,128)(2,1)S(1)}, u32[]{:S(2)}, u32[]{:S(2)}) async-start(bf16[4,128,256]{2,1,0:T(8,128)(2,1)} %gate_up.1), calls=%async_computation.3 | async-start | bytes 524288 | tf_op jit(solution)/shard_map/all_to_all | solution.py:280
  109.3 15.0 %copy-start.1 = (s32[8,2]{0,1:T(2,128)S(1)}, s32[8,2]{0,1:T(2,128)}, u32[]{:S(2)}) copy-start(s32[8,2]{0,1:T(2,128)} %param.10) | copy-start | bytes 196
  109.3 40.0 %copy-start.2 = (f32[32,2]{0,1:T(2,128)S(1)}, f32[32,2]{0,1:T(2,128)}, u32[]{:S(2)}) copy-start(f32[32,2]{0,1:T(2,128)} %param.9) | copy-start | bytes 772
  118.2 19.8 %all-to-all-start.4 = ((bf16[8,128,256]{2,1,0:T(8,128)(2,1)}), bf16[8,128,256]{2,1,0:T(8,128)(2,1)S(1)}, u32[]{:S(2)}, u32[]{:S(2)}) async-start(bf16[8,128,256]{2,1,0:T(8,128)(2,1)} %down.1), calls=%async_computation.4 | async-start | bytes 1048576 | tf_op jit(solution)/shard_map/all_to_all | solution.py:280
  139.4 15.6 %all-to-all-start.5 = ((bf16[8,32,256]{2,1,0:T(8,128)(2,1)}), bf16[8,32,256]{2,1,0:T(8,128)(2,1)S(1)}, u32[]{:S(2)}, u32[]{:S(2)}) async-start(bf16[8,32,256]{2,1,0:T(8,128)(2,1)} %home.1), calls=%async_computation.5 | async-start | bytes 262144 | tf_op jit(solution)/shard_map/all_to_all | solution.py:280

commit v11 on v10

--- a/solution.py
+++ b/solution.py
@@ -68,7 +68,7 @@
             load.start()
     scales = []
     for x in range(2):
-        parts = [x_ref[2 * s + x, n * rows : n * rows + 8, 0:rows].astype(F32) for s in range(2)]
+        parts = [x_ref[3 - 2 * s - x, n * rows : n * rows + 8, 0:rows].astype(F32) for s in range(2)]
         both = parts[0] + parts[1]
         total = both[0:1, :] + both[1:2, :] + both[2:3, :]
         inv = 1.0 / jnp.sqrt(total / deep + 1e-05)
@@ -78,7 +78,7 @@
         xs = jnp.concatenate(
             [
                 jnp.concatenate(
-                    [x_ref[2 * (p // n) + x, (p % n) * rows : (p % n + 1) * rows, :] for p in pieces], axis=1
+                    [x_ref[3 - 2 * (p // n) - x, (p % n) * rows : (p % n + 1) * rows, :] for p in pieces], axis=1
                 )
                 for x in range(2)
             ],
@@ -100,7 +100,7 @@
             up = block[:, ff:] * scales[x]
             act = (gate / (1.0 + jnp.exp(-gate)) * up).astype(BF16)
             for s in range(2):
-                act_ref[2 * s + x, :, k * ff : (k + 1) * ff] = act
+                act_ref[3 - 2 * s - x, :, k * ff : (k + 1) * ff] = act
 
 
 def down_kernel(act_ref, *refs):
@@ -113,7 +113,7 @@
     place = lax.axis_index("sec") * 2 + lax.axis_index("xlo")
     sends = []
     for h in range(2):
-        act = jnp.concatenate([act_ref[place ^ k] for k in (2 * h, 2 * h + 1)], axis=1)
+        act = jnp.concatenate([act_ref[3 - (place ^ k)] for k in (2 * h, 2 * h + 1)], axis=1)
         for load in loads[4 * h : 4 * h + 4]:
             load.wait()
         for z in range(n):
@@ -281,6 +281,7 @@
 
 
 ACROSS = [[g ^ FAR for g in range(EXPERTS)]]
+CORNERS = [[3, 2, 1, 0]]
 COLUMN = [sorted(range(HID), key=place_of)]
 
 
@@ -314,8 +315,8 @@
     downs = [d for piece in direct for d in (piece, swapped(piece))]
     wide = exchange(wide, "hid", COLUMN)
     ready = prepared(wide)
-    every = exchange(ready, SQUARE)
-    act = exchange(gated(every, (gate0, up0, gate1, up1)), SQUARE)
+    every = exchange(ready, SQUARE, CORNERS)
+    act = exchange(gated(every, (gate0, up0, gate1, up1)), SQUARE, CORNERS)
     back = exchange(homed(block_experts, exchange(lowered(act, downs), "hid", COLUMN)), GROUP, ACROSS)
     return jnp.sum(back.astype(F32) * factor[:, :, None], axis=0).astype(BF16)
 

time: 157 us -> 155 us (0.987)
  no operation moved by 1% of the time
where the time goes in v11:
time: 155 us
  waiting for transfers between devices  52.6 us (34%)
  starting transfers between devices  45.8 us (30%)
  blocking collectives  40.9 us (26%)
  Pallas kernels  11.6 us (7%)
  local copies, waits for them, and re-layouts  2.7 us (2%)
    all_to_all x2, blocking collectives, exchange(): lax.all_to_all(x, axes, split_axis=0, concat_axis=0, axis_index_groups=li...  40.9 us
    ppermute x3, waiting for transfers between devices, sent(): return lax.ppermute(x, SQUARE, [(i, i ^ flip) for i in range(4)])  27.9 us
    all_to_all x4, waiting for transfers between devices, exchange(): lax.all_to_all(x, axes, split_axis=0, concat_axis=0, axis_index_groups=li...  24.6 us
    all_to_all x4, starting transfers between devices, exchange(): lax.all_to_all(x, axes, split_axis=0, concat_axis=0, axis_index_groups=li...  24.1 us
    ppermute x6, starting transfers between devices, swapped(): return lax.ppermute(x, 'core', [(0, 1), (1, 0)])  12.5 us
    ppermute x3, starting transfers between devices, sent(): return lax.ppermute(x, SQUARE, [(i, i ^ flip) for i in range(4)])  9.19 us
    pallas_call x1, Pallas kernels, gated(): pl.pallas_call(gate_up_kernel, out_shape=pltpu.HBM((4, rows, 2 * ff), BF1...  3.59 us
    pallas_call x1, Pallas kernels, lowered(): pl.pallas_call(down_kernel, out_shape=pltpu.HBM(shape, BF16), in_specs=[V...  3.39 us
  transfers between devices with their start and end apart: 13, of which 5 were waited for; matrix products, arithmetic and copies ran while one was open for 1% of the time, Pallas kernels for 2%

profile of v11, /device:TPU:6, one launch (start us, length us, event | category | flops | bytes accessed | tf_op | source)
XLA Modules:
  0.0 154.6 jit_solution(14834462022568157627)
XLA Ops:
  0.8 14.1 %all_to_all.30.x_ref = bf16[8,32,256]{2,1,0:T(8,128)(2,1)S(1)} all-to-all(bf16[8,32,256]{2,1,0:T(8,128)(2,1)S(1)} %broadcast_in_dim.35), channel_id=1, replica_groups={{160,128,224,192,32,0,96,64},{161,129,225,193,33,1,97,65},{162,130,226,..., dimensions={0} | all-to-all | bytes 262144 | tf_op jit(solution)/shard_map/all_to_all | solution.py:280
  14.9 1.6 %shard_map.73 = bf16[8,136,256]{2,1,0:T(8,128)(2,1)} custom-call(s32[2,8]{1,0:T(2,128)} %bitcast.7, bf16[8,32,256]{2,1,0:T(8,128)(2,1)S(1)} %all_to_all.30.x_ref, bf16[256]{0:T(256)(128)(2,1)} %gain_hbm.1), custom_call_target="tpu_custom_call" | custom-call | tf_op jit(solution)/shard_map/pallas_call | solution.py:250
  16.6 26.8 %all_to_all.31.x_ref = bf16[8,136,256]{2,1,0:T(8,128)(2,1)S(1)} all-to-all(bf16[8,136,256]{2,1,0:T(8,128)(2,1)} %shard_map.73), channel_id=1, replica_groups={{7,0,1,2,3,4,5,6},{15,8,9,10,11,12,13,14},{23,16,17,18,19,20,21,22},{31..., dimensions={0} | all-to-all | bytes 1114112 | tf_op jit(solution)/shard_map/all_to_all | solution.py:280
  43.4 1.6 %prep.1 = bf16[4,1032,256]{2,1,0:T(8,128)(2,1)} custom-call(bf16[8,136,256]{2,1,0:T(8,128)(2,1)S(1)} %all_to_all.31.x_ref), custom_call_target="tpu_custom_call" | custom-call | tf_op jit(solution)/shard_map/prep/pallas_call | solution.py:196
  45.0 5.0 %all-to-all-start.2 = ((bf16[4,1032,256]{2,1,0:T(8,128)(2,1)}), bf16[4,1032,256]{2,1,0:T(8,128)(2,1)S(1)}, u32[]{:S(2)}, u32[]{:S(2)}) async-start(bf16[4,1032,256]{2,1,0:T(8,128)(2,1)} %prep.1), calls=%async_computation.2 | async-start | bytes 4227072 | tf_op jit(solution)/shard_map/all_to_all | solution.py:280
  50.0 1.9 %collective-permute-start = (bf16[4096,128]{1,0:T(8,128)(2,1)}, bf16[4096,128]{1,0:T(8,128)(2,1)}, u32[]{:S(2)}, u32[]{:S(2)}) collective-permute-start(bf16[4096,128]{1,0:T(8,128)(2,1)} %bitcast.9), channel_id=1, source_target_pairs={{0,8},{8,0},{1,9},{9,1},{2,10},{10,2},{3,11},{11,3},{4,12},{12,4},... | collective-permute-start | bytes 3145736 | tf_op jit(solution)/shard_map/ppermute | solution.py:301
  51.9 2.4 %collective-permute-start.1 = (bf16[4096,128]{1,0:T(8,128)(2,1)}, bf16[4096,128]{1,0:T(8,128)(2,1)}, u32[]{:S(2)}, u32[]{:S(2)}) collective-permute-start(bf16[4096,128]{1,0:T(8,128)(2,1)} %bitcast.11), channel_id=1, source_target_pairs={{0,8},{8,0},{1,9},{9,1},{2,10},{10,2},{3,11},{11,3},{4,12},{12,4},... | collective-permute-start | bytes 3145736 | tf_op jit(solution)/shard_map/ppermute | solution.py:301
  55.2 1.9 %collective-permute-start.5 = (bf16[128,2048]{1,0:T(8,128)(2,1)}, bf16[128,2048]{1,0:T(8,128)(2,1)}, u32[]{:S(2)}, u32[]{:S(2)}) collective-permute-start(bf16[128,2048]{1,0:T(8,128)(2,1)} %dynamic-slice_bitcast_fusion), channel_id=1, source_target_pairs={{0,256},{16,272},{256,0},{272,16},{1,257},{17,273},{257,1},{273,17... | collective-permute-start | bytes 1572872 | tf_op jit(solution)/shard_map/ppermute | solution.py:298
  57.2 4.8 %collective-permute-start.7 = (bf16[128,2048]{1,0:T(8,128)(2,1)}, bf16[128,2048]{1,0:T(8,128)(2,1)}, u32[]{:S(2)}, u32[]{:S(2)}) collective-permute-start(bf16[128,2048]{1,0:T(8,128)(2,1)} %dynamic-slice_bitcast_fusion), channel_id=1, source_target_pairs={{0,272},{16,256},{256,16},{272,0},{1,273},{17,257},{257,17},{273,1... | collective-permute-start | bytes 1572872 | tf_op jit(solution)/shard_map/ppermute | solution.py:298
  62.8 2.5 %collective-permute-start.3 = (bf16[128,2048]{1,0:T(8,128)(2,1)}, bf16[128,2048]{1,0:T(8,128)(2,1)}, u32[]{:S(2)}, u32[]{:S(2)}) collective-permute-start(bf16[128,2048]{1,0:T(8,128)(2,1)} %constant_dynamic-slice_fusion.refs_0_), channel_id=1, source_target_pairs={{0,16},{16,0},{256,272},{272,256},{1,17},{17,1},{257,273},{273,257... | collective-permute-start | bytes 1572872 | tf_op jit(solution)/shard_map/ppermute | solution.py:298
  65.3 20.5 %collective-permute-done.5.refs_4_ = bf16[128,2048]{1,0:T(8,128)(2,1)} collective-permute-done((bf16[128,2048]{1,0:T(8,128)(2,1)}, bf16[128,2048]{1,0:T(8,128)(2,1)}, u32[]{:S(2)}, u32[]{:S(2)}) %collective-permute-start.5) | collective-permute-done | bytes 524320 | tf_op jit(solution)/shard_map/ppermute | solution.py:298
  85.8 1.9 %collective-permute-start.2 = (bf16[128,2048]{1,0:T(8,128)(2,1)}, bf16[128,2048]{1,0:T(8,128)(2,1)}, u32[]{:S(2)}, u32[]{:S(2)}) collective-permute-start(bf16[128,2048]{1,0:T(8,128)(2,1)} %constant_dynamic-slice_fusion.refs_0_), channel_id=1, source_target_pairs={{0,8},{8,0},{1,9},{9,1},{2,10},{10,2},{3,11},{11,3},{4,12},{12,4},... | collective-permute-start | bytes 1572872 | tf_op jit(solution)/shard_map/ppermute | solution.py:301
  87.7 7.5 %collective-permute-done.7.refs_6_ = bf16[128,2048]{1,0:T(8,128)(2,1)} collective-permute-done((bf16[128,2048]{1,0:T(8,128)(2,1)}, bf16[128,2048]{1,0:T(8,128)(2,1)}, u32[]{:S(2)}, u32[]{:S(2)}) %collective-permute-start.7) | collective-permute-done | bytes 524320 | tf_op jit(solution)/shard_map/ppermute | solution.py:298
  95.2 1.9 %collective-permute-start.6 = (bf16[128,2048]{1,0:T(8,128)(2,1)}, bf16[128,2048]{1,0:T(8,128)(2,1)}, u32[]{:S(2)}, u32[]{:S(2)}) collective-permute-start(bf16[128,2048]{1,0:T(8,128)(2,1)} %collective-permute-done.5.refs_4_), channel_id=1, source_target_pairs={{0,8},{8,0},{1,9},{9,1},{2,10},{10,2},{3,11},{11,3},{4,12},{12,4},... | collective-permute-start | bytes 1572872 | tf_op jit(solution)/shard_map/ppermute | solution.py:301
  97.1 2.4 %collective-permute-start.8 = (bf16[128,2048]{1,0:T(8,128)(2,1)}, bf16[128,2048]{1,0:T(8,128)(2,1)}, u32[]{:S(2)}, u32[]{:S(2)}) collective-permute-start(bf16[128,2048]{1,0:T(8,128)(2,1)} %collective-permute-done.7.refs_6_), channel_id=1, source_target_pairs={{0,8},{8,0},{1,9},{9,1},{2,10},{10,2},{3,11},{11,3},{4,12},{12,4},... | collective-permute-start | bytes 1572872 | tf_op jit(solution)/shard_map/ppermute | solution.py:301
  99.5 1.9 %collective-permute-start.4 = (bf16[128,2048]{1,0:T(8,128)(2,1)}, bf16[128,2048]{1,0:T(8,128)(2,1)}, u32[]{:S(2)}, u32[]{:S(2)}) collective-permute-start(bf16[128,2048]{1,0:T(8,128)(2,1)} %collective-permute-done.3.refs_2_), channel_id=1, source_target_pairs={{0,8},{8,0},{1,9},{9,1},{2,10},{10,2},{3,11},{11,3},{4,12},{12,4},... | collective-permute-start | bytes 1572872 | tf_op jit(solution)/shard_map/ppermute | solution.py:301
  101.5 3.6 %gate_up.1 = bf16[4,128,256]{2,1,0:T(8,128)(2,1)} custom-call(bf16[4,1032,256]{2,1,0:T(8,128)(2,1)S(1)} %all-to-all-done.2.x_ref, bf16[4096,128]{1,0:T(8,128)(2,1)} %bitcast.10, bf16[4096,128]{1,0:T(8,128)(2,1)} %bitcast.12, bf16[4096,128]{1,0:T(8,128)(2,1)} %collective-permute-done.g1, bf16[4096,128]{1,0:T(8,128)(2,1)} %collective-permute-done.1.u1), custom_call_target="tpu_custom_call" | custom-call | tf_op jit(solution)/shard_map/gate_up/pallas_call | solution.py:211
  105.1 4.9 %all-to-all-start.3 = ((bf16[4,128,256]{2,1,0:T(8,128)(2,1)}), bf16[4,128,256]{2,1,0:T(8,128)(2,1)S(1)}, u32[]{:S(2)}, u32[]{:S(2)}) async-start(bf16[4,128,256]{2,1,0:T(8,128)(2,1)} %gate_up.1), calls=%async_computation.3 | async-start | bytes 524288 | tf_op jit(solution)/shard_map/all_to_all | solution.py:280
  110.0 5.5 %all-to-all-done.3.act_ref = bf16[4,128,256]{2,1,0:T(8,128)(2,1)S(1)} async-done(((bf16[4,128,256]{2,1,0:T(8,128)(2,1)}), bf16[4,128,256]{2,1,0:T(8,128)(2,1)S(1)}, u32[]{:S(2)}, u32[]{:S(2)}) %all-to-all-start.3) | async-done | bytes 262176 | tf_op jit(solution)/shard_map/all_to_all | solution.py:280
  115.5 3.4 %down.1 = bf16[8,128,256]{2,1,0:T(8,128)(2,1)} custom-call(bf16[4,128,256]{2,1,0:T(8,128)(2,1)S(1)} %all-to-all-done.3.act_ref, bf16[128,2048]{1,0:T(8,128)(2,1)} %constant_dynamic-slice_fusion.refs_0_, bf16[128,2048]{1,0:T(8,128)(2,1)} %collective-permute-done.2.refs_1_, bf16[128,2048]{1,0:T(8,128)(2,1)} %collective-permute-done.3.refs_2_, ...), custom_call_target="tpu_custom_call" | custom-call | tf_op jit(solution)/shard_map/down/pallas_call | solution.py:230
  118.9 6.4 %all-to-all-start.4 = ((bf16[8,128,256]{2,1,0:T(8,128)(2,1)}), bf16[8,128,256]{2,1,0:T(8,128)(2,1)S(1)}, u32[]{:S(2)}, u32[]{:S(2)}) async-start(bf16[8,128,256]{2,1,0:T(8,128)(2,1)} %down.1), calls=%async_computation.4 | async-start | bytes 1048576 | tf_op jit(solution)/shard_map/all_to_all | solution.py:280
  125.5 13.7 %all-to-all-done.4.x_ref = bf16[8,128,256]{2,1,0:T(8,128)(2,1)S(1)} async-done(((bf16[8,128,256]{2,1,0:T(8,128)(2,1)}), bf16[8,128,256]{2,1,0:T(8,128)(2,1)S(1)}, u32[]{:S(2)}, u32[]{:S(2)}) %all-to-all-start.4) | async-done | bytes 524320 | tf_op jit(solution)/shard_map/all_to_all | solution.py:280
  140.5 7.8 %all-to-all-start.5 = ((bf16[8,32,256]{2,1,0:T(8,128)(2,1)}), bf16[8,32,256]{2,1,0:T(8,128)(2,1)S(1)}, u32[]{:S(2)}, u32[]{:S(2)}) async-start(bf16[8,32,256]{2,1,0:T(8,128)(2,1)} %home.1), calls=%async_computation.5 | async-start | bytes 262144 | tf_op jit(solution)/shard_map/all_to_all | solution.py:280
  148.5 5.4 %all-to-all-done.5 = bf16[8,32,256]{2,1,0:T(8,128)(2,1)S(1)} async-done(((bf16[8,32,256]{2,1,0:T(8,128)(2,1)}), bf16[8,32,256]{2,1,0:T(8,128)(2,1)S(1)}, u32[]{:S(2)}, u32[]{:S(2)}) %all-to-all-start.5) | async-done | bytes 131104 | tf_op jit(solution)/shard_map/all_to_all | solution.py:280
  (23 shorter events, 4.9 us)
Async XLA Ops:
  0.0 54.4 %copy-start = (bf16[1,128,4096]{2,1,0:T(8,128)(2,1)S(1)}, bf16[1,128,4096]{2,1,0:T(8,128)(2,1)}, u32[]{:S(2)}) copy-start(bf16[1,128,4096]{2,1,0:T(8,128)(2,1)} %param.13) | copy-start | bytes 3145732
  45.0 56.4 %all-to-all-start.2 = ((bf16[4,1032,256]{2,1,0:T(8,128)(2,1)}), bf16[4,1032,256]{2,1,0:T(8,128)(2,1)S(1)}, u32[]{:S(2)}, u32[]{:S(2)}) async-start(bf16[4,1032,256]{2,1,0:T(8,128)(2,1)} %prep.1), calls=%async_computation.2 | async-start | bytes 4227072 | tf_op jit(solution)/shard_map/all_to_all | solution.py:280
  50.0 49.5 %collective-permute-start = (bf16[4096,128]{1,0:T(8,128)(2,1)}, bf16[4096,128]{1,0:T(8,128)(2,1)}, u32[]{:S(2)}, u32[]{:S(2)}) collective-permute-start(bf16[4096,128]{1,0:T(8,128)(2,1)} %bitcast.9), channel_id=1, source_target_pairs={{0,8},{8,0},{1,9},{9,1},{2,10},{10,2},{3,11},{11,3},{4,12},{12,4},... | collective-permute-start | bytes 3145736 | tf_op jit(solution)/shard_map/ppermute | solution.py:301
  51.9 49.5 %collective-permute-start.1 = (bf16[4096,128]{1,0:T(8,128)(2,1)}, bf16[4096,128]{1,0:T(8,128)(2,1)}, u32[]{:S(2)}, u32[]{:S(2)}) collective-permute-start(bf16[4096,128]{1,0:T(8,128)(2,1)} %bitcast.11), channel_id=1, source_target_pairs={{0,8},{8,0},{1,9},{9,1},{2,10},{10,2},{3,11},{11,3},{4,12},{12,4},... | collective-permute-start | bytes 3145736 | tf_op jit(solution)/shard_map/ppermute | solution.py:301
  55.2 30.6 %collective-permute-start.5 = (bf16[128,2048]{1,0:T(8,128)(2,1)}, bf16[128,2048]{1,0:T(8,128)(2,1)}, u32[]{:S(2)}, u32[]{:S(2)}) collective-permute-start(bf16[128,2048]{1,0:T(8,128)(2,1)} %dynamic-slice_bitcast_fusion), channel_id=1, source_target_pairs={{0,256},{16,272},{256,0},{272,16},{1,257},{17,273},{257,1},{273,17... | collective-permute-start | bytes 1572872 | tf_op jit(solution)/shard_map/ppermute | solution.py:298
  57.2 38.0 %collective-permute-start.7 = (bf16[128,2048]{1,0:T(8,128)(2,1)}, bf16[128,2048]{1,0:T(8,128)(2,1)}, u32[]{:S(2)}, u32[]{:S(2)}) collective-permute-start(bf16[128,2048]{1,0:T(8,128)(2,1)} %dynamic-slice_bitcast_fusion), channel_id=1, source_target_pairs={{0,272},{16,256},{256,16},{272,0},{1,273},{17,257},{257,17},{273,1... | collective-permute-start | bytes 1572872 | tf_op jit(solution)/shard_map/ppermute | solution.py:298
  62.8 34.3 %collective-permute-start.3 = (bf16[128,2048]{1,0:T(8,128)(2,1)}, bf16[128,2048]{1,0:T(8,128)(2,1)}, u32[]{:S(2)}, u32[]{:S(2)}) collective-permute-start(bf16[128,2048]{1,0:T(8,128)(2,1)} %constant_dynamic-slice_fusion.refs_0_), channel_id=1, source_target_pairs={{0,16},{16,0},{256,272},{272,256},{1,17},{17,1},{257,273},{273,257... | collective-permute-start | bytes 1572872 | tf_op jit(solution)/shard_map/ppermute | solution.py:298
  85.8 24.1 %collective-permute-start.2 = (bf16[128,2048]{1,0:T(8,128)(2,1)}, bf16[128,2048]{1,0:T(8,128)(2,1)}, u32[]{:S(2)}, u32[]{:S(2)}) collective-permute-start(bf16[128,2048]{1,0:T(8,128)(2,1)} %constant_dynamic-slice_fusion.refs_0_), channel_id=1, source_target_pairs={{0,8},{8,0},{1,9},{9,1},{2,10},{10,2},{3,11},{11,3},{4,12},{12,4},... | collective-permute-start | bytes 1572872 | tf_op jit(solution)/shard_map/ppermute | solution.py:301
  95.2 14.8 %collective-permute-start.6 = (bf16[128,2048]{1,0:T(8,128)(2,1)}, bf16[128,2048]{1,0:T(8,128)(2,1)}, u32[]{:S(2)}, u32[]{:S(2)}) collective-permute-start(bf16[128,2048]{1,0:T(8,128)(2,1)} %collective-permute-done.5.refs_4_), channel_id=1, source_target_pairs={{0,8},{8,0},{1,9},{9,1},{2,10},{10,2},{3,11},{11,3},{4,12},{12,4},... | collective-permute-start | bytes 1572872 | tf_op jit(solution)/shard_map/ppermute | solution.py:301
  97.1 12.9 %collective-permute-start.8 = (bf16[128,2048]{1,0:T(8,128)(2,1)}, bf16[128,2048]{1,0:T(8,128)(2,1)}, u32[]{:S(2)}, u32[]{:S(2)}) collective-permute-start(bf16[128,2048]{1,0:T(8,128)(2,1)} %collective-permute-done.7.refs_6_), channel_id=1, source_target_pairs={{0,8},{8,0},{1,9},{9,1},{2,10},{10,2},{3,11},{11,3},{4,12},{12,4},... | collective-permute-start | bytes 1572872 | tf_op jit(solution)/shard_map/ppermute | solution.py:301
  99.5 10.4 %collective-permute-start.4 = (bf16[128,2048]{1,0:T(8,128)(2,1)}, bf16[128,2048]{1,0:T(8,128)(2,1)}, u32[]{:S(2)}, u32[]{:S(2)}) collective-permute-start(bf16[128,2048]{1,0:T(8,128)(2,1)} %collective-permute-done.3.refs_2_), channel_id=1, source_target_pairs={{0,8},{8,0},{1,9},{9,1},{2,10},{10,2},{3,11},{11,3},{4,12},{12,4},... | collective-permute-start | bytes 1572872 | tf_op jit(solution)/shard_map/ppermute | solution.py:301
  105.1 10.4 %all-to-all-start.3 = ((bf16[4,128,256]{2,1,0:T(8,128)(2,1)}), bf16[4,128,256]{2,1,0:T(8,128)(2,1)S(1)}, u32[]{:S(2)}, u32[]{:S(2)}) async-start(bf16[4,128,256]{2,1,0:T(8,128)(2,1)} %gate_up.1), calls=%async_computation.3 | async-start | bytes 524288 | tf_op jit(solution)/shard_map/all_to_all | solution.py:280
  109.9 15.4 %copy-start.1 = (s32[8,2]{0,1:T(2,128)S(1)}, s32[8,2]{0,1:T(2,128)}, u32[]{:S(2)}) copy-start(s32[8,2]{0,1:T(2,128)} %param.10) | copy-start | bytes 196
  109.9 38.5 %copy-start.2 = (f32[32,2]{0,1:T(2,128)S(1)}, f32[32,2]{0,1:T(2,128)}, u32[]{:S(2)}) copy-start(f32[32,2]{0,1:T(2,128)} %param.9) | copy-start | bytes 772
  118.9 20.3 %all-to-all-start.4 = ((bf16[8,128,256]{2,1,0:T(8,128)(2,1)}), bf16[8,128,256]{2,1,0:T(8,128)(2,1)S(1)}, u32[]{:S(2)}, u32[]{:S(2)}) async-start(bf16[8,128,256]{2,1,0:T(8,128)(2,1)} %down.1), calls=%async_computation.4 | async-start | bytes 1048576 | tf_op jit(solution)/shard_map/all_to_all | solution.py:280
  140.5 13.4 %all-to-all-start.5 = ((bf16[8,32,256]{2,1,0:T(8,128)(2,1)}), bf16[8,32,256]{2,1,0:T(8,128)(2,1)S(1)}, u32[]{:S(2)}, u32[]{:S(2)}) async-start(bf16[8,32,256]{2,1,0:T(8,128)(2,1)} %home.1), calls=%async_computation.5 | async-start | bytes 262144 | tf_op jit(solution)/shard_map/all_to_all | solution.py:280
